TPU v7x, 32 devices: a whole 2x2x4 slice. The times are simulated.
32 devices in a mesh: groups: 2 (over y), pulse: 4 (over x, core), range: 4 (over z).
Axes of the slice: x: 2, y: 2, z: 4, core: 2. Of those that a mesh axis runs over, the one named last changes fastest.
Arguments:
- echoes: bfloat16 [2048, 2, 8192], P(('groups', 'pulse'), None, 'range'), parts along dimension 0, may hold values from -6 to 6
- shifts: int32 [2048], P(('groups', 'pulse')), parts along dimension 0, may hold values from -64 to 64
- tap_weights: float32 [2048, 8], P(('groups', 'pulse')), parts along dimension 0, may hold values from -2 to 2
- angles: float32 [2048], P(('groups', 'pulse')), parts along dimension 0, may hold values from -3.140625 to 3.140625
- slopes: float32 [2048], P(('groups', 'pulse')), parts along dimension 0, may hold values from -0.05 to 0.05
- steering: bfloat16 [2, 8, 32], replicated, may hold values from -0.75 to 0.75
- footprint: int32 [32, 32], P('groups'), parts along dimension 0, may hold values from 0 to 255, as said below
- tile_coeffs: bfloat16 [32, 2, 64, 32], P(('groups', 'pulse')), parts along dimension 0, may hold values from -0.75 to 0.75
Outputs:
- image_tiles: bfloat16 [32, 2, 64, 8192], P(('groups', 'pulse'), None, None, 'range'), parts along dimension 0
There are 2 independent parts, one for each index of `groups`. A program takes and returns all parts, laid end to end along the dimension named above; an argument that names none is the same for every part. Nothing has to cross between parts.
Inputs may be any that keep to these rules, and one draw needn't show every extreme that they name: `footprint`: beam s * 8 + b belongs to subaperture s. The 128 entries of tiles k * 4 to k * 4 + 3 are distinct beams; at most 64 of them lie in any one range of beams j * 64 to j * 64 + 63, and for every k exactly 64 lie in some such range.
All inputs are finite; a program needn't handle non-finite values.
Results may differ from a plain program's by a relative error of at most 0.0058.
Values may be sent and summed in bfloat16 or wider, within the bound.
No kernel may reach another device: no remote copies, remote signals or barrier semaphores. Data moves between devices by JAX's collectives and lax.ppermute only.
A program may use at most 64 MiB of HBM per device.

v0:
```python
import jax
import jax.numpy as jnp
from jax import lax
from jax.sharding import PartitionSpec as P

SUB = 32
TAPS = 8
MAXS = 64
TILE_DEV = 4
FOOT = 32
HALO = 68


def padded_2(cells, sides, width):
    for axis, dim in sides:
        count = lax.axis_size(axis)
        ends = count - 1
        head = lax.slice_in_dim(cells, 0, width, axis=dim)
        tail = lax.slice_in_dim(cells, cells.shape[dim] - width, cells.shape[dim], axis=dim)
        cells = jnp.concatenate(
            [
                lax.ppermute(tail, axis, [(i, (i + 1) % count) for i in range(ends)]),
                cells,
                lax.ppermute(head, axis, [((i + 1) % count, i) for i in range(ends)]),
            ],
            axis=dim,
        )
    return cells


def align_block(padded, shifts, tap_weights, angles, slopes, start_cell):
    pulse_rows = padded.shape[0]
    span_cells = padded.shape[2] - 2 * HALO
    reach = 2 * MAXS + TAPS
    offsets = jnp.arange(reach, dtype=jnp.int32)
    tap_where = shifts[:, None] + MAXS + jnp.arange(TAPS, dtype=jnp.int32)[None, :]
    kernel = jnp.sum(
        jnp.where(
            offsets[None, None, :] == tap_where[:, :, None],
            tap_weights[:, :, None],
            jnp.float32(0.0),
        ),
        axis=1,
    )
    kernel = jnp.repeat(kernel, 2, axis=0)[:, None, :]
    source = padded[:, :, 1:].astype(jnp.float32).reshape(1, pulse_rows * 2, span_cells + reach - 1)
    summed = lax.conv_general_dilated(
        source,
        kernel,
        (1,),
        "VALID",
        dimension_numbers=("NCH", "OIH", "NCH"),
        feature_group_count=pulse_rows * 2,
        precision=lax.Precision.HIGHEST,
    )
    summed = summed.reshape(pulse_rows, 2, span_cells)
    positions = (start_cell + jnp.arange(span_cells)).astype(jnp.float32)
    phases = angles[:, None] + slopes[:, None] * positions[None, :]
    cosine_values = jnp.cos(phases)
    sine_values = jnp.sin(phases)
    real_part = cosine_values * summed[:, 0] - sine_values * summed[:, 1]
    imag_part = sine_values * summed[:, 0] + cosine_values * summed[:, 1]
    return jnp.stack([real_part, imag_part], axis=1).astype(jnp.bfloat16)


def project(picked, tile_coeffs):
    weight_real = tile_coeffs[:, 0]
    weight_imag = tile_coeffs[:, 1]
    real_in = picked[:, :, 0]
    imag_in = picked[:, :, 1]
    real_part = jnp.einsum(
        "taf,tfw->taw", weight_real, real_in, preferred_element_type=jnp.float32
    ) - jnp.einsum("taf,tfw->taw", weight_imag, imag_in, preferred_element_type=jnp.float32)
    imag_part = jnp.einsum(
        "taf,tfw->taw", weight_real, imag_in, preferred_element_type=jnp.float32
    ) + jnp.einsum("taf,tfw->taw", weight_imag, real_in, preferred_element_type=jnp.float32)
    return jnp.stack([real_part, imag_part], axis=1).astype(jnp.bfloat16)


def body(echoes, shifts, tap_weights, angles, slopes, steering, footprint, tile_coeffs):
    cells = echoes.shape[2]
    padded = padded_2(echoes, (("range", 2),), HALO)
    start_cell = lax.axis_index("range") * cells
    aligned = align_block(padded, shifts, tap_weights, angles, slopes, start_cell)
    groups = aligned.reshape(aligned.shape[0] // SUB, SUB, 2, cells)
    real_in = groups[:, :, 0]
    imag_in = groups[:, :, 1]
    real_part = jnp.einsum(
        "bj,sjw->sbw", steering[0], real_in, preferred_element_type=jnp.float32
    ) - jnp.einsum("bj,sjw->sbw", steering[1], imag_in, preferred_element_type=jnp.float32)
    imag_part = jnp.einsum(
        "bj,sjw->sbw", steering[0], imag_in, preferred_element_type=jnp.float32
    ) + jnp.einsum("bj,sjw->sbw", steering[1], real_in, preferred_element_type=jnp.float32)
    beam_rows = jnp.stack([real_part, imag_part], axis=2).astype(jnp.bfloat16)
    beam_rows = beam_rows.reshape(-1, 2, cells)
    pulse_count = lax.axis_size("pulse")
    my_index = lax.axis_index("pulse")
    entries = TILE_DEV * FOOT
    owner_ids = footprint.reshape(pulse_count, entries)
    my_entries = lax.dynamic_index_in_dim(owner_ids, my_index, 0, keepdims=False)
    gathered = lax.all_gather(beam_rows, "pulse", axis=0, tiled=True)
    picked = jnp.take(gathered, my_entries, axis=0).reshape(TILE_DEV, FOOT, 2, cells)
    image_tiles = project(picked, tile_coeffs)
    return image_tiles


def solution(mesh):
    placed = (
        P(("groups", "pulse"), None, "range"),
        P(("groups", "pulse")),
        P(("groups", "pulse"), None),
        P(("groups", "pulse")),
        P(("groups", "pulse")),
        P(),
        P("groups", None),
        P(("groups", "pulse"), None, None, None),
    )
    return jax.shard_map(
        body,
        mesh=mesh,
        in_specs=placed,
        out_specs=P(("groups", "pulse"), None, None, "range"),
        check_vma=False,
    )
```

profile of v0, /device:TPU:0, one launch (start us, length us, event | category | flops | bytes accessed | tf_op | source)
XLA Modules:
  0.0 247.5 jit_solution(8722996066743790988)
XLA Ops:
  6.5 0.0 all-gather.2.cloned.1.call-start
  6.5 1.2 fusion.47
  7.8 5.0 %collective-permute-start = (bf16[256,2,68]{2,1,0:T(2,128)(2,1)S(1)}, bf16[256,2,68]{2,1,0:T(2,128)(2,1)S(1)}, u32[]{:S(2)}, u32[]{:S(2)}) collective-permute-start(bf16[256,2,68]{2,1,0:T(2,128)(2,1)S(1)} %get-tuple-element.10), channel_id=1, source_target_pairs={{0,1},{1,2},{2,3},{4,5},{5,6},{6,7},{8,9},{9,10},{10,11},{12,13},{... | collective-permute-start | bytes 208904 | tf_op jit(solution)/shard_map/ppermute | solution.py:22
  12.7 1.3 collective-permute-start.1
  14.0 0.7 broadcast_add_fusion
  14.7 0.8 select_reduce_fusion
  15.6 0.1 copy.68
  15.7 0.2 broadcast_in_dim.36
  15.9 0.4 broadcast_in_dim_reshape.3
  16.3 0.2 copy.69
  16.4 0.0 collective-permute-done
  16.5 3.1 %collective-permute-done.1 = bf16[256,2,68]{2,1,0:T(2,128)(2,1)S(1)} collective-permute-done((bf16[256,2,68]{2,1,0:T(2,128)(2,1)S(1)}, bf16[256,2,68]{2,1,0:T(2,128)(2,1)S(1)}, u32[]{:S(2)}, u32[]{:S(2)}) %collective-permute-start.1) | collective-permute-done | bytes 69664 | tf_op jit(solution)/shard_map/ppermute | solution.py:24
  19.6 14.3 %concatenate.7 = bf16[256,2,2184]{2,1,0:T(2,128)(2,1)S(1)} concatenate(bf16[256,2,68]{2,1,0:T(2,128)(2,1)S(1)} %collective-permute-done, bf16[256,2,2048]{2,1,0:T(2,128)(2,1)} %param.8, bf16[256,2,68]{2,1,0:T(2,128)(2,1)S(1)} %collective-permute-done.1), dimensions={2} | concatenate | bytes 4472832 | tf_op jit(solution)/shard_map/concatenate | solution.py:20
  34.0 6.5 %slice.54 = bf16[256,2,2183]{2,1,0:T(2,128)(2,1)} slice(bf16[256,2,2184]{2,1,0:T(2,128)(2,1)S(1)} %concatenate.7), slice={[0:256], [0:2], [1:2184]} | slice | bytes 4470784 | tf_op jit(solution)/shard_map/slice | solution.py:46
  40.5 4.9 %reshape.215 = bf16[512,1,2183]{2,0,1:T(8,128)(2,1)S(1)} reshape(bf16[256,2,2183]{2,1,0:T(2,128)(2,1)} %slice.54) | data formatting | bytes 4470784 | tf_op jit(solution)/shard_map/reshape | solution.py:46
  45.4 1.7 pad
  47.1 6.8 %reshape.230 = bf16[512,1,8,273]{3,2,0,1:T(8,128)(2,1)} reshape(bf16[512,1,2184]{2,0,1:T(8,128)(2,1)} %pad) | data formatting | bytes 4472832 | tf_op jit(solution)/shard_map/conv_general_dilated | solution.py:47
  53.9 4.4 %copy.67 = bf16[512,1,8,273]{0,2,3,1:T(8,128)(2,1)S(1)} copy(bf16[512,1,8,273]{3,2,0,1:T(8,128)(2,1)} %reshape.230) | data formatting | bytes 4472832 | tf_op jit(solution)/shard_map/conv_general_dilated | solution.py:47
  58.2 0.3 slice.55
  58.5 0.0 copy-start.5
  58.5 0.3 fusion.56
  58.9 0.4 copy-done.5
  59.3 103.2 %broadcast_select_fusion = f32[8,273,512]{2,0,1:T(8,128)S(1)} fusion(pred[8,273]{0,1:T(8,128)(4,1)S(1)} %copy-done.5, f32[512,1,136]{0,1,2:T(1,128)S(1)} %copy.69, bf16[512,8,408]{0,1,2:T(8,128)(2,1)S(1)} %fusion.56), kind=kOutput, calls=%fused_computation.22 | convolution fusion | flops 1826033664 | bytes 8095880 | tf_op jit(solution)/shard_map/conv_general_dilated | solution.py:47
  162.5 4.7 %copy.70 = f32[8,273,512]{2,1,0:T(8,128)} copy(f32[8,273,512]{2,0,1:T(8,128)S(1)} %broadcast_select_fusion) | data formatting | bytes 8945664 | tf_op jit(solution)/shard_map/conv_general_dilated | solution.py:47
  167.1 5.1 %reshape.214 = f32[1,2184,512]{2,1,0:T(8,128)} reshape(f32[8,273,512]{2,1,0:T(8,128)} %copy.70) | data formatting | bytes 8945664 | tf_op jit(solution)/shard_map/conv_general_dilated | solution.py:47
  172.3 4.6 %slice_bitcast_fusion = f32[1,512,2048]{1,2,0:T(8,128)} fusion(f32[1,2184,512]{2,1,0:T(8,128)} %reshape.214), kind=kLoop, calls=%fused_computation.3 | loop fusion | bytes 8388608 | tf_op jit(solution)/shard_map/conv_general_dilated | solution.py:47
  176.8 5.5 %copy.71 = f32[1,512,2048]{2,1,0:T(8,128)} copy(f32[1,512,2048]{1,2,0:T(8,128)} %slice_bitcast_fusion) | data formatting | bytes 8388608 | tf_op jit(solution)/shard_map/conv_general_dilated | solution.py:47
  182.3 5.8 %reshape.207 = f32[256,2,2048]{2,1,0:T(2,128)} reshape(f32[1,512,2048]{2,1,0:T(8,128)} %copy.71) | data formatting | bytes 8388608 | tf_op jit(solution)/shard_map/reshape | solution.py:56
  188.1 0.0 copy-start.3
  188.1 0.0 copy-start.4
  188.1 7.8 %fusion.46 = (f32[256,1,2048]{2,1,0:T(1,128)S(1)}, f32[256,1,2048]{2,1,0:T(1,128)S(1)}) fusion(f32[256,2,2048]{2,1,0:T(2,128)} %reshape.207), kind=kLoop, calls=%fused_computation.69 | loop fusion | bytes 8388608 | tf_op jit(solution)/shard_map/slice | solution.py:61
  195.9 0.0 copy-done.3
  195.9 0.0 copy-done.4
  195.9 0.0 copy-start.1
  195.9 9.1 %subtract_convert_fusion = (bf16[256,1,2048]{2,0,1:T(8,128)(2,1)S(1)}, bf16[256,1,2048]{2,0,1:T(8,128)(2,1)S(1)}) fusion(f32[256,1,2048]{2,1,0:T(1,128)S(1)} %get-tuple-element.8, f32[256,1,2048]{2,1,0:T(1,128)S(1)} %get-tuple-element.7, f32[2048]{0:T(1024)S(1)} %add_convert_fusion.1, f32[256]{0:T(256)S(1)} %copy-done.3, f32[256]{0:T(256)S(1)} %copy-done.4), kind=kLoop, calls=%fused_computation.25 | loop fusion | flops 5242880 | bytes 6301696 | tf_op jit(solution)/shard_map/convert.15
  205.1 0.0 copy-done.1
  205.1 0.3 fusion.35
  205.4 0.3 fusion.33
  205.6 0.3 fusion.15
  205.9 0.4 copy.74
  206.3 0.0 copy-start.2
  206.3 0.3 fusion.14
  206.6 0.4 copy.75
  207.0 2.0 pad_maximum_fusion.1
  209.0 0.0 all-gather.2.cloned.1.call-update
  209.0 0.0 copy-done.2
  209.0 0.1 reshape.205
  209.1 0.1 squeeze.36
  209.2 22.7 %all-gather.2.cloned.1.call-done = bf16[256,2,2048]{2,1,0:T(2,128)(2,1)} async-done(((bf16[64,2,2048]{2,1,0:T(2,128)(2,1)}), bf16[256,2,2048]{2,1,0:T(2,128)(2,1)}) %all-gather.2.cloned.1.call-update) | async-done | bytes 2097168 | tf_op jit(solution)/shard_map/all_gather | solution.py:101
  232.0 4.3 %gather_fusion = bf16[128,2,2048]{2,1,0:T(2,128)(2,1)S(1)} fusion(bf16[256,2,2048]{2,1,0:T(2,128)(2,1)} %all-gather.2.cloned.1.call-done, s32[1024]{0:T(1024)S(1)} %pad_clamp_fusion), kind=kCustom, calls=%fused_computation | custom fusion | bytes 2097664 | tf_op jit(solution)/shard_map/jit(_take)/gather | solution.py:102
  236.2 0.0 copy-start
  236.2 0.4 copy.76
  236.6 0.2 broadcast_select_fusion.1
  236.8 0.3 copy-done
  237.1 0.5 fusion.21
  237.5 0.5 fusion.22
  238.0 0.5 fusion.11
  238.5 0.5 fusion.10
  239.0 0.2 pad_maximum_fusion
  239.2 1.5 copy.79
  (6 shorter events, 0.1 us)
Async XLA Ops:
  6.5 225.4 %all-gather.2.cloned.1.call-start = ((), (), s32[]{:S(2)}) async-start(), calls=%async_computation | async-start | bytes 2621440 | tf_op jit(solution)/shard_map/all_gather | solution.py:101
  7.8 8.7 %collective-permute-start = (bf16[256,2,68]{2,1,0:T(2,128)(2,1)S(1)}, bf16[256,2,68]{2,1,0:T(2,128)(2,1)S(1)}, u32[]{:S(2)}, u32[]{:S(2)}) collective-permute-start(bf16[256,2,68]{2,1,0:T(2,128)(2,1)S(1)} %get-tuple-element.10), channel_id=1, source_target_pairs={{0,1},{1,2},{2,3},{4,5},{5,6},{6,7},{8,9},{9,10},{10,11},{12,13},{... | collective-permute-start | bytes 208904 | tf_op jit(solution)/shard_map/ppermute | solution.py:22
  12.7 6.9 %collective-permute-start.1 = (bf16[256,2,68]{2,1,0:T(2,128)(2,1)S(1)}, bf16[256,2,68]{2,1,0:T(2,128)(2,1)S(1)}, u32[]{:S(2)}, u32[]{:S(2)}) collective-permute-start(bf16[256,2,68]{2,1,0:T(2,128)(2,1)S(1)} %get-tuple-element.9), channel_id=1, source_target_pairs={{1,0},{2,1},{3,2},{5,4},{6,5},{7,6},{9,8},{10,9},{11,10},{13,12},{... | collective-permute-start | bytes 208904 | tf_op jit(solution)/shard_map/ppermute | solution.py:24
  58.5 0.8 copy-start.5
  188.1 7.8 %copy-start.3 = (f32[256]{0:T(256)S(1)}, f32[256]{0:T(256)}, u32[]{:S(2)}) copy-start(f32[256]{0:T(256)} %param.12) | copy-start | bytes 3076
  188.1 7.8 %copy-start.4 = (f32[256]{0:T(256)S(1)}, f32[256]{0:T(256)}, u32[]{:S(2)}) copy-start(f32[256]{0:T(256)} %param.11) | copy-start | bytes 3076
  195.9 9.2 %copy-start.1 = (bf16[2,8,32]{2,1,0:T(8,128)(2,1)S(1)}, bf16[2,8,32]{2,1,0:T(8,128)(2,1)}, u32[]{:S(2)}) copy-start(bf16[2,8,32]{2,1,0:T(8,128)(2,1)} %param.13) | copy-start | bytes 3076
  206.3 2.7 %copy-start.2 = (s32[16,32]{1,0:T(8,128)S(1)}, s32[16,32]{1,0:T(8,128)}, u32[]{:S(2)}) copy-start(s32[16,32]{1,0:T(8,128)} %param.14) | copy-start | bytes 6148
  236.2 0.8 copy-start
Sparse Core Ops, SparseCore 0:
  209.1 22.7 all-gather.1
where the time goes:
time: 249 us; the launch traced here: 248 us
  matrix products  106 us (43%)
  local copies, waits for them, and re-layouts  82.2 us (33%)
  waiting for transfers between devices  25.9 us (10%)
  between operations  13.7 us (6%)
  other arithmetic  13.4 us (5%)
  starting transfers between devices  6.26 us (3%)
    conv_general_dilated x1, matrix products, align_block(): lax.conv_general_dilated(source, kernel, (1,), 'VALID', dimension_numbers...  103 us
    conv_general_dilated x7, local copies, waits for them, and re-layouts, align_block(): lax.conv_general_dilated(source, kernel, (1,), 'VALID', dimension_numbers...  31.2 us
    all_gather x1, waiting for transfers between devices, body(): gathered = lax.all_gather(beam_rows, 'pulse', axis=0, tiled=True)  22.7 us
    concatenate x1, local copies, waits for them, and re-layouts, padded_2(): jnp.concatenate([lax.ppermute(tail, axis, [(i, (i + 1) % count) for i in...  14.3 us
    another operation x1, other arithmetic  9.14 us
    slice x1, local copies, waits for them, and re-layouts, align_block(): real_part = cosine_values * summed[:, 0] - sine_values * summed[:, 1]  7.79 us
    reshape x2, local copies, waits for them, and re-layouts, align_block(): padded[:, :, 1:].astype(jnp.float32)  6.6 us
    slice x1, local copies, waits for them, and re-layouts, align_block(): padded[:, :, 1:].astype(jnp.float32)  6.51 us
  transfers between devices with their start and end apart: 3, of which 2 were waited for; matrix products, arithmetic and copies ran while one was open for 1% of the time, Pallas kernels for 0%

commit v1 on v0

v1 whole, which is shorter than its diff:
```python
import functools

import jax
import jax.numpy as jnp
from jax import lax
from jax.experimental import pallas as pl
from jax.experimental.pallas import tpu as pltpu
from jax.sharding import PartitionSpec as P

SUB = 32
BEAMS = 8
TAPS = 8
TILE_DEV = 4
FOOT = 32
AZ = 64
LANES = 128
ROWS = 264
GROUP = 128
UNROLL = 16


def beam_kernel(slots, first_row, segments, pulses, shift_ref, x_hbm, table_ref, factor_ref, steer_ref, out_ref, xbuf, aligned, demod, weights, products, sems):
    rows = 2 * slots
    subs = pulses // SUB

    def fetch(sub):
        window = pl.ds(sub * SUB, SUB)
        return pltpu.make_async_copy(
            x_hbm.at[window, pl.ds(first_row, rows), :], xbuf.at[window], sems.at[sub]
        )

    for sub in range(subs):
        fetch(sub).start()
    lane = lax.broadcasted_iota(jnp.int32, (rows, LANES), 1)
    for sub in range(subs):
        fetch(sub).wait()

        def align(step, carry, sub=sub):
            for inner in range(UNROLL):
                pulse = sub * SUB + step * UNROLL + inner
                offset = shift_ref[pulse] - 3
                rest = offset & (LANES - 1)
                block = offset >> 7
                here = xbuf[pulse].astype(jnp.float32)
                after = pltpu.roll(here, rows - 2, 0)
                mixed = jnp.where(lane >= rest, here, after)
                turned = pltpu.roll(mixed, (LANES - rest) & (LANES - 1), 1)
                aligned[pl.ds(pulse - 2 * block * ROWS, rows, stride=ROWS), :] = turned
            return carry

        lax.fori_loop(0, SUB // UNROLL, align, 0)

    lane8 = lax.broadcasted_iota(jnp.int32, (8, LANES), 1)
    steer_re, steer_im = steer_ref[0], steer_ref[1]
    for group in range(pulses // GROUP):
        window = pl.ds(group * GROUP, GROUP)
        base_cos, base_sin = table_ref[0, window, :], table_ref[1, window, :]
        cos_a, sin_a = base_cos[:, 127:128], base_sin[:, 127:128]
        cos_b, sin_b = base_cos[:, 1:2], base_sin[:, 1:2]
        step_cos = jnp.broadcast_to(cos_a * cos_b - sin_a * sin_b, (GROUP, LANES))
        step_sin = jnp.broadcast_to(sin_a * cos_b + cos_a * sin_b, (GROUP, LANES))
        for slot, blocks, region, column in segments:
            for tap in range(TAPS):
                fac_re = factor_ref[region, 0, tap : tap + 1, window]
                fac_im = factor_ref[region, 1, tap : tap + 1, window]
                w_re = steer_re * fac_re - steer_im * fac_im
                w_im = steer_re * fac_im + steer_im * fac_re
                for sub in range(GROUP // SUB):
                    keep = (lane8 >= sub * SUB) & (lane8 < (sub + 1) * SUB)
                    p_re = jnp.where(keep, w_re, 0.0)
                    p_im = jnp.where(keep, w_im, 0.0)
                    top = jnp.concatenate([p_re, 0.0 - p_im], axis=1)
                    low = jnp.concatenate([p_im, p_re], axis=1)
                    weights[pl.ds(tap * 64 + sub * 16, 16), :] = jnp.concatenate(
                        [top, low], axis=0
                    ).astype(jnp.bfloat16)
            cos_now, sin_now = base_cos, base_sin
            for block in range(blocks + 1):
                at = 2 * (slot + block) * ROWS + group * GROUP
                real = aligned[pl.ds(at, GROUP), :]
                imag = aligned[pl.ds(at + ROWS, GROUP), :]
                here = pl.ds(block * LANES, LANES)
                demod[0:GROUP, here] = (real * cos_now - imag * sin_now).astype(jnp.bfloat16)
                demod[GROUP : 2 * GROUP, here] = (real * sin_now + imag * cos_now).astype(jnp.bfloat16)
                if block < blocks:
                    cos_now, sin_now = (
                        cos_now * step_cos - sin_now * step_sin,
                        sin_now * step_cos + cos_now * step_sin,
                    )
            width = (blocks + 1) * LANES
            for start in range(0, width, 256):
                here = pl.ds(start, min(256, width - start))
                products[:, here] = jnp.dot(
                    weights[...], demod[:, here], preferred_element_type=jnp.float32
                )

            def combine(step, carry, blocks=blocks, group=group, column=column):
                row = pl.multiple_of(step * 8, 8)
                later = None
                for block in range(blocks, -1, -1):
                    turned = []
                    for tap in range(TAPS):
                        piece = products[pl.ds(tap * 64 + row, 8), pl.ds(block * LANES, LANES)]
                        turned.append(pltpu.roll(piece, LANES - tap, 1) if tap else piece)
                    if later is not None:
                        total = turned[0]
                        for tap in range(1, TAPS):
                            total = total + jnp.where(lane8 < LANES - tap, turned[tap], later[tap])
                        out_ref[pl.ds(group * 64 + row, 8), pl.ds(column + block * LANES, LANES)] = (
                            total.astype(jnp.bfloat16)
                        )
                    later = turned
                return carry

            lax.fori_loop(0, 8, combine, 0)


def make_beams(x3, shifts, table, factors, steer, slots, first_row, segments, name):
    pulses = x3.shape[0]
    blocks = max(seg[1] for seg in segments)
    width = sum(seg[1] for seg in segments) * LANES
    return pl.pallas_call(
        functools.partial(beam_kernel, slots, first_row, segments, pulses),
        name=name,
        out_shape=jax.ShapeDtypeStruct((pulses // 2, width), jnp.bfloat16),
        in_specs=[
            pl.BlockSpec(memory_space=pltpu.SMEM),
            pl.BlockSpec(memory_space=pl.ANY),
            pl.BlockSpec(memory_space=pltpu.VMEM),
            pl.BlockSpec(memory_space=pltpu.VMEM),
            pl.BlockSpec(memory_space=pltpu.VMEM),
        ],
        out_specs=pl.BlockSpec(memory_space=pltpu.VMEM),
        scratch_shapes=[
            pltpu.VMEM((pulses, 2 * slots, LANES), jnp.bfloat16),
            pltpu.VMEM((2 * (slots + 1) * ROWS, LANES), jnp.float32),
            pltpu.VMEM((2 * GROUP, (blocks + 1) * LANES), jnp.bfloat16),
            pltpu.VMEM((64 * TAPS, 2 * GROUP), jnp.bfloat16),
            pltpu.VMEM((64 * TAPS, (blocks + 1) * LANES), jnp.float32),
            pltpu.SemaphoreType.DMA((pulses // SUB,)),
        ],
        cost_estimate=pl.CostEstimate(flops=2000000000, bytes_accessed=8000000, transcendentals=0),
    )(shifts, x3, table, factors, steer)


def expand_kernel(where_ref, coeff_ref, out_ref):
    width = out_ref.shape[1]
    lane = lax.broadcasted_iota(jnp.int32, (FOOT, width), 1)
    dims = (((0,), (0,)), ((), ()))
    for tile in range(TILE_DEV):
        spot = where_ref[pl.ds(tile * FOOT, FOOT), :]
        hot_re = (lane == spot).astype(jnp.float32).astype(jnp.bfloat16)
        hot_im = (lane == spot + BEAMS).astype(jnp.float32).astype(jnp.bfloat16)
        c_re, c_im = coeff_ref[tile, 0], coeff_ref[tile, 1]
        dot = functools.partial(lax.dot_general, dimension_numbers=dims, preferred_element_type=jnp.float32)
        at = tile * 2 * AZ
        out_ref[pl.ds(at, AZ), :] = (dot(c_re, hot_re) - dot(c_im, hot_im)).astype(jnp.bfloat16)
        out_ref[pl.ds(at + AZ, AZ), :] = (dot(c_im, hot_re) + dot(c_re, hot_im)).astype(jnp.bfloat16)


def project_kernel(count, pieces, coeff_ref, *refs):
    sources = refs[:count]
    out_hbm, tile, sems = refs[-3], refs[-2], refs[-1]
    depth = sources[0].shape[0]
    copies = []
    for index, (source, target, width) in enumerate(pieces):
        for start in range(0, width, 256):
            size = min(256, width - start)
            here = pl.ds(source + start, size)
            total = None
            for first in range(0, count, 2):
                data = jnp.concatenate([ref[:, here] for ref in sources[first : first + 2]], axis=0)
                term = jnp.dot(
                    coeff_ref[:, first * depth : (first + 2) * depth], data, preferred_element_type=jnp.float32
                )
                total = term if total is None else total + term
            tile[:, here] = total.astype(jnp.bfloat16)
        copy = pltpu.make_async_copy(
            tile.at[:, pl.ds(source, width)], out_hbm.at[:, pl.ds(target, width)], sems.at[index]
        )
        copy.start()
        copies.append(copy)
    for copy in copies:
        copy.wait()


def project(coeffs, sources, image, pieces, cells, name):
    count = len(sources)
    width = sources[0].shape[1]
    rows = coeffs.shape[0]
    any_spec = pl.BlockSpec(memory_space=pl.ANY)
    vmem = pl.BlockSpec(memory_space=pltpu.VMEM)
    extra = [] if image is None else [image]
    return pl.pallas_call(
        functools.partial(project_kernel, count, pieces),
        name=name,
        out_shape=jax.ShapeDtypeStruct((rows, cells), jnp.bfloat16),
        in_specs=[vmem] * (1 + count) + [any_spec] * len(extra),
        out_specs=any_spec,
        input_output_aliases={1 + count: 0} if extra else {},
        scratch_shapes=[
            pltpu.VMEM((rows, width), jnp.bfloat16),
            pltpu.SemaphoreType.DMA((len(pieces),)),
        ],
        cost_estimate=pl.CostEstimate(
            flops=2 * rows * width * count * sources[0].shape[0], bytes_accessed=3000000, transcendentals=0
        ),
    )(coeffs, *sources, *extra)


def body(echoes, shifts, tap_weights, angles, slopes, steering, footprint, tile_coeffs):
    pulses, _, cells = echoes.shape
    blocks = cells // LANES
    pulse_count = lax.axis_size("pulse")
    range_count = lax.axis_size("range")
    me = lax.axis_index("pulse")
    start_cell = lax.axis_index("range") * cells

    x4 = echoes.reshape(pulses, 2, blocks, LANES).transpose(0, 2, 1, 3)
    ends = range_count - 1
    left = lax.ppermute(x4[:, blocks - 1 :], "range", [(i, i + 1) for i in range(ends)])
    right = lax.ppermute(x4[:, :1], "range", [(i + 1, i) for i in range(ends)])

    half = blocks // 2
    origins = [1, half - 1, 0, blocks - 1]
    taps = jnp.arange(TAPS, dtype=jnp.int32)
    cell = (start_cell + LANES * jnp.array(origins, dtype=jnp.int32)[:, None] - taps[None, :]).astype(jnp.float32)
    phases = angles[None, None, :] + slopes[None, None, :] * cell[:, :, None]
    tap_rows = tap_weights.T[None]
    factors = jnp.stack([tap_rows * jnp.cos(phases), tap_rows * jnp.sin(phases)], axis=1)
    turn = slopes[:, None] * jnp.arange(LANES, dtype=jnp.float32)[None, :]
    table = jnp.stack([jnp.cos(turn), jnp.sin(turn)])
    steer = jnp.tile(steering.astype(jnp.float32), (1, 1, GROUP // SUB))

    x3 = x4.reshape(pulses, 2 * blocks, LANES)
    beams = [
        make_beams(x3, shifts, table, factors, steer, half, 0, ((1, half - 2, 0, 0),), "beams_a"),
        make_beams(x3, shifts, table, factors, steer, half + 4, 2 * (half - 4), ((3, half, 1, 0),), "beams_b"),
    ]
    edge = jnp.concatenate([left, x4[:, :3], x4[:, blocks - 3 :], right], axis=1)
    edge = edge.reshape(pulses, 16, LANES)
    beams.append(
        make_beams(edge, shifts, table, factors, steer, 8, 0, ((1, 1, 2, 0), (6, 1, 3, LANES)), "beams_c")
    )
    inner = (half - 2) * LANES
    pieces = [
        ((0, LANES, inner),),
        ((0, (half - 1) * LANES, half * LANES),),
        ((0, 0, LANES), (LANES, (blocks - 1) * LANES, LANES)),
    ]

    entries = TILE_DEV * FOOT
    chips = pulse_count // 2
    beam_dev = pulses // SUB * BEAMS
    ids = lax.dynamic_index_in_dim(footprint.reshape(pulse_count, entries), me, 0, keepdims=False)
    owner = ids // beam_dev
    inside = ids % beam_dev
    place = 2 * ((me // 2 - owner // 2) % chips) + (me % 2 + owner % 2) % 2
    where = place * (2 * beam_dev) + (inside // BEAMS) * (2 * BEAMS) + inside % BEAMS
    coeffs = pl.pallas_call(
        expand_kernel,
        name="expand",
        out_shape=jax.ShapeDtypeStruct((TILE_DEV * 2 * AZ, pulse_count * 2 * beam_dev), jnp.bfloat16),
    )(where[:, None], tile_coeffs.transpose(0, 1, 3, 2))

    swap = [(i, i ^ 1) for i in range(pulse_count)]
    image = None
    for index, own in enumerate(beams):
        sources = []
        for hop in range(chips):
            ahead = own
            if hop:
                ahead = lax.ppermute(own, "pulse", [(i, (i + 2 * hop) % pulse_count) for i in range(pulse_count)])
            sources += [ahead, lax.ppermute(ahead, "pulse", swap)]
        image = project(coeffs, sources, image, pieces[index], cells, "project_" + "abc"[index])
    return image.reshape(TILE_DEV, 2, AZ, cells)


def solution(mesh):
    placed = (
        P(("groups", "pulse"), None, "range"),
        P(("groups", "pulse")),
        P(("groups", "pulse"), None),
        P(("groups", "pulse")),
        P(("groups", "pulse")),
        P(),
        P("groups", None),
        P(("groups", "pulse"), None, None, None),
    )
    return jax.shard_map(
        body,
        mesh=mesh,
        in_specs=placed,
        out_specs=P(("groups", "pulse"), None, None, "range"),
        check_vma=False,
    )
```

time: 249 us -> 62.9 us (0.25)
  matrix products: 106 us -> 0 us
  local copies, waits for them, and re-layouts: 82.2 us -> 8.08 us
  Pallas kernels: 0 us -> 35.3 us
  waiting for transfers between devices: 25.9 us -> 0.03 us
  between operations: 13.7 us -> 0.2 us
  other arithmetic: 13.4 us -> 7.57 us
  starting transfers between devices: 6.26 us -> 11.1 us
    conv_general_dilated x1 -> x0, matrix products: 103 us -> none  [align_block(): lax.conv_general_dilated(source, kernel, (1,), 'VALID', dimension_numbers...]
    pallas_call x0 -> x7, Pallas kernels: none -> 35.3 us  [the longest x3 25.1 us: make_beams(): pl.pallas_call(functools.partial(beam_kernel, slots, first_row, segments,...]
    conv_general_dilated x7 -> x0, local copies, waits for them, and re-layouts: 31.2 us -> none  [align_block(): lax.conv_general_dilated(source, kernel, (1,), 'VALID', dimension_numbers...]
    all_gather x1 -> x0, waiting for transfers between devices: 22.7 us -> none  [body(): gathered = lax.all_gather(beam_rows, 'pulse', axis=0, tiled=True)]
    concatenate x1 -> x0, local copies, waits for them, and re-layouts: 14.3 us -> none  [padded_2(): jnp.concatenate([lax.ppermute(tail, axis, [(i, (i + 1) % count) for i in...]
    slice x3 -> x2, local copies, waits for them, and re-layouts: 15.5 us -> 2.83 us  [the longest x1 1.66 us: body(): edge = jnp.concatenate([left, x4[:, :3], x4[:, blocks - 3:], right], axis=1)]
    reshape x4 -> x1, local copies, waits for them, and re-layouts: 12.5 us -> 0.08 us  [body(): footprint.reshape(pulse_count, entries)]
    another operation x3 -> x2, other arithmetic: 11.3 us -> 1.35 us  [the longest x1 0.73 us: body(): table = jnp.stack([jnp.cos(turn), jnp.sin(turn)])]
  transfers between devices with their start and end apart: 3 -> 11, of which waited for: 2 -> 0; matrix products, arithmetic and copies ran while one was open for 1% -> 10% of each run, Pallas kernels for 0% -> 40%
where the time goes in v1:
time: 62.9 us; the launch traced here: 62.3 us
  Pallas kernels  35.3 us (56%)
  starting transfers between devices  11.1 us (18%)
  local copies, waits for them, and re-layouts  8.08 us (13%)
  other arithmetic  7.57 us (12%)
    pallas_call x3, Pallas kernels, make_beams(): pl.pallas_call(functools.partial(beam_kernel, slots, first_row, segments,...  25.1 us
    pallas_call x3, Pallas kernels, project(): pl.pallas_call(functools.partial(project_kernel, count, pieces), name=nam...  8.11 us
    ppermute x3, starting transfers between devices, body(): lax.ppermute(own, 'pulse', [(i, (i + 2 * hop) % pulse_count) for i in ran...  5.19 us
    unnamed x20, local copies, waits for them, and re-layouts  3.68 us
    ppermute x1, starting transfers between devices, body(): lax.ppermute(x4[:, blocks - 1:], 'range', [(i, i + 1) for i in range(ends)])  3.49 us
    concatenate x1, other arithmetic, body(): edge = jnp.concatenate([left, x4[:, :3], x4[:, blocks - 3:], right], axis=1)  2.48 us
    pallas_call x1, Pallas kernels, body(): pl.pallas_call(expand_kernel, name='expand', out_shape=jax.ShapeDtypeStru...  2.17 us
    slice x1, local copies, waits for them, and re-layouts, body(): edge = jnp.concatenate([left, x4[:, :3], x4[:, blocks - 3:], right], axis=1)  1.66 us
  transfers between devices with their start and end apart: 11, of which 0 were waited for; matrix products, arithmetic and copies ran while one was open for 10% of the time, Pallas kernels for 40%

profile of v1, /device:TPU:0, one launch (start us, length us, event | category | flops | bytes accessed | tf_op | source)
XLA Modules:
  0.0 62.3 jit_solution(2614162624634962218)
XLA Ops:
  0.0 0.7 %broadcast_add_fusion = s32[4]{0:T(128)S(1)} fusion(s32[4]{0:T(128)} %constant.115, s32[]{:T(128)S(6)} %mul.130), kind=kLoop, calls=%fused_computation.51 | loop fusion | flops 4 | bytes 36 | tf_op jit(solution)/shard_map/add | solution.py:227
  0.7 0.1 subtract_convert_fusion
  0.7 0.7 %tile.4 = f32[2,8,4,32]{3,2,1,0:T(4,128)S(1)} broadcast(bf16[2,8,32]{2,1,0:T(8,128)(2,1)} %param.14), dimensions={0,1,3} | broadcast | bytes 9216 | tf_op jit(solution)/shard_map/tile | solution.py:233
  1.4 0.7 %tile.10.steer_ref = f32[2,8,128]{2,1,0:T(8,128)} reshape(f32[2,8,4,32]{3,2,1,0:T(4,128)S(1)} %tile.4) | data formatting | bytes 16384 | tf_op jit(solution)/shard_map/tile | solution.py:233
  2.1 1.2 %fusion.1 = (f32[1,256,128]{2,1,0:T(8,128)S(1)}, f32[1,256,128]{2,1,0:T(8,128)S(1)}) fusion(f32[256]{0:T(256)} %param.13), kind=kLoop, calls=%fused_computation.4 | loop fusion | flops 32768 | bytes 263168 | tf_op jit(solution)/shard_map/cos | solution.py:232
  3.3 0.9 %cosine_multiply_fusion = (f32[4,1,8,256]{3,2,1,0:T(8,128)S(1)}, f32[4,1,8,256]{3,2,1,0:T(8,128)S(1)}) fusion(f32[4,8]{1,0:T(4,128)S(1)} %subtract_convert_fusion, f32[256]{0:T(256)} %param.13, f32[256]{0:T(256)} %param.12, f32[8,256]{1,0:T(8,128)} %bitcast.17), kind=kLoop, calls=%fused_computation.47 | loop fusion | flops 32768 | bytes 75904 | tf_op jit(solution)/shard_map/mul | solution.py:230
  4.3 0.6 %pad_maximum_fusion.2.factor_ref = f32[4,2,8,256]{3,2,1,0:T(8,128)} fusion(f32[4,1,8,256]{3,2,1,0:T(8,128)S(1)} %get-tuple-element.10, f32[4,1,8,256]{3,2,1,0:T(8,128)S(1)} %get-tuple-element.9), kind=kLoop, calls=%fused_computation.36 | loop fusion | flops 16384 | bytes 131072 | tf_op jit(solution)/shard_map/stack | solution.py:230
  4.9 0.7 %pad_maximum_fusion.1.table_ref = f32[2,256,128]{2,1,0:T(8,128)} fusion(f32[1,256,128]{2,1,0:T(8,128)S(1)} %get-tuple-element.12, f32[1,256,128]{2,1,0:T(8,128)S(1)} %get-tuple-element.11), kind=kLoop, calls=%fused_computation.1 | loop fusion | flops 65536 | bytes 524288 | tf_op jit(solution)/shard_map/stack | solution.py:232
  5.6 7.9 %beams_a.1.refs_0_ = bf16[128,768]{1,0:T(8,128)(2,1)} custom-call(s32[256]{0:T(256)} %shift_ref.5, bf16[256,32,128]{2,1,0:T(8,128)(2,1)} %bitcast.12, f32[2,256,128]{2,1,0:T(8,128)} %pad_maximum_fusion.1.table_ref, f32[4,2,8,256]{3,2,1,0:T(8,128)} %pad_maximum_fusion.2.factor_ref, f32[2,8,128]{2,1,0:T(8,128)} %tile.10.steer_ref), custom_call_target="tpu_custom_call" | custom-call | flops 2000000000 | bytes 8000000 | tf_op jit(solution)/shard_map/beams_a/pallas_call | solution.py:122
  13.5 3.0 %collective-permute-start.9 = (bf16[128,768]{1,0:T(8,128)(2,1)}, bf16[128,768]{1,0:T(8,128)(2,1)S(1)}, u32[]{:S(2)}, u32[]{:S(2)}) collective-permute-start(bf16[128,768]{1,0:T(8,128)(2,1)} %beams_a.1.refs_0_), channel_id=1, source_target_pairs={{0,8},{4,12},{8,0},{12,4},{1,9},{5,13},{9,1},{13,5},{2,10},{6,14},... | collective-permute-start | bytes 589832 | tf_op jit(solution)/shard_map/ppermute | solution.py:273
  16.6 0.0 collective-permute-start.8
  16.6 1.2 %fusion.18 = (bf16[256,1,2,128]{3,2,1,0:T(2,128)(2,1)S(1)}, bf16[256,1,2,128]{3,2,1,0:T(2,128)(2,1)S(1)}) fusion(bf16[256,16,2,128]{3,2,1,0:T(2,128)(2,1)} %bitcast.13), kind=kLoop, calls=%fused_computation.52 | loop fusion | bytes 524288 | tf_op jit(solution)/shard_map/slice | solution.py:221
  17.8 3.5 %collective-permute-start = (bf16[256,1,2,128]{3,2,1,0:T(2,128)(2,1)S(1)}, bf16[256,1,2,128]{3,2,1,0:T(2,128)(2,1)S(1)}, u32[]{:S(2)}, u32[]{:S(2)}) collective-permute-start(bf16[256,1,2,128]{3,2,1,0:T(2,128)(2,1)S(1)} %get-tuple-element.5), channel_id=1, source_target_pairs={{0,1},{1,2},{2,3},{4,5},{5,6},{6,7},{8,9},{9,10},{10,11},{12,13},{... | collective-permute-start | bytes 393224 | tf_op jit(solution)/shard_map/ppermute | solution.py:221
  21.2 0.0 copy-start.9
  21.3 1.3 %collective-permute-start.1 = (bf16[256,1,2,128]{3,2,1,0:T(2,128)(2,1)S(1)}, bf16[256,1,2,128]{3,2,1,0:T(2,128)(2,1)S(1)}, u32[]{:S(2)}, u32[]{:S(2)}) collective-permute-start(bf16[256,1,2,128]{3,2,1,0:T(2,128)(2,1)S(1)} %get-tuple-element.6), channel_id=1, source_target_pairs={{1,0},{2,1},{3,2},{5,4},{6,5},{7,6},{9,8},{10,9},{11,10},{13,12},{... | collective-permute-start | bytes 393224 | tf_op jit(solution)/shard_map/ppermute | solution.py:222
  22.6 8.6 %beams_b.1.refs_0_ = bf16[128,1024]{1,0:T(8,128)(2,1)} custom-call(s32[256]{0:T(256)} %shift_ref.5, bf16[256,32,128]{2,1,0:T(8,128)(2,1)} %bitcast.14, f32[2,256,128]{2,1,0:T(8,128)} %pad_maximum_fusion.1.table_ref, f32[4,2,8,256]{3,2,1,0:T(8,128)} %pad_maximum_fusion.2.factor_ref, f32[2,8,128]{2,1,0:T(8,128)} %tile.10.steer_ref), custom_call_target="tpu_custom_call" | custom-call | flops 2000000000 | bytes 8000000 | tf_op jit(solution)/shard_map/beams_b/pallas_call | solution.py:122
  31.1 0.6 collective-permute-start.6
  31.7 0.0 copy-done.9
  31.7 0.1 reshape.437
  31.8 0.1 copy.12
  31.9 1.7 %fusion.19 = (bf16[256,3,2,128]{3,2,1,0:T(2,128)(2,1)S(1)}, bf16[256,3,2,128]{3,2,1,0:T(2,128)(2,1)S(1)}) fusion(bf16[256,16,2,128]{3,2,1,0:T(2,128)(2,1)} %bitcast.15), kind=kLoop, calls=%fused_computation.53 | loop fusion | bytes 1572864 | tf_op jit(solution)/shard_map/slice | solution.py:240
  33.6 0.0 collective-permute-done
  33.6 0.1 collective-permute-start.5
  33.7 0.0 collective-permute-done.1
  33.7 2.5 %pad_maximum_fusion = bf16[256,8,2,128]{3,2,1,0:T(2,128)(2,1)} fusion(bf16[256,1,2,128]{3,2,1,0:T(2,128)(2,1)S(1)} %collective-permute-done.1, bf16[256,3,2,128]{3,2,1,0:T(2,128)(2,1)S(1)} %get-tuple-element.8, bf16[256,3,2,128]{3,2,1,0:T(2,128)(2,1)S(1)} %get-tuple-element.7, bf16[256,1,2,128]{3,2,1,0:T(2,128)(2,1)S(1)} %collective-permute-done), kind=kLoop, calls=%fused_computation | loop fusion | flops 1572864 | bytes 2097152 | tf_op jit(solution)/shard_map/concatenate | solution.py:240
  36.2 8.6 %beams_c.1.refs_0_ = bf16[128,256]{1,0:T(8,128)(2,1)} custom-call(s32[256]{0:T(256)} %shift_ref.5, bf16[256,16,128]{2,1,0:T(8,128)(2,1)} %bitcast.11, f32[2,256,128]{2,1,0:T(8,128)} %pad_maximum_fusion.1.table_ref, f32[4,2,8,256]{3,2,1,0:T(8,128)} %pad_maximum_fusion.2.factor_ref, f32[2,8,128]{2,1,0:T(8,128)} %tile.10.steer_ref), custom_call_target="tpu_custom_call" | custom-call | flops 2000000000 | bytes 8000000 | tf_op jit(solution)/shard_map/beams_c/pallas_call | solution.py:122
  44.8 1.6 %collective-permute-start.3 = (bf16[128,256]{1,0:T(8,128)(2,1)}, bf16[128,256]{1,0:T(8,128)(2,1)S(1)}, u32[]{:S(2)}, u32[]{:S(2)}) collective-permute-start(bf16[128,256]{1,0:T(8,128)(2,1)} %beams_c.1.refs_0_), channel_id=1, source_target_pairs={{0,8},{4,12},{8,0},{12,4},{1,9},{5,13},{9,1},{13,5},{2,10},{6,14},... | collective-permute-start | bytes 196616 | tf_op jit(solution)/shard_map/ppermute | solution.py:273
  46.3 0.0 collective-permute-done.9.refs_2_
  46.3 0.0 copy-start.3
  46.3 0.2 collective-permute-start.10
  46.5 0.0 collective-permute-done.6.refs_2_
  46.5 0.0 copy-start
  46.5 0.3 collective-permute-start.7
  46.8 0.9 %fusion.8.where_ref = s32[128,1]{1,0:T(8,128)} fusion(s32[128,1]{1,0:T(8,128)S(1)} %copy.12, s32[]{:T(128)S(6)} %select_n.109, s32[]{:T(128)S(6)} %select_n.104), kind=kLoop, calls=%fused_computation.32 | loop fusion | flops 11136 | bytes 1032 | tf_op jit(solution)/shard_map/add | solution.py:259
  47.7 2.2 %expand.1.coeff_ref = bf16[512,512]{1,0:T(8,128)(2,1)} custom-call(s32[128,1]{1,0:T(8,128)} %fusion.8.where_ref, bf16[4,2,32,64]{3,2,1,0:T(8,128)(2,1)} %bitcast.16), custom_call_target="tpu_custom_call" | custom-call | tf_op jit(solution)/shard_map/expand/pallas_call | solution.py:260
  49.9 0.0 collective-permute-done.3.refs_2_
  49.9 0.0 copy-start.6
  49.9 0.2 collective-permute-start.2
  50.1 0.0 collective-permute-done.8.refs_1_
  50.1 0.0 copy-start.4
  50.1 0.3 collective-permute-start.4
  50.4 0.0 collective-permute-done.10.refs_3_
  50.4 0.0 copy-done.3
  50.4 0.4 copy-done.4
  50.8 0.0 copy-start.5
  50.8 0.7 %copy-done.5 = bf16[128,768]{1,0:T(8,128)(2,1)} copy-done((bf16[128,768]{1,0:T(8,128)(2,1)}, bf16[128,768]{1,0:T(8,128)(2,1)S(1)}, u32[]{:S(2)}) %copy-start.5) | copy-done | bytes 196632
  51.4 2.8 %project_a.1.refs_4_ = bf16[512,2048]{1,0:T(8,128)(2,1)} custom-call(bf16[512,512]{1,0:T(8,128)(2,1)} %expand.1.coeff_ref, bf16[128,768]{1,0:T(8,128)(2,1)} %beams_a.1.refs_0_, bf16[128,768]{1,0:T(8,128)(2,1)} %copy-done.4, bf16[128,768]{1,0:T(8,128)(2,1)} %copy-done.3, bf16[128,768]{1,0:T(8,128)(2,1)} %copy-done.5), custom_call_target="tpu_custom_call" | custom-call | flops 402653184 | bytes 3000000 | tf_op jit(solution)/shard_map/project_a/pallas_call | solution.py:194
  54.3 0.0 copy-done
  54.3 0.0 collective-permute-done.5.refs_1_
  54.3 0.0 copy-start.1
  54.3 0.0 collective-permute-done.7.refs_3_
  54.3 0.7 %copy-done.1 = bf16[128,1024]{1,0:T(8,128)(2,1)} copy-done((bf16[128,1024]{1,0:T(8,128)(2,1)}, bf16[128,1024]{1,0:T(8,128)(2,1)S(1)}, u32[]{:S(2)}) %copy-start.1) | copy-done | bytes 262168
  55.0 0.0 copy-start.2
  55.0 0.7 %copy-done.2 = bf16[128,1024]{1,0:T(8,128)(2,1)} copy-done((bf16[128,1024]{1,0:T(8,128)(2,1)}, bf16[128,1024]{1,0:T(8,128)(2,1)S(1)}, u32[]{:S(2)}) %copy-start.2) | copy-done | bytes 262168
  55.7 3.0 %project_b.1.refs_4_ = bf16[512,2048]{1,0:T(8,128)(2,1)} custom-call(bf16[512,512]{1,0:T(8,128)(2,1)} %expand.1.coeff_ref, bf16[128,1024]{1,0:T(8,128)(2,1)} %beams_b.1.refs_0_, bf16[128,1024]{1,0:T(8,128)(2,1)} %copy-done.1, bf16[128,1024]{1,0:T(8,128)(2,1)} %copy-done, bf16[128,1024]{1,0:T(8,128)(2,1)} %copy-done.2, ...), custom_call_target="tpu_custom_call", output_to_operand_aliasing={{}: (5, {})} | custom-call | flops 536870912 | bytes 3000000 | tf_op jit(solution)/shard_map/project_b/pallas_call | solution.py:194
  58.7 0.0 collective-permute-done.2.refs_1_
  58.7 0.0 copy-start.7
  58.7 0.0 collective-permute-done.4.refs_3_
  58.7 0.0 copy-done.6
  58.8 0.6 copy-done.7
  59.4 0.0 copy-start.8
  59.4 0.6 %copy-done.8 = bf16[128,256]{1,0:T(8,128)(2,1)} copy-done((bf16[128,256]{1,0:T(8,128)(2,1)}, bf16[128,256]{1,0:T(8,128)(2,1)S(1)}, u32[]{:S(2)}) %copy-start.8) | copy-done | bytes 65560
  60.0 2.3 %project_c.1 = bf16[512,2048]{1,0:T(8,128)(2,1)} custom-call(bf16[512,512]{1,0:T(8,128)(2,1)} %expand.1.coeff_ref, bf16[128,256]{1,0:T(8,128)(2,1)} %beams_c.1.refs_0_, bf16[128,256]{1,0:T(8,128)(2,1)} %copy-done.7, bf16[128,256]{1,0:T(8,128)(2,1)} %copy-done.6, bf16[128,256]{1,0:T(8,128)(2,1)} %copy-done.8, ...), custom_call_target="tpu_custom_call", output_to_operand_aliasing={{}: (5, {})} | custom-call | flops 134217728 | bytes 3000000 | tf_op jit(solution)/shard_map/project_c/pallas_call | solution.py:194
  (1 shorter events, 0.0 us)
Async XLA Ops:
  13.5 32.8 %collective-permute-start.9 = (bf16[128,768]{1,0:T(8,128)(2,1)}, bf16[128,768]{1,0:T(8,128)(2,1)S(1)}, u32[]{:S(2)}, u32[]{:S(2)}) collective-permute-start(bf16[128,768]{1,0:T(8,128)(2,1)} %beams_a.1.refs_0_), channel_id=1, source_target_pairs={{0,8},{4,12},{8,0},{12,4},{1,9},{5,13},{9,1},{13,5},{2,10},{6,14},... | collective-permute-start | bytes 589832 | tf_op jit(solution)/shard_map/ppermute | solution.py:273
  16.6 33.5 %collective-permute-start.8 = (bf16[128,768]{1,0:T(8,128)(2,1)}, bf16[128,768]{1,0:T(8,128)(2,1)S(1)}, u32[]{:S(2)}, u32[]{:S(2)}) collective-permute-start(bf16[128,768]{1,0:T(8,128)(2,1)} %beams_a.1.refs_0_), channel_id=1, source_target_pairs={{0,4},{4,0},{8,12},{12,8},{1,5},{5,1},{9,13},{13,9},{2,6},{6,2},{1... | collective-permute-start | bytes 589832 | tf_op jit(solution)/shard_map/ppermute | solution.py:274
  17.8 15.8 %collective-permute-start = (bf16[256,1,2,128]{3,2,1,0:T(2,128)(2,1)S(1)}, bf16[256,1,2,128]{3,2,1,0:T(2,128)(2,1)S(1)}, u32[]{:S(2)}, u32[]{:S(2)}) collective-permute-start(bf16[256,1,2,128]{3,2,1,0:T(2,128)(2,1)S(1)} %get-tuple-element.5), channel_id=1, source_target_pairs={{0,1},{1,2},{2,3},{4,5},{5,6},{6,7},{8,9},{9,10},{10,11},{12,13},{... | collective-permute-start | bytes 393224 | tf_op jit(solution)/shard_map/ppermute | solution.py:221
  21.2 10.5 %copy-start.9 = (s32[16,32]{1,0:T(8,128)S(1)}, s32[16,32]{1,0:T(8,128)}, u32[]{:S(2)}) copy-start(s32[16,32]{1,0:T(8,128)} %param.15) | copy-start | bytes 6148
  21.3 12.4 %collective-permute-start.1 = (bf16[256,1,2,128]{3,2,1,0:T(2,128)(2,1)S(1)}, bf16[256,1,2,128]{3,2,1,0:T(2,128)(2,1)S(1)}, u32[]{:S(2)}, u32[]{:S(2)}) collective-permute-start(bf16[256,1,2,128]{3,2,1,0:T(2,128)(2,1)S(1)} %get-tuple-element.6), channel_id=1, source_target_pairs={{1,0},{2,1},{3,2},{5,4},{6,5},{7,6},{9,8},{10,9},{11,10},{13,12},{... | collective-permute-start | bytes 393224 | tf_op jit(solution)/shard_map/ppermute | solution.py:222
  31.1 15.4 %collective-permute-start.6 = (bf16[128,1024]{1,0:T(8,128)(2,1)}, bf16[128,1024]{1,0:T(8,128)(2,1)S(1)}, u32[]{:S(2)}, u32[]{:S(2)}) collective-permute-start(bf16[128,1024]{1,0:T(8,128)(2,1)} %beams_b.1.refs_0_), channel_id=1, source_target_pairs={{0,8},{4,12},{8,0},{12,4},{1,9},{5,13},{9,1},{13,5},{2,10},{6,14},... | collective-permute-start | bytes 786440 | tf_op jit(solution)/shard_map/ppermute | solution.py:273
  33.6 20.7 %collective-permute-start.5 = (bf16[128,1024]{1,0:T(8,128)(2,1)}, bf16[128,1024]{1,0:T(8,128)(2,1)S(1)}, u32[]{:S(2)}, u32[]{:S(2)}) collective-permute-start(bf16[128,1024]{1,0:T(8,128)(2,1)} %beams_b.1.refs_0_), channel_id=1, source_target_pairs={{0,4},{4,0},{8,12},{12,8},{1,5},{5,1},{9,13},{13,9},{2,6},{6,2},{1... | collective-permute-start | bytes 786440 | tf_op jit(solution)/shard_map/ppermute | solution.py:274
  44.8 5.1 %collective-permute-start.3 = (bf16[128,256]{1,0:T(8,128)(2,1)}, bf16[128,256]{1,0:T(8,128)(2,1)S(1)}, u32[]{:S(2)}, u32[]{:S(2)}) collective-permute-start(bf16[128,256]{1,0:T(8,128)(2,1)} %beams_c.1.refs_0_), channel_id=1, source_target_pairs={{0,8},{4,12},{8,0},{12,4},{1,9},{5,13},{9,1},{13,5},{2,10},{6,14},... | collective-permute-start | bytes 196616 | tf_op jit(solution)/shard_map/ppermute | solution.py:273
  46.3 4.1 %copy-start.3 = (bf16[128,768]{1,0:T(8,128)(2,1)}, bf16[128,768]{1,0:T(8,128)(2,1)S(1)}, u32[]{:S(2)}) copy-start(bf16[128,768]{1,0:T(8,128)(2,1)S(1)} %collective-permute-done.9.refs_2_) | copy-start | bytes 589828
  46.3 4.1 %collective-permute-start.10 = (bf16[128,768]{1,0:T(8,128)(2,1)S(1)}, bf16[128,768]{1,0:T(8,128)(2,1)S(1)}, u32[]{:S(2)}, u32[]{:S(2)}) collective-permute-start(bf16[128,768]{1,0:T(8,128)(2,1)S(1)} %collective-permute-done.9.refs_2_), channel_id=1, source_target_pairs={{0,4},{4,0},{8,12},{12,8},{1,5},{5,1},{9,13},{13,9},{2,6},{6,2},{1... | collective-permute-start | bytes 589832 | tf_op jit(solution)/shard_map/ppermute | solution.py:274
  46.5 7.7 %copy-start = (bf16[128,1024]{1,0:T(8,128)(2,1)}, bf16[128,1024]{1,0:T(8,128)(2,1)S(1)}, u32[]{:S(2)}) copy-start(bf16[128,1024]{1,0:T(8,128)(2,1)S(1)} %collective-permute-done.6.refs_2_) | copy-start | bytes 786436
  46.5 7.8 %collective-permute-start.7 = (bf16[128,1024]{1,0:T(8,128)(2,1)S(1)}, bf16[128,1024]{1,0:T(8,128)(2,1)S(1)}, u32[]{:S(2)}, u32[]{:S(2)}) collective-permute-start(bf16[128,1024]{1,0:T(8,128)(2,1)S(1)} %collective-permute-done.6.refs_2_), channel_id=1, source_target_pairs={{0,4},{4,0},{8,12},{12,8},{1,5},{5,1},{9,13},{13,9},{2,6},{6,2},{1... | collective-permute-start | bytes 786440 | tf_op jit(solution)/shard_map/ppermute | solution.py:274
  49.9 8.9 %copy-start.6 = (bf16[128,256]{1,0:T(8,128)(2,1)}, bf16[128,256]{1,0:T(8,128)(2,1)S(1)}, u32[]{:S(2)}) copy-start(bf16[128,256]{1,0:T(8,128)(2,1)S(1)} %collective-permute-done.3.refs_2_) | copy-start | bytes 196612
  49.9 8.8 %collective-permute-start.2 = (bf16[128,256]{1,0:T(8,128)(2,1)}, bf16[128,256]{1,0:T(8,128)(2,1)S(1)}, u32[]{:S(2)}, u32[]{:S(2)}) collective-permute-start(bf16[128,256]{1,0:T(8,128)(2,1)} %beams_c.1.refs_0_), channel_id=1, source_target_pairs={{0,4},{4,0},{8,12},{12,8},{1,5},{5,1},{9,13},{13,9},{2,6},{6,2},{1... | collective-permute-start | bytes 196616 | tf_op jit(solution)/shard_map/ppermute | solution.py:274
  50.1 0.7 %copy-start.4 = (bf16[128,768]{1,0:T(8,128)(2,1)}, bf16[128,768]{1,0:T(8,128)(2,1)S(1)}, u32[]{:S(2)}) copy-start(bf16[128,768]{1,0:T(8,128)(2,1)S(1)} %collective-permute-done.8.refs_1_) | copy-start | bytes 589828
  50.1 8.7 %collective-permute-start.4 = (bf16[128,256]{1,0:T(8,128)(2,1)S(1)}, bf16[128,256]{1,0:T(8,128)(2,1)S(1)}, u32[]{:S(2)}, u32[]{:S(2)}) collective-permute-start(bf16[128,256]{1,0:T(8,128)(2,1)S(1)} %collective-permute-done.3.refs_2_), channel_id=1, source_target_pairs={{0,4},{4,0},{8,12},{12,8},{1,5},{5,1},{9,13},{13,9},{2,6},{6,2},{1... | collective-permute-start | bytes 196616 | tf_op jit(solution)/shard_map/ppermute | solution.py:274
  50.8 0.7 %copy-start.5 = (bf16[128,768]{1,0:T(8,128)(2,1)}, bf16[128,768]{1,0:T(8,128)(2,1)S(1)}, u32[]{:S(2)}) copy-start(bf16[128,768]{1,0:T(8,128)(2,1)S(1)} %collective-permute-done.10.refs_3_) | copy-start | bytes 589828
  54.3 0.7 %copy-start.1 = (bf16[128,1024]{1,0:T(8,128)(2,1)}, bf16[128,1024]{1,0:T(8,128)(2,1)S(1)}, u32[]{:S(2)}) copy-start(bf16[128,1024]{1,0:T(8,128)(2,1)S(1)} %collective-permute-done.5.refs_1_) | copy-start | bytes 786436
  55.0 0.7 %copy-start.2 = (bf16[128,1024]{1,0:T(8,128)(2,1)}, bf16[128,1024]{1,0:T(8,128)(2,1)S(1)}, u32[]{:S(2)}) copy-start(bf16[128,1024]{1,0:T(8,128)(2,1)S(1)} %collective-permute-done.7.refs_3_) | copy-start | bytes 786436
  58.7 0.6 %copy-start.7 = (bf16[128,256]{1,0:T(8,128)(2,1)}, bf16[128,256]{1,0:T(8,128)(2,1)S(1)}, u32[]{:S(2)}) copy-start(bf16[128,256]{1,0:T(8,128)(2,1)S(1)} %collective-permute-done.2.refs_1_) | copy-start | bytes 196612
  59.4 0.6 %copy-start.8 = (bf16[128,256]{1,0:T(8,128)(2,1)}, bf16[128,256]{1,0:T(8,128)(2,1)S(1)}, u32[]{:S(2)}) copy-start(bf16[128,256]{1,0:T(8,128)(2,1)S(1)} %collective-permute-done.4.refs_3_) | copy-start | bytes 196612

commit v2 on v1

v2 whole, which is shorter than its diff:
```python
import functools

import jax
import jax.numpy as jnp
from jax import lax
from jax.experimental import pallas as pl
from jax.experimental.pallas import tpu as pltpu
from jax.sharding import PartitionSpec as P

SUB = 32
BEAMS = 8
TAPS = 8
TILE_DEV = 4
FOOT = 32
AZ = 64
LANES = 128
ROWS = 264
GROUP = 128
NEAR = 5


def fetch_sub(x_hbm, xbuf, sems, sub):
    window = pl.ds(pl.multiple_of(sub * SUB, SUB), SUB)
    return pltpu.make_async_copy(x_hbm.at[window], xbuf.at[window], sems.at[sub])


def align_all(rows, subs, shift_ref, x_hbm, xbuf, aligned, sems):
    lane = lax.broadcasted_iota(jnp.int32, (rows, LANES), 1)

    def align(sub, carry):
        fetch_sub(x_hbm, xbuf, sems, sub).wait()
        for inner in range(SUB):
            pulse = sub * SUB + inner
            raised = shift_ref[pulse] + (LANES - 3)
            rest = raised & (LANES - 1)
            here = xbuf[pulse].astype(jnp.float32)
            after = pltpu.roll(here, rows - 2, 0)
            mixed = jnp.where(lane >= rest, here, after)
            turned = pltpu.roll(mixed, (LANES - rest) & (LANES - 1), 1)
            first = pulse + 2 * ROWS * (1 - (raised >> 7))
            aligned[pl.ds(first, rows, stride=ROWS), :] = turned
        return carry

    lax.fori_loop(0, subs, align, 0)


def turn_by(a, b):
    return a[0] * b[0] - a[1] * b[1], a[0] * b[1] + a[1] * b[0]


def read_demod(aligned, slot, group, phase):
    at = 2 * slot * ROWS + group * GROUP
    real = aligned[pl.ds(at, GROUP), :]
    imag = aligned[pl.ds(at + ROWS, GROUP), :]
    real, imag = turn_by((real, imag), phase)
    return jnp.concatenate([real, imag], axis=0).astype(jnp.bfloat16)


def multiply(weights, demod, products, width):
    for start in range(0, width, 256):
        here = pl.ds(start, min(256, width - start))
        products[:, here] = jnp.dot(weights[...], demod[:, here], preferred_element_type=jnp.float32)


def combine(products, out_ref, group, runs):
    lane = lax.broadcasted_iota(jnp.int32, (8, LANES), 1)
    for row in range(0, 64, 8):
        for first, blocks, column in runs:
            later = None
            for block in range(blocks, -1, -1):
                turned = []
                for tap in range(TAPS):
                    piece = products[pl.ds(tap * 64 + row, 8), pl.ds((first + block) * LANES, LANES)]
                    turned.append(pltpu.roll(piece, LANES - tap, 1) if tap else piece)
                if later is not None:
                    total = turned[0]
                    for tap in range(1, TAPS):
                        total = total + jnp.where(lane < LANES - tap, turned[tap], later[tap])
                    here = pl.ds(column + block * LANES, LANES)
                    out_ref[pl.ds(group * 64 + row, 8), here] = total.astype(jnp.bfloat16)
                later = turned


def front_kernel(near, far, start_ref, shift_ref, x_hbm, tap_ref, angle_ref, slope_ref, steer_ref, out_ref, far_ref, weight_ref, phase_ref, xbuf, aligned, demod, products, sems):
    pulses = shift_ref.shape[0]
    subs = pulses // SUB
    for sub in range(subs):
        fetch_sub(x_hbm, xbuf, sems, sub).start()

    slope = slope_ref[...]
    row = lax.broadcasted_iota(jnp.int32, (8, pulses), 0)
    cell = (start_ref[0] - row).astype(jnp.float32)
    factor_arg = angle_ref[...] + slope * cell
    factor_re = tap_ref[...] * jnp.cos(factor_arg)
    factor_im = tap_ref[...] * jnp.sin(factor_arg)
    low = slope * row.astype(jnp.float32)
    rows = [(jnp.cos(low), jnp.sin(low))]
    power = slope * jnp.left_shift(8, row).astype(jnp.float32)
    power_cos, power_sin = jnp.cos(power), jnp.sin(power)
    for bit in range(4):
        by = power_cos[bit : bit + 1], power_sin[bit : bit + 1]
        rows = rows + [turn_by(item, by) for item in rows]
    base_cos = jnp.concatenate([item[0] for item in rows], axis=0).T
    base_sin = jnp.concatenate([item[1] for item in rows], axis=0).T

    lane8 = lax.broadcasted_iota(jnp.int32, (8, LANES), 1)
    steer_re = jnp.concatenate([steer_ref[0].astype(jnp.float32)] * (GROUP // SUB), axis=1)
    steer_im = jnp.concatenate([steer_ref[1].astype(jnp.float32)] * (GROUP // SUB), axis=1)
    groups = pulses // GROUP
    for group in range(groups):
        here = slice(group * GROUP, (group + 1) * GROUP)
        for tap in range(TAPS):
            factor = factor_re[tap : tap + 1, here], factor_im[tap : tap + 1, here]
            w_re, w_im = turn_by((steer_re, steer_im), factor)
            for sub in range(GROUP // SUB):
                keep = (lane8 >= sub * SUB) & (lane8 < (sub + 1) * SUB)
                p_re = jnp.where(keep, w_re, 0.0)
                p_im = jnp.where(keep, w_im, 0.0)
                top = jnp.concatenate([p_re, 0.0 - p_im], axis=1)
                bottom = jnp.concatenate([p_im, p_re], axis=1)
                weight_ref[group, pl.ds(tap * 64 + sub * 16, 16), :] = jnp.concatenate(
                    [top, bottom], axis=0
                ).astype(jnp.bfloat16)

    align_all(xbuf.shape[1], subs, shift_ref, x_hbm, xbuf, aligned, sems)

    for group in range(groups):
        here = slice(group * GROUP, (group + 1) * GROUP)
        phase = base_cos[here], base_sin[here]
        step = turn_by((phase[0][:, 127:128], phase[1][:, 127:128]), (phase[0][:, 1:2], phase[1][:, 1:2]))
        step = jnp.broadcast_to(step[0], (GROUP, LANES)), jnp.broadcast_to(step[1], (GROUP, LANES))
        last = near + far + 1
        for block in range(last + 2):
            if block in (0, 1, last, last + 1):
                spot = (0, 1, last, last + 1).index(block)
                phase_ref[spot, 0, here, :] = phase[0]
                phase_ref[spot, 1, here, :] = phase[1]
            if 1 <= block <= last:
                data = read_demod(aligned, block, group, phase)
                if block <= near + 1:
                    demod[group, :, pl.ds((block - 1) * LANES, LANES)] = data
                if block >= near + 1:
                    far_ref[group, :, pl.ds((block - near - 1) * LANES, LANES)] = data
            phase = turn_by(phase, step)
        multiply(weight_ref.at[group], demod.at[group], products.at[group], (near + 1) * LANES)
    for group in range(groups):
        combine(products.at[group], out_ref, group, ((0, near, 0),))


def middle_kernel(far, demod_ref, weight_ref, out_ref, products):
    groups = weight_ref.shape[0]
    for group in range(groups):
        multiply(weight_ref.at[group], demod_ref.at[group], products.at[group], (far + 1) * LANES)
    for group in range(groups):
        combine(products.at[group], out_ref, group, ((0, far, 0),))


def edge_kernel(shift_ref, x_hbm, weight_ref, phase_ref, out_ref, xbuf, aligned, demod, products, sems):
    pulses = shift_ref.shape[0]
    subs = pulses // SUB
    for sub in range(subs):
        fetch_sub(x_hbm, xbuf, sems, sub).start()
    align_all(xbuf.shape[1], subs, shift_ref, x_hbm, xbuf, aligned, sems)
    groups = pulses // GROUP
    for group in range(groups):
        here = pl.ds(group * GROUP, GROUP)
        for spot, slot in enumerate((1, 2, 6, 7)):
            phase = phase_ref[spot, 0, here, :], phase_ref[spot, 1, here, :]
            demod[group, :, pl.ds(spot * LANES, LANES)] = read_demod(aligned, slot, group, phase)
        multiply(weight_ref.at[group], demod.at[group], products.at[group], 4 * LANES)
    for group in range(groups):
        combine(products.at[group], out_ref, group, ((0, 1, 0), (2, 1, LANES)))


def beam_scratch(pulses, rows, blocks):
    groups = pulses // GROUP
    return [
        pltpu.VMEM((pulses, rows, LANES), jnp.bfloat16),
        pltpu.VMEM(((rows + 2) * ROWS, LANES), jnp.float32),
        pltpu.VMEM((groups, 2 * GROUP, blocks * LANES), jnp.bfloat16),
        pltpu.VMEM((groups, 64 * TAPS, blocks * LANES), jnp.float32),
        pltpu.SemaphoreType.DMA((pulses // SUB,)),
    ]


SMEM = pl.BlockSpec(memory_space=pltpu.SMEM)
VMEM = pl.BlockSpec(memory_space=pltpu.VMEM)
ANY = pl.BlockSpec(memory_space=pl.ANY)


def make_beams(x3, start, shifts, tap_rows, angles, slopes, steering, near):
    pulses, rows, _ = x3.shape
    far = rows // 2 - 2 - near
    groups = pulses // GROUP
    out = jax.ShapeDtypeStruct
    first, rest, weights, phases = pl.pallas_call(
        functools.partial(front_kernel, near, far),
        name="front",
        out_shape=(
            out((pulses // 2, near * LANES), jnp.bfloat16),
            out((groups, 2 * GROUP, (far + 1) * LANES), jnp.bfloat16),
            out((groups, 64 * TAPS, 2 * GROUP), jnp.bfloat16),
            out((4, 2, pulses, LANES), jnp.float32),
        ),
        in_specs=[SMEM, SMEM, ANY, VMEM, VMEM, VMEM, VMEM],
        out_specs=(VMEM, VMEM, VMEM, VMEM),
        scratch_shapes=beam_scratch(pulses, rows, near + 1),
        cost_estimate=pl.CostEstimate(flops=3000000000, bytes_accessed=8000000, transcendentals=0),
    )(start, shifts, x3, tap_rows, angles, slopes, steering)
    second = pl.pallas_call(
        functools.partial(middle_kernel, far),
        name="middle",
        out_shape=out((pulses // 2, far * LANES), jnp.bfloat16),
        in_specs=[VMEM, VMEM],
        out_specs=VMEM,
        scratch_shapes=[pltpu.VMEM((groups, 64 * TAPS, (far + 1) * LANES), jnp.float32)],
        cost_estimate=pl.CostEstimate(flops=2000000000, bytes_accessed=4000000, transcendentals=0),
    )(rest, weights)
    return first, second, weights, phases


def make_edges(edge, shifts, weights, phases):
    pulses, rows, _ = edge.shape
    return pl.pallas_call(
        edge_kernel,
        name="edges",
        out_shape=jax.ShapeDtypeStruct((pulses // 2, 2 * LANES), jnp.bfloat16),
        in_specs=[SMEM, ANY, VMEM, VMEM],
        out_specs=VMEM,
        scratch_shapes=beam_scratch(pulses, rows, 4),
        cost_estimate=pl.CostEstimate(flops=2000000000, bytes_accessed=4000000, transcendentals=0),
    )(shifts, edge, weights, phases)


def expand_kernel(where_ref, coeff_ref, out_ref):
    width = out_ref.shape[1]
    lane = lax.broadcasted_iota(jnp.int32, (FOOT, width), 1)
    dims = (((0,), (0,)), ((), ()))
    for tile in range(TILE_DEV):
        spot = where_ref[pl.ds(tile * FOOT, FOOT), :]
        hot_re = (lane == spot).astype(jnp.float32).astype(jnp.bfloat16)
        hot_im = (lane == spot + BEAMS).astype(jnp.float32).astype(jnp.bfloat16)
        c_re, c_im = coeff_ref[tile, 0], coeff_ref[tile, 1]
        dot = functools.partial(lax.dot_general, dimension_numbers=dims, preferred_element_type=jnp.float32)
        at = tile * 2 * AZ
        out_ref[pl.ds(at, AZ), :] = (dot(c_re, hot_re) - dot(c_im, hot_im)).astype(jnp.bfloat16)
        out_ref[pl.ds(at + AZ, AZ), :] = (dot(c_im, hot_re) + dot(c_re, hot_im)).astype(jnp.bfloat16)


def project_kernel(count, pieces, coeff_ref, *refs):
    sources = refs[:count]
    out_hbm, held, tile, in_sems, sems = refs[-5:]
    depth = sources[0].shape[0]
    loads = [
        pltpu.make_async_copy(ref, held.at[pl.ds(index * depth, depth)], in_sems.at[index])
        for index, ref in enumerate(sources)
    ]
    for load in loads:
        load.start()
    for load in loads:
        load.wait()
    copies = []
    for source, target, width in pieces:
        for start in range(0, width, 256):
            size = min(256, width - start)
            here = pl.ds(source + start, size)
            total = None
            for first in range(0, count, 2):
                window = pl.ds(first * depth, 2 * depth)
                term = jnp.dot(coeff_ref[:, window], held[window, here], preferred_element_type=jnp.float32)
                total = term if total is None else total + term
            tile[:, here] = total.astype(jnp.bfloat16)
            copy = pltpu.make_async_copy(
                tile.at[:, here], out_hbm.at[:, pl.ds(target + start, size)], sems.at[len(copies)]
            )
            copy.start()
            copies.append(copy)
    for copy in copies:
        copy.wait()


def project(coeffs, sources, image, pieces, cells, name):
    count = len(sources)
    depth, width = sources[0].shape
    rows = coeffs.shape[0]
    extra = [] if image is None else [image]
    return pl.pallas_call(
        functools.partial(project_kernel, count, pieces),
        name=name,
        out_shape=jax.ShapeDtypeStruct((rows, cells), jnp.bfloat16),
        in_specs=[VMEM] + [ANY] * (count + len(extra)),
        out_specs=ANY,
        input_output_aliases={1 + count: 0} if extra else {},
        scratch_shapes=[
            pltpu.VMEM((count * depth, width), jnp.bfloat16),
            pltpu.VMEM((rows, width), jnp.bfloat16),
            pltpu.SemaphoreType.DMA((count,)),
            pltpu.SemaphoreType.DMA((sum(-(-piece[2] // 256) for piece in pieces),)),
        ],
        cost_estimate=pl.CostEstimate(
            flops=2 * rows * width * count * depth, bytes_accessed=3000000, transcendentals=0
        ),
    )(coeffs, *sources, *extra)


def body(echoes, shifts, tap_weights, angles, slopes, steering, footprint, tile_coeffs):
    pulses, _, cells = echoes.shape
    blocks = cells // LANES
    pulse_count = lax.axis_size("pulse")
    range_count = lax.axis_size("range")
    me = lax.axis_index("pulse")
    start_cell = lax.axis_index("range") * cells

    x4 = echoes.reshape(pulses, 2, blocks, LANES).transpose(0, 2, 1, 3)
    ends = range_count - 1
    left = lax.ppermute(x4[:, blocks - 1 :], "range", [(i, i + 1) for i in range(ends)])
    right = lax.ppermute(x4[:, :1], "range", [(i + 1, i) for i in range(ends)])

    x3 = x4.reshape(pulses, 2 * blocks, LANES)
    near = NEAR
    first, second, weights, phases = make_beams(
        x3,
        jnp.reshape(start_cell, (1,)),
        shifts,
        tap_weights.T,
        angles[None, :],
        slopes[None, :],
        steering,
        near,
    )
    edge = jnp.concatenate([left, x4[:, :3], x4[:, blocks - 3 :], right], axis=1)
    beams = [first, second, make_edges(edge.reshape(pulses, 16, LANES), shifts, weights, phases)]
    pieces = [
        ((0, LANES, near * LANES),),
        ((0, (near + 1) * LANES, (blocks - 2 - near) * LANES),),
        ((0, 0, LANES), (LANES, (blocks - 1) * LANES, LANES)),
    ]

    entries = TILE_DEV * FOOT
    chips = pulse_count // 2
    beam_dev = pulses // SUB * BEAMS
    ids = lax.dynamic_index_in_dim(footprint.reshape(pulse_count, entries), me, 0, keepdims=False)
    owner = ids // beam_dev
    inside = ids % beam_dev
    place = 2 * ((me // 2 - owner // 2) % chips) + (me % 2 + owner % 2) % 2
    where = place * (2 * beam_dev) + (inside // BEAMS) * (2 * BEAMS) + inside % BEAMS
    coeffs = pl.pallas_call(
        expand_kernel,
        name="expand",
        out_shape=jax.ShapeDtypeStruct((TILE_DEV * 2 * AZ, pulse_count * 2 * beam_dev), jnp.bfloat16),
    )(where[:, None], tile_coeffs.transpose(0, 1, 3, 2))

    swap = [(i, i ^ 1) for i in range(pulse_count)]
    image = None
    for index, own in enumerate(beams):
        sources = []
        for hop in range(chips):
            ahead = own
            if hop:
                ahead = lax.ppermute(own, "pulse", [(i, (i + 2 * hop) % pulse_count) for i in range(pulse_count)])
            sources += [ahead, lax.ppermute(ahead, "pulse", swap)]
        image = project(coeffs, sources, image, pieces[index], cells, "project_" + "abc"[index])
    return image.reshape(TILE_DEV, 2, AZ, cells)


def solution(mesh):
    placed = (
        P(("groups", "pulse"), None, "range"),
        P(("groups", "pulse")),
        P(("groups", "pulse"), None),
        P(("groups", "pulse")),
        P(("groups", "pulse")),
        P(),
        P("groups", None),
        P(("groups", "pulse"), None, None, None),
    )
    return jax.shard_map(
        body,
        mesh=mesh,
        in_specs=placed,
        out_specs=P(("groups", "pulse"), None, None, "range"),
        check_vma=False,
    )
```

time: 62.9 us -> 52 us (0.83)
  Pallas kernels: 35.3 us -> 28.1 us
  waiting for transfers between devices: 0.03 us -> 6.04 us
  other arithmetic: 7.57 us -> 3.32 us
  local copies, waits for them, and re-layouts: 8.08 us -> 4.27 us
  starting transfers between devices: 11.1 us -> 9.54 us
    pallas_call x3, Pallas kernels: 25.1 us -> 15.2 us  [the longest x1 6.33 us: make_beams(): pl.pallas_call(functools.partial(front_kernel, near, far), name='front',...]
    ppermute x3, waiting for transfers between devices: 0.01 us -> 4.87 us  [body(): lax.ppermute(own, 'pulse', [(i, (i + 2 * hop) % pulse_count) for i in ran...]
    pallas_call x3, Pallas kernels: 8.11 us -> 10.7 us  [project(): pl.pallas_call(functools.partial(project_kernel, count, pieces), name=nam...]
    another operation x2 -> x0, local copies, waits for them, and re-layouts: 1.37 us -> none  [body(): steer = jnp.tile(steering.astype(jnp.float32), (1, 1, GROUP // SUB))]
    another operation x2 -> x0, other arithmetic: 1.35 us -> none  [the longest x1 0.73 us: body(): table = jnp.stack([jnp.cos(turn), jnp.sin(turn)])]
    cos x1 -> x0, other arithmetic: 1.21 us -> none  [body(): table = jnp.stack([jnp.cos(turn), jnp.sin(turn)])]
    ppermute x1, waiting for transfers between devices: 0.01 us -> 1.15 us  [body(): right = lax.ppermute(x4[:, :1], 'range', [(i + 1, i) for i in range(ends)])]
    slice x1, local copies, waits for them, and re-layouts: 1.66 us -> 0.54 us  [body(): edge = jnp.concatenate([left, x4[:, :3], x4[:, blocks - 3:], right], axis=1)]
  transfers between devices with their start and end apart: 11 -> 11, of which waited for: 0 -> 3; matrix products, arithmetic and copies ran while one was open for 10% -> 8% of each run, Pallas kernels for 40% -> 36%
where the time goes in v2:
time: 52 us; the launch traced here: 51.5 us
  Pallas kernels  28.1 us (54%)
  starting transfers between devices  9.54 us (18%)
  waiting for transfers between devices  6.04 us (12%)
  local copies, waits for them, and re-layouts  4.27 us (8%)
  other arithmetic  3.32 us (6%)
    pallas_call x3, Pallas kernels, project(): pl.pallas_call(functools.partial(project_kernel, count, pieces), name=nam...  10.7 us
    pallas_call x1, Pallas kernels, make_beams(): pl.pallas_call(functools.partial(front_kernel, near, far), name='front',...  6.33 us
    pallas_call x1, Pallas kernels, make_edges(): pl.pallas_call(edge_kernel, name='edges', out_shape=jax.ShapeDtypeStruct(...  5.24 us
    ppermute x3, waiting for transfers between devices, body(): lax.ppermute(own, 'pulse', [(i, (i + 2 * hop) % pulse_count) for i in ran...  4.87 us
    ppermute x3, starting transfers between devices, body(): lax.ppermute(own, 'pulse', [(i, (i + 2 * hop) % pulse_count) for i in ran...  4.17 us
    pallas_call x1, Pallas kernels, make_beams(): pl.pallas_call(functools.partial(middle_kernel, far), name='middle', out_...  3.66 us
    ppermute x1, starting transfers between devices, body(): lax.ppermute(x4[:, blocks - 1:], 'range', [(i, i + 1) for i in range(ends)])  3.48 us
    unnamed x22, local copies, waits for them, and re-layouts  3.35 us
  transfers between devices with their start and end apart: 11, of which 3 were waited for; matrix products, arithmetic and copies ran while one was open for 8% of the time, Pallas kernels for 36%

profile of v2, /device:TPU:0, one launch (start us, length us, event | category | flops | bytes accessed | tf_op | source)
XLA Modules:
  0.0 51.5 jit_solution(11168062482425735777)
XLA Ops:
  0.0 0.0 copy-start
  0.0 6.3 %front.1 = (bf16[128,640]{1,0:T(8,128)(2,1)}, bf16[2,256,1280]{2,1,0:T(8,128)(2,1)}, bf16[2,512,256]{2,1,0:T(8,128)(2,1)}, f32[4,2,256,128]{3,2,1,0:T(8,128)}) custom-call(s32[1]{0:T(128)} %bitcast.6.start_ref, s32[256]{0:T(256)} %shift_ref.3, bf16[256,32,128]{2,1,0:T(8,128)(2,1)} %bitcast.15, f32[8,256]{1,0:T(8,128)} %bitcast.19, f32[1,256]{1,0:T(1,128)} %bitcast.20, ...), custom_call_target="tpu_custom_call" | custom-call | flops 3000000000 | bytes 8000000 | tf_op jit(solution)/shard_map/front/pallas_call | solution.py:196
  6.3 3.0 %collective-permute-start.9 = (bf16[128,640]{1,0:T(8,128)(2,1)}, bf16[128,640]{1,0:T(8,128)(2,1)S(1)}, u32[]{:S(2)}, u32[]{:S(2)}) collective-permute-start(bf16[128,640]{1,0:T(8,128)(2,1)} %get-tuple-element.12.refs_0_), channel_id=1, source_target_pairs={{0,8},{4,12},{8,0},{12,4},{1,9},{5,13},{9,1},{13,5},{2,10},{6,14},... | collective-permute-start | bytes 491528 | tf_op jit(solution)/shard_map/ppermute | solution.py:360
  9.4 0.0 collective-permute-start.8
  9.4 0.0 copy-done
  9.4 0.2 fusion.16
  9.6 3.5 %collective-permute-start = (bf16[256,1,2,128]{3,2,1,0:T(2,128)(2,1)S(1)}, bf16[256,1,2,128]{3,2,1,0:T(2,128)(2,1)S(1)}, u32[]{:S(2)}, u32[]{:S(2)}) collective-permute-start(bf16[256,1,2,128]{3,2,1,0:T(2,128)(2,1)S(1)} %get-tuple-element.13), channel_id=1, source_target_pairs={{0,1},{1,2},{2,3},{4,5},{5,6},{6,7},{8,9},{9,10},{10,11},{12,13},{... | collective-permute-start | bytes 393224 | tf_op jit(solution)/shard_map/ppermute | solution.py:316
  13.1 1.3 %collective-permute-start.1 = (bf16[256,1,2,128]{3,2,1,0:T(2,128)(2,1)S(1)}, bf16[256,1,2,128]{3,2,1,0:T(2,128)(2,1)S(1)}, u32[]{:S(2)}, u32[]{:S(2)}) collective-permute-start(bf16[256,1,2,128]{3,2,1,0:T(2,128)(2,1)S(1)} %get-tuple-element.14), channel_id=1, source_target_pairs={{1,0},{2,1},{3,2},{5,4},{6,5},{7,6},{9,8},{10,9},{11,10},{13,12},{... | collective-permute-start | bytes 393224 | tf_op jit(solution)/shard_map/ppermute | solution.py:317
  14.4 0.0 copy-start.10
  14.4 3.7 %middle.1.refs_0_ = bf16[128,1152]{1,0:T(8,128)(2,1)} custom-call(bf16[2,256,1280]{2,1,0:T(8,128)(2,1)} %get-tuple-element.11.demod_ref, bf16[2,512,256]{2,1,0:T(8,128)(2,1)} %get-tuple-element.9.weight_ref), custom_call_target="tpu_custom_call" | custom-call | flops 2000000000 | bytes 4000000 | tf_op jit(solution)/shard_map/middle/pallas_call | solution.py:210
  18.0 0.5 %collective-permute-start.6 = (bf16[128,1152]{1,0:T(8,128)(2,1)}, bf16[128,1152]{1,0:T(8,128)(2,1)S(1)}, u32[]{:S(2)}, u32[]{:S(2)}) collective-permute-start(bf16[128,1152]{1,0:T(8,128)(2,1)} %middle.1.refs_0_), channel_id=1, source_target_pairs={{0,8},{4,12},{8,0},{12,4},{1,9},{5,13},{9,1},{13,5},{2,10},{6,14},... | collective-permute-start | bytes 884744 | tf_op jit(solution)/shard_map/ppermute | solution.py:360
  18.6 0.0 copy-done.10
  18.6 0.1 reshape.331
  18.7 0.1 copy.11
  18.8 0.5 %fusion.17 = (bf16[256,3,2,128]{3,2,1,0:T(2,128)(2,1)S(1)}, bf16[256,3,2,128]{3,2,1,0:T(2,128)(2,1)S(1)}) fusion(bf16[256,16,2,128]{3,2,1,0:T(2,128)(2,1)S(1)} %bitcast.17), kind=kLoop, calls=%fused_computation.43 | loop fusion | bytes 1572864 | tf_op jit(solution)/shard_map/slice | solution.py:331
  19.3 0.0 collective-permute-done
  19.4 0.1 collective-permute-start.5
  19.4 1.2 %collective-permute-done.1 = bf16[256,1,2,128]{3,2,1,0:T(2,128)(2,1)S(1)} collective-permute-done((bf16[256,1,2,128]{3,2,1,0:T(2,128)(2,1)S(1)}, bf16[256,1,2,128]{3,2,1,0:T(2,128)(2,1)S(1)}, u32[]{:S(2)}, u32[]{:S(2)}) %collective-permute-start.1) | collective-permute-done | bytes 131104 | tf_op jit(solution)/shard_map/ppermute | solution.py:317
  20.6 2.5 %pad_maximum_fusion = bf16[256,8,2,128]{3,2,1,0:T(2,128)(2,1)} fusion(bf16[256,1,2,128]{3,2,1,0:T(2,128)(2,1)S(1)} %collective-permute-done.1, bf16[256,3,2,128]{3,2,1,0:T(2,128)(2,1)S(1)} %get-tuple-element.16, bf16[256,3,2,128]{3,2,1,0:T(2,128)(2,1)S(1)} %get-tuple-element.15, bf16[256,1,2,128]{3,2,1,0:T(2,128)(2,1)S(1)} %collective-permute-done), kind=kLoop, calls=%fused_computation | loop fusion | flops 1572864 | bytes 2097152 | tf_op jit(solution)/shard_map/concatenate | solution.py:331
  23.0 4.3 %collective-permute-done.6.refs_2_ = bf16[128,1152]{1,0:T(8,128)(2,1)S(1)} collective-permute-done((bf16[128,1152]{1,0:T(8,128)(2,1)}, bf16[128,1152]{1,0:T(8,128)(2,1)S(1)}, u32[]{:S(2)}, u32[]{:S(2)}) %collective-permute-start.6) | collective-permute-done | bytes 294944 | tf_op jit(solution)/shard_map/ppermute | solution.py:360
  27.4 0.0 copy-start.1
  27.4 0.0 collective-permute-start.7
  27.4 5.2 %edges.1.refs_0_ = bf16[128,256]{1,0:T(8,128)(2,1)} custom-call(s32[256]{0:T(256)} %shift_ref.3, bf16[256,16,128]{2,1,0:T(8,128)(2,1)} %bitcast.14, bf16[2,512,256]{2,1,0:T(8,128)(2,1)} %get-tuple-element.9.weight_ref, f32[4,2,256,128]{3,2,1,0:T(8,128)} %get-tuple-element.10.phase_ref), custom_call_target="tpu_custom_call" | custom-call | flops 2000000000 | bytes 4000000 | tf_op jit(solution)/shard_map/edges/pallas_call | solution.py:224
  32.6 0.0 copy-done.1
  32.7 0.6 %collective-permute-start.3 = (bf16[128,256]{1,0:T(8,128)(2,1)}, bf16[128,256]{1,0:T(8,128)(2,1)S(1)}, u32[]{:S(2)}, u32[]{:S(2)}) collective-permute-start(bf16[128,256]{1,0:T(8,128)(2,1)} %edges.1.refs_0_), channel_id=1, source_target_pairs={{0,8},{4,12},{8,0},{12,4},{1,9},{5,13},{9,1},{13,5},{2,10},{6,14},... | collective-permute-start | bytes 196616 | tf_op jit(solution)/shard_map/ppermute | solution.py:360
  33.3 0.0 collective-permute-done.9.refs_2_
  33.3 0.0 copy-start.4
  33.3 0.1 collective-permute-start.10
  33.4 0.9 %fusion.6.where_ref = s32[128,1]{1,0:T(8,128)} fusion(s32[128,1]{1,0:T(8,128)S(1)} %copy.11, s32[]{:T(128)S(6)} %select_n.109, s32[]{:T(128)S(6)} %select_n.104), kind=kLoop, calls=%fused_computation.28 | loop fusion | flops 11136 | bytes 1032 | tf_op jit(solution)/shard_map/add | solution.py:346
  34.3 2.2 %expand.1.coeff_ref = bf16[512,512]{1,0:T(8,128)(2,1)} custom-call(s32[128,1]{1,0:T(8,128)} %fusion.6.where_ref, bf16[4,2,32,64]{3,2,1,0:T(8,128)(2,1)} %bitcast.18), custom_call_target="tpu_custom_call" | custom-call | tf_op jit(solution)/shard_map/expand/pallas_call | solution.py:347
  36.4 0.0 collective-permute-done.8.refs_1_
  36.4 0.0 copy-start.5
  36.4 0.4 collective-permute-start.2
  36.8 0.5 %collective-permute-done.3.refs_2_ = bf16[128,256]{1,0:T(8,128)(2,1)S(1)} collective-permute-done((bf16[128,256]{1,0:T(8,128)(2,1)}, bf16[128,256]{1,0:T(8,128)(2,1)S(1)}, u32[]{:S(2)}, u32[]{:S(2)}) %collective-permute-start.3) | collective-permute-done | bytes 65568 | tf_op jit(solution)/shard_map/ppermute | solution.py:360
  37.3 0.0 copy-start.7
  37.3 0.0 collective-permute-start.4
  37.3 0.0 collective-permute-done.10.refs_3_
  37.3 0.0 copy-done.4
  37.4 0.0 copy-done.5
  37.4 0.0 copy-start.6
  37.4 0.7 %copy-done.6 = bf16[128,640]{1,0:T(8,128)(2,1)} copy-done((bf16[128,640]{1,0:T(8,128)(2,1)}, bf16[128,640]{1,0:T(8,128)(2,1)S(1)}, u32[]{:S(2)}) %copy-start.6) | copy-done | bytes 163864
  38.0 3.6 %project_a.1.refs_4_ = bf16[512,2048]{1,0:T(8,128)(2,1)} custom-call(bf16[512,512]{1,0:T(8,128)(2,1)} %expand.1.coeff_ref, bf16[128,640]{1,0:T(8,128)(2,1)} %get-tuple-element.12.refs_0_, bf16[128,640]{1,0:T(8,128)(2,1)} %copy-done.5, bf16[128,640]{1,0:T(8,128)(2,1)} %copy-done.4, bf16[128,640]{1,0:T(8,128)(2,1)} %copy-done.6), custom_call_target="tpu_custom_call" | custom-call | flops 335544320 | bytes 3000000 | tf_op jit(solution)/shard_map/project_a/pallas_call | solution.py:287
  41.6 0.0 collective-permute-done.5.refs_1_
  41.6 0.0 copy-start.2
  41.6 0.0 collective-permute-done.7.refs_3_
  41.6 0.7 %copy-done.2 = bf16[128,1152]{1,0:T(8,128)(2,1)} copy-done((bf16[128,1152]{1,0:T(8,128)(2,1)}, bf16[128,1152]{1,0:T(8,128)(2,1)S(1)}, u32[]{:S(2)}) %copy-start.2) | copy-done | bytes 294936
  42.3 0.0 copy-start.3
  42.3 0.7 %copy-done.3 = bf16[128,1152]{1,0:T(8,128)(2,1)} copy-done((bf16[128,1152]{1,0:T(8,128)(2,1)}, bf16[128,1152]{1,0:T(8,128)(2,1)S(1)}, u32[]{:S(2)}) %copy-start.3) | copy-done | bytes 294936
  43.1 4.0 %project_b.1.refs_4_ = bf16[512,2048]{1,0:T(8,128)(2,1)} custom-call(bf16[512,512]{1,0:T(8,128)(2,1)} %expand.1.coeff_ref, bf16[128,1152]{1,0:T(8,128)(2,1)} %middle.1.refs_0_, bf16[128,1152]{1,0:T(8,128)(2,1)} %copy-done.2, bf16[128,1152]{1,0:T(8,128)(2,1)} %copy-done.1, bf16[128,1152]{1,0:T(8,128)(2,1)} %copy-done.3, ...), custom_call_target="tpu_custom_call", output_to_operand_aliasing={{}: (5, {})} | custom-call | flops 603979776 | bytes 3000000 | tf_op jit(solution)/shard_map/project_b/pallas_call | solution.py:287
  47.0 0.0 collective-permute-done.2.refs_1_
  47.0 0.0 copy-start.8
  47.0 0.0 collective-permute-done.4.refs_3_
  47.1 0.0 copy-done.7
  47.1 0.6 %copy-done.8 = bf16[128,256]{1,0:T(8,128)(2,1)} copy-done((bf16[128,256]{1,0:T(8,128)(2,1)}, bf16[128,256]{1,0:T(8,128)(2,1)S(1)}, u32[]{:S(2)}) %copy-start.8) | copy-done | bytes 65560
  47.7 0.0 copy-start.9
  47.7 0.6 %copy-done.9 = bf16[128,256]{1,0:T(8,128)(2,1)} copy-done((bf16[128,256]{1,0:T(8,128)(2,1)}, bf16[128,256]{1,0:T(8,128)(2,1)S(1)}, u32[]{:S(2)}) %copy-start.9) | copy-done | bytes 65560
  48.3 3.2 %project_c.1 = bf16[512,2048]{1,0:T(8,128)(2,1)} custom-call(bf16[512,512]{1,0:T(8,128)(2,1)} %expand.1.coeff_ref, bf16[128,256]{1,0:T(8,128)(2,1)} %edges.1.refs_0_, bf16[128,256]{1,0:T(8,128)(2,1)} %copy-done.8, bf16[128,256]{1,0:T(8,128)(2,1)} %copy-done.7, bf16[128,256]{1,0:T(8,128)(2,1)} %copy-done.9, ...), custom_call_target="tpu_custom_call", output_to_operand_aliasing={{}: (5, {})} | custom-call | flops 134217728 | bytes 3000000 | tf_op jit(solution)/shard_map/project_c/pallas_call | solution.py:287
  (1 shorter events, 0.0 us)
Async XLA Ops:
  0.0 9.4 %copy-start = (bf16[256,2,2048]{2,1,0:T(2,128)(2,1)S(1)}, bf16[256,2,2048]{2,1,0:T(2,128)(2,1)}, u32[]{:S(2)}) copy-start(bf16[256,2,2048]{2,1,0:T(2,128)(2,1)} %param.8) | copy-start | bytes 6291460
  6.3 26.9 %collective-permute-start.9 = (bf16[128,640]{1,0:T(8,128)(2,1)}, bf16[128,640]{1,0:T(8,128)(2,1)S(1)}, u32[]{:S(2)}, u32[]{:S(2)}) collective-permute-start(bf16[128,640]{1,0:T(8,128)(2,1)} %get-tuple-element.12.refs_0_), channel_id=1, source_target_pairs={{0,8},{4,12},{8,0},{12,4},{1,9},{5,13},{9,1},{13,5},{2,10},{6,14},... | collective-permute-start | bytes 491528 | tf_op jit(solution)/shard_map/ppermute | solution.py:360
  9.4 27.0 %collective-permute-start.8 = (bf16[128,640]{1,0:T(8,128)(2,1)}, bf16[128,640]{1,0:T(8,128)(2,1)S(1)}, u32[]{:S(2)}, u32[]{:S(2)}) collective-permute-start(bf16[128,640]{1,0:T(8,128)(2,1)} %get-tuple-element.12.refs_0_), channel_id=1, source_target_pairs={{0,4},{4,0},{8,12},{12,8},{1,5},{5,1},{9,13},{13,9},{2,6},{6,2},{1... | collective-permute-start | bytes 491528 | tf_op jit(solution)/shard_map/ppermute | solution.py:361
  9.6 9.8 %collective-permute-start = (bf16[256,1,2,128]{3,2,1,0:T(2,128)(2,1)S(1)}, bf16[256,1,2,128]{3,2,1,0:T(2,128)(2,1)S(1)}, u32[]{:S(2)}, u32[]{:S(2)}) collective-permute-start(bf16[256,1,2,128]{3,2,1,0:T(2,128)(2,1)S(1)} %get-tuple-element.13), channel_id=1, source_target_pairs={{0,1},{1,2},{2,3},{4,5},{5,6},{6,7},{8,9},{9,10},{10,11},{12,13},{... | collective-permute-start | bytes 393224 | tf_op jit(solution)/shard_map/ppermute | solution.py:316
  13.1 7.5 %collective-permute-start.1 = (bf16[256,1,2,128]{3,2,1,0:T(2,128)(2,1)S(1)}, bf16[256,1,2,128]{3,2,1,0:T(2,128)(2,1)S(1)}, u32[]{:S(2)}, u32[]{:S(2)}) collective-permute-start(bf16[256,1,2,128]{3,2,1,0:T(2,128)(2,1)S(1)} %get-tuple-element.14), channel_id=1, source_target_pairs={{1,0},{2,1},{3,2},{5,4},{6,5},{7,6},{9,8},{10,9},{11,10},{13,12},{... | collective-permute-start | bytes 393224 | tf_op jit(solution)/shard_map/ppermute | solution.py:317
  14.4 4.2 %copy-start.10 = (s32[16,32]{1,0:T(8,128)S(1)}, s32[16,32]{1,0:T(8,128)}, u32[]{:S(2)}) copy-start(s32[16,32]{1,0:T(8,128)} %param.14) | copy-start | bytes 6148
  18.0 9.4 %collective-permute-start.6 = (bf16[128,1152]{1,0:T(8,128)(2,1)}, bf16[128,1152]{1,0:T(8,128)(2,1)S(1)}, u32[]{:S(2)}, u32[]{:S(2)}) collective-permute-start(bf16[128,1152]{1,0:T(8,128)(2,1)} %middle.1.refs_0_), channel_id=1, source_target_pairs={{0,8},{4,12},{8,0},{12,4},{1,9},{5,13},{9,1},{13,5},{2,10},{6,14},... | collective-permute-start | bytes 884744 | tf_op jit(solution)/shard_map/ppermute | solution.py:360
  19.4 22.3 %collective-permute-start.5 = (bf16[128,1152]{1,0:T(8,128)(2,1)}, bf16[128,1152]{1,0:T(8,128)(2,1)S(1)}, u32[]{:S(2)}, u32[]{:S(2)}) collective-permute-start(bf16[128,1152]{1,0:T(8,128)(2,1)} %middle.1.refs_0_), channel_id=1, source_target_pairs={{0,4},{4,0},{8,12},{12,8},{1,5},{5,1},{9,13},{13,9},{2,6},{6,2},{1... | collective-permute-start | bytes 884744 | tf_op jit(solution)/shard_map/ppermute | solution.py:361
  27.4 5.3 %copy-start.1 = (bf16[128,1152]{1,0:T(8,128)(2,1)}, bf16[128,1152]{1,0:T(8,128)(2,1)S(1)}, u32[]{:S(2)}) copy-start(bf16[128,1152]{1,0:T(8,128)(2,1)S(1)} %collective-permute-done.6.refs_2_) | copy-start | bytes 884740
  27.4 14.2 %collective-permute-start.7 = (bf16[128,1152]{1,0:T(8,128)(2,1)S(1)}, bf16[128,1152]{1,0:T(8,128)(2,1)S(1)}, u32[]{:S(2)}, u32[]{:S(2)}) collective-permute-start(bf16[128,1152]{1,0:T(8,128)(2,1)S(1)} %collective-permute-done.6.refs_2_), channel_id=1, source_target_pairs={{0,4},{4,0},{8,12},{12,8},{1,5},{5,1},{9,13},{13,9},{2,6},{6,2},{1... | collective-permute-start | bytes 884744 | tf_op jit(solution)/shard_map/ppermute | solution.py:361
  32.7 4.7 %collective-permute-start.3 = (bf16[128,256]{1,0:T(8,128)(2,1)}, bf16[128,256]{1,0:T(8,128)(2,1)S(1)}, u32[]{:S(2)}, u32[]{:S(2)}) collective-permute-start(bf16[128,256]{1,0:T(8,128)(2,1)} %edges.1.refs_0_), channel_id=1, source_target_pairs={{0,8},{4,12},{8,0},{12,4},{1,9},{5,13},{9,1},{13,5},{2,10},{6,14},... | collective-permute-start | bytes 196616 | tf_op jit(solution)/shard_map/ppermute | solution.py:360
  33.3 4.1 %copy-start.4 = (bf16[128,640]{1,0:T(8,128)(2,1)}, bf16[128,640]{1,0:T(8,128)(2,1)S(1)}, u32[]{:S(2)}) copy-start(bf16[128,640]{1,0:T(8,128)(2,1)S(1)} %collective-permute-done.9.refs_2_) | copy-start | bytes 491524
  33.3 4.1 %collective-permute-start.10 = (bf16[128,640]{1,0:T(8,128)(2,1)S(1)}, bf16[128,640]{1,0:T(8,128)(2,1)S(1)}, u32[]{:S(2)}, u32[]{:S(2)}) collective-permute-start(bf16[128,640]{1,0:T(8,128)(2,1)S(1)} %collective-permute-done.9.refs_2_), channel_id=1, source_target_pairs={{0,4},{4,0},{8,12},{12,8},{1,5},{5,1},{9,13},{13,9},{2,6},{6,2},{1... | collective-permute-start | bytes 491528 | tf_op jit(solution)/shard_map/ppermute | solution.py:361
  36.4 0.9 %copy-start.5 = (bf16[128,640]{1,0:T(8,128)(2,1)}, bf16[128,640]{1,0:T(8,128)(2,1)S(1)}, u32[]{:S(2)}) copy-start(bf16[128,640]{1,0:T(8,128)(2,1)S(1)} %collective-permute-done.8.refs_1_) | copy-start | bytes 491524
  36.4 10.6 %collective-permute-start.2 = (bf16[128,256]{1,0:T(8,128)(2,1)}, bf16[128,256]{1,0:T(8,128)(2,1)S(1)}, u32[]{:S(2)}, u32[]{:S(2)}) collective-permute-start(bf16[128,256]{1,0:T(8,128)(2,1)} %edges.1.refs_0_), channel_id=1, source_target_pairs={{0,4},{4,0},{8,12},{12,8},{1,5},{5,1},{9,13},{13,9},{2,6},{6,2},{1... | collective-permute-start | bytes 196616 | tf_op jit(solution)/shard_map/ppermute | solution.py:361
  37.3 9.7 %copy-start.7 = (bf16[128,256]{1,0:T(8,128)(2,1)}, bf16[128,256]{1,0:T(8,128)(2,1)S(1)}, u32[]{:S(2)}) copy-start(bf16[128,256]{1,0:T(8,128)(2,1)S(1)} %collective-permute-done.3.refs_2_) | copy-start | bytes 196612
  37.3 9.7 %collective-permute-start.4 = (bf16[128,256]{1,0:T(8,128)(2,1)S(1)}, bf16[128,256]{1,0:T(8,128)(2,1)S(1)}, u32[]{:S(2)}, u32[]{:S(2)}) collective-permute-start(bf16[128,256]{1,0:T(8,128)(2,1)S(1)} %collective-permute-done.3.refs_2_), channel_id=1, source_target_pairs={{0,4},{4,0},{8,12},{12,8},{1,5},{5,1},{9,13},{13,9},{2,6},{6,2},{1... | collective-permute-start | bytes 196616 | tf_op jit(solution)/shard_map/ppermute | solution.py:361
  37.4 0.7 %copy-start.6 = (bf16[128,640]{1,0:T(8,128)(2,1)}, bf16[128,640]{1,0:T(8,128)(2,1)S(1)}, u32[]{:S(2)}) copy-start(bf16[128,640]{1,0:T(8,128)(2,1)S(1)} %collective-permute-done.10.refs_3_) | copy-start | bytes 491524
  41.6 0.7 %copy-start.2 = (bf16[128,1152]{1,0:T(8,128)(2,1)}, bf16[128,1152]{1,0:T(8,128)(2,1)S(1)}, u32[]{:S(2)}) copy-start(bf16[128,1152]{1,0:T(8,128)(2,1)S(1)} %collective-permute-done.5.refs_1_) | copy-start | bytes 884740
  42.3 0.7 %copy-start.3 = (bf16[128,1152]{1,0:T(8,128)(2,1)}, bf16[128,1152]{1,0:T(8,128)(2,1)S(1)}, u32[]{:S(2)}) copy-start(bf16[128,1152]{1,0:T(8,128)(2,1)S(1)} %collective-permute-done.7.refs_3_) | copy-start | bytes 884740
  47.0 0.6 %copy-start.8 = (bf16[128,256]{1,0:T(8,128)(2,1)}, bf16[128,256]{1,0:T(8,128)(2,1)S(1)}, u32[]{:S(2)}) copy-start(bf16[128,256]{1,0:T(8,128)(2,1)S(1)} %collective-permute-done.2.refs_1_) | copy-start | bytes 196612
  47.7 0.6 %copy-start.9 = (bf16[128,256]{1,0:T(8,128)(2,1)}, bf16[128,256]{1,0:T(8,128)(2,1)S(1)}, u32[]{:S(2)}) copy-start(bf16[128,256]{1,0:T(8,128)(2,1)S(1)} %collective-permute-done.4.refs_3_) | copy-start | bytes 196612

commit v3 on v0

v3 whole, which is shorter than its diff:
```python
import functools

import jax
import jax.numpy as jnp
from jax import lax
from jax.experimental import pallas as pl
from jax.experimental.pallas import tpu as pltpu
from jax.sharding import PartitionSpec as P

SUB = 32
BEAMS = 8
TAPS = 8
TILE_DEV = 4
FOOT = 32
AZ = 64
LANES = 128
STRIDE = 136
GROUP = 128


def turn_by(a, b):
    return a[0] * b[0] - a[1] * b[1], a[0] * b[1] + a[1] * b[0]


def row_of(pair, index):
    return pair[0][index : index + 1], pair[1][index : index + 1]


def angle_pair(value):
    return jnp.cos(value), jnp.sin(value)


def lane_phases(slope):
    row = lax.broadcasted_iota(jnp.int32, (8, GROUP), 0)
    rows = [angle_pair(slope * row.astype(jnp.float32))]
    powers = angle_pair(slope * jnp.left_shift(8, row).astype(jnp.float32))
    for bit in range(4):
        rows = rows + [turn_by(item, row_of(powers, bit)) for item in rows]
    base = tuple(jnp.concatenate([item[part] for item in rows], axis=0).T for part in range(2))
    step = turn_by((base[0][:, 127:128], base[1][:, 127:128]), (base[0][:, 1:2], base[1][:, 1:2]))
    step = tuple(jnp.broadcast_to(part, (GROUP, LANES)) for part in step)
    return base, step


def tap_factors(start_ref, tap_ref, angle, slope, here):
    row = lax.broadcasted_iota(jnp.int32, (8, GROUP), 0)
    cell = (start_ref[0] - LANES - row).astype(jnp.float32)
    cosine, sine = angle_pair(angle + slope * cell)
    taps = tap_ref[:, here]
    return taps * cosine, taps * sine


def fill_weights(factors, steer_ref, weight_ref):
    lane = lax.broadcasted_iota(jnp.int32, (8, LANES), 1)
    steer = tuple(
        jnp.concatenate([steer_ref[part].astype(jnp.float32)] * (GROUP // SUB), axis=1) for part in range(2)
    )
    for tap in range(TAPS):
        w_re, w_im = turn_by(steer, row_of(factors, tap))
        for sub in range(GROUP // SUB):
            keep = (lane >= sub * SUB) & (lane < (sub + 1) * SUB)
            p_re = jnp.where(keep, w_re, 0.0)
            p_im = jnp.where(keep, w_im, 0.0)
            top = jnp.concatenate([p_re, 0.0 - p_im], axis=1)
            bottom = jnp.concatenate([p_im, p_re], axis=1)
            weight_ref[pl.ds(tap * 64 + sub * 16, 16), :] = jnp.concatenate([top, bottom], axis=0).astype(
                jnp.bfloat16
            )


def place_of(shift_ref, pulse, local):
    raised = shift_ref[pulse] + (LANES - 3)
    rest = raised & (LANES - 1)
    return rest, (LANES - rest) & (LANES - 1), local + 2 * STRIDE * (1 - (raised >> 7))


def split_ends(aligned, offset, last):
    lane = lax.broadcasted_iota(jnp.int32, (GROUP, LANES), 1)

    def rows(slot, part):
        return aligned[pl.ds((2 * slot + part) * STRIDE, GROUP), :]

    def first(part):
        return jnp.where(offset >= 0, rows(0, part), jnp.where(lane >= 0 - offset, rows(last + 1, part), 0.0))

    return {
        -1: lambda part: jnp.where(lane >= LANES - offset, rows(last, part), 0.0),
        0: first,
        last: lambda part: jnp.where(lane < LANES - offset, rows(last, part), 0.0),
        last + 1: lambda part: jnp.where(lane < 0 - offset, rows(last + 1, part), 0.0),
    }


def sweep(last, aligned, offset, phase, step, weight_ref, demod, products, carry, store):
    lane = lax.broadcasted_iota(jnp.int32, (8, LANES), 1)
    ends = split_ends(aligned, offset, last)
    for start in range(-1, last + 2, 2):
        for block in (start, start + 1):
            if block in ends:
                data = ends[block](0), ends[block](1)
            else:
                at = 2 * block * STRIDE
                data = aligned[pl.ds(at, GROUP), :], aligned[pl.ds(at + STRIDE, GROUP), :]
            data = turn_by(data, phase)
            phase = turn_by(phase, step)
            here = pl.ds((block + 1) * LANES, LANES)
            demod[:, here] = jnp.concatenate(data, axis=0).astype(jnp.bfloat16)
        here = pl.ds((start + 1) * LANES, 2 * LANES)
        products[:, here] = jnp.dot(weight_ref[...], demod[:, here], preferred_element_type=jnp.float32)
        for row in range(0, 64, 8):
            before = None
            if start >= 0:
                before = [carry[pl.ds(tap * 64 + row, 8), :] for tap in range(TAPS)]
            for block in (start, start + 1):
                turned = []
                for tap in range(TAPS):
                    piece = products[pl.ds(tap * 64 + row, 8), pl.ds((block + 1) * LANES, LANES)]
                    turned.append(pltpu.roll(piece, LANES - tap, 1) if tap else piece)
                if before is not None:
                    total = before[0]
                    for tap in range(1, TAPS):
                        total = total + jnp.where(lane < LANES - tap, before[tap], turned[tap])
                    store(row, block - 1, total)
                before = turned
            if start + 2 < last + 2:
                for tap in range(TAPS):
                    carry[pl.ds(tap * 64 + row, 8), :] = before[tap]
            else:
                total = before[0]
                for tap in range(1, TAPS):
                    total = total + jnp.where(lane < LANES - tap, before[tap], 0.0)
                store(row, last + 1, total)


def fetch_small(sources, targets, sems):
    copies = [pltpu.make_async_copy(s, t, sems.at[i]) for i, (s, t) in enumerate(zip(sources, targets))]
    for copy in copies:
        copy.start()
    return copies


def inner_kernel(group, start_ref, x_hbm, shift_hbm, row_hbm, tap_hbm, angle_hbm, slope_hbm, steer_hbm, *refs):
    if group:
        given_ref, out_ref, below_ref, above_ref, own_ref = refs[:5]
        refs = refs[5:]
    else:
        out_ref, partial_ref = refs[:2]
        refs = refs[2:]
    shift_ref, row_ref, tap_ref, angle_ref, slope_ref, steer_ref, small_sems = refs[:7]
    xbuf, aligned, weights, demod, products, carry, sems = refs[7:]
    small = fetch_small(
        (shift_hbm, row_hbm, tap_hbm, angle_hbm, slope_hbm, steer_hbm),
        (shift_ref, row_ref, tap_ref, angle_ref, slope_ref, steer_ref),
        small_sems,
    )
    first_pulse = group * GROUP
    rows = x_hbm.shape[1]
    fetches = []
    for sub in range(GROUP // SUB):
        window = pl.ds(sub * SUB, SUB)
        fetches.append(
            pltpu.make_async_copy(
                x_hbm.at[pl.ds(first_pulse + sub * SUB, SUB)], xbuf.at[window], sems.at[sub]
            )
        )
        fetches[-1].start()
    for copy in small:
        copy.wait()
    here = slice(first_pulse, first_pulse + GROUP)
    slope, angle = slope_ref[:, here], angle_ref[:, here]
    phase, step = lane_phases(slope)
    fill_weights(tap_factors(start_ref, tap_ref, angle, slope, here), steer_ref, weights)
    offset = jnp.broadcast_to((row_ref[:, here] - 3).astype(jnp.float32), (GROUP, GROUP)).T.astype(jnp.int32)
    lane = lax.broadcasted_iota(jnp.int32, (rows, LANES), 1)
    for local in range(GROUP):
        if local % SUB == 0:
            fetches[local // SUB].wait()
        rest, back, first = place_of(shift_ref, first_pulse + local, local)
        data = xbuf[local].astype(jnp.float32)
        mixed = jnp.where(lane >= rest, data, pltpu.roll(data, rows - 2, 0))
        aligned[pl.ds(first, rows, stride=STRIDE), :] = pltpu.roll(mixed, back, 1)

    last = rows // 2 - 1
    edges = (-1, 0, last, last + 1)

    def store(row, block, total):
        if 0 < block < last:
            out_ref[pl.ds(row, 8), pl.ds((block - 1) * LANES, LANES)] = total.astype(jnp.bfloat16)
            return
        spot = edges.index(block)
        if not group:
            partial_ref[pl.ds(row, 8), pl.ds(spot * LANES, LANES)] = total
            return
        target, column = ((below_ref, 0), (own_ref, 0), (own_ref, LANES), (above_ref, 0))[spot]
        here = pl.ds(column, LANES)
        target[pl.ds(64 + row, 8), here] = total.astype(target.dtype)
        target[pl.ds(row, 8), here] = given_ref[pl.ds(row, 8), pl.ds(spot * LANES, LANES)].astype(target.dtype)

    sweep(last, aligned, offset, phase, step, weights, demod, products, carry, store)


def seal_kernel(ends, place_ref, own_ref, left_ref, right_ref, out_ref):
    for column, ref, outer in ((0, left_ref, 0), (LANES, right_ref, ends)):
        here = pl.ds(column, LANES)
        side = jnp.where(place_ref[0] == outer, 0.0, ref[...].astype(jnp.float32))
        out_ref[:, here] = (own_ref[:, here] + side).astype(jnp.bfloat16)


def grant(mebibytes):
    return pltpu.CompilerParams(vmem_limit_bytes=mebibytes * 1024 * 1024)


SMEM = pl.BlockSpec(memory_space=pltpu.SMEM)
VMEM = pl.BlockSpec(memory_space=pltpu.VMEM)
ANY = pl.BlockSpec(memory_space=pl.ANY)
HBM = pl.BlockSpec(memory_space=pltpu.HBM)


def small_scratch(small):
    spaces = [pltpu.SMEM] + [pltpu.VMEM] * (len(small) - 1)
    return [space(item.shape, item.dtype) for space, item in zip(spaces, small)] + [
        pltpu.SemaphoreType.DMA((len(small),))
    ]


def make_inner(group, start, x3, small, partial=None):
    _, rows, _ = x3.shape
    width = (rows // 2 + 2) * LANES
    inner = jax.ShapeDtypeStruct((64, width - 4 * LANES), jnp.bfloat16)
    if group:
        side = jax.ShapeDtypeStruct((128, LANES), jnp.bfloat16)
        outs = (inner, side, side, jax.ShapeDtypeStruct((128, 2 * LANES), jnp.float32))
        given = (partial,)
    else:
        outs = (inner, jax.ShapeDtypeStruct((64, 4 * LANES), jnp.float32))
        given = ()
    return pl.pallas_call(
        functools.partial(inner_kernel, group),
        out_shape=outs,
        in_specs=[SMEM] + [HBM] * (1 + len(small)) + [VMEM] * len(given),
        out_specs=(VMEM,) * len(outs),
        scratch_shapes=small_scratch(small)
        + [
            pltpu.VMEM((GROUP, rows, LANES), jnp.bfloat16),
            pltpu.VMEM(((rows + 2) * STRIDE, LANES), jnp.float32),
            pltpu.VMEM((64 * TAPS, 2 * GROUP), jnp.bfloat16),
            pltpu.VMEM((2 * GROUP, width), jnp.bfloat16),
            pltpu.VMEM((64 * TAPS, width), jnp.float32),
            pltpu.VMEM((64 * TAPS, LANES), jnp.float32),
            pltpu.SemaphoreType.DMA((GROUP // SUB,)),
        ],
        compiler_params=grant(60),
        cost_estimate=pl.CostEstimate(flops=2000000000, bytes_accessed=4000000, transcendentals=0),
    )(start, x3, *small, *given)


def seal(ends, place, own, left, right):
    return pl.pallas_call(
        functools.partial(seal_kernel, ends),
        name="seal",
        out_shape=jax.ShapeDtypeStruct(own.shape, jnp.bfloat16),
        in_specs=[SMEM] + [VMEM] * 3,
        out_specs=VMEM,
        compiler_params=grant(4),
        cost_estimate=pl.CostEstimate(flops=1000000, bytes_accessed=300000, transcendentals=0),
    )(place, own, left, right)


def expand_kernel(where_ref, coeff_ref, out_ref):
    width = out_ref.shape[1]
    lane = lax.broadcasted_iota(jnp.int32, (FOOT, width), 1)
    dims = (((0,), (0,)), ((), ()))
    for tile in range(TILE_DEV):
        spot = where_ref[pl.ds(tile * FOOT, FOOT), :]
        hot_re = (lane == spot).astype(jnp.float32).astype(jnp.bfloat16)
        hot_im = (lane == spot + BEAMS).astype(jnp.float32).astype(jnp.bfloat16)
        c_re, c_im = coeff_ref[tile, 0], coeff_ref[tile, 1]
        dot = functools.partial(lax.dot_general, dimension_numbers=dims, preferred_element_type=jnp.float32)
        at = tile * 2 * AZ
        out_ref[pl.ds(at, AZ), :] = (dot(c_re, hot_re) - dot(c_im, hot_im)).astype(jnp.bfloat16)
        out_ref[pl.ds(at + AZ, AZ), :] = (dot(c_im, hot_re) + dot(c_re, hot_im)).astype(jnp.bfloat16)


def project_kernel(count, pieces, coeff_ref, *refs):
    sources = refs[:count]
    if sources[0].shape[0] > 64:
        sources = [ref.at[pl.ds(row, 64)] for row in range(0, sources[0].shape[0], 64) for ref in sources]
    out_hbm, tile, sems = refs[-3:]
    depth, count = 64, len(sources)
    copies = []
    for source, target, width in pieces:
        for start in range(0, width, 256):
            size = min(256, width - start)
            here = pl.ds(source + start, size)
            total = None
            for first in range(0, count, 256 // depth):
                part = sources[first : first + 256 // depth]
                data = jnp.concatenate([ref[:, here] for ref in part], axis=0)
                window = pl.ds(first * depth, len(part) * depth)
                term = jnp.dot(coeff_ref[:, window], data, preferred_element_type=jnp.float32)
                total = term if total is None else total + term
            tile[:, here] = total.astype(jnp.bfloat16)
            copy = pltpu.make_async_copy(
                tile.at[:, here], out_hbm.at[:, pl.ds(target + start, size)], sems.at[len(copies)]
            )
            copy.start()
            copies.append(copy)
    for copy in copies:
        copy.wait()


def project(coeffs, sources, image, pieces, cells):
    count = len(sources)
    width = sources[0].shape[1]
    rows, depth = coeffs.shape
    extra = [] if image is None else [image]
    return pl.pallas_call(
        functools.partial(project_kernel, count, pieces),
        out_shape=jax.ShapeDtypeStruct((rows, cells), jnp.bfloat16),
        in_specs=[VMEM] * (1 + count) + [HBM] * len(extra),
        out_specs=HBM,
        input_output_aliases={1 + count: 0} if extra else {},
        scratch_shapes=[
            pltpu.VMEM((rows, width), jnp.bfloat16),
            pltpu.SemaphoreType.DMA((sum(-(-piece[2] // 256) for piece in pieces),)),
        ],
        compiler_params=grant(10 + 2 * depth // 1024),
        cost_estimate=pl.CostEstimate(flops=2 * rows * width * depth, bytes_accessed=3000000, transcendentals=0),
    )(coeffs, *sources, *extra)


def body(echoes, shifts, tap_weights, angles, slopes, steering, footprint, tile_coeffs):
    pulses, _, cells = echoes.shape
    blocks = cells // LANES
    pulse_count = lax.axis_size("pulse")
    range_count = lax.axis_size("range")
    me = lax.axis_index("pulse")
    start_cell = lax.axis_index("range") * cells

    x4 = echoes.reshape(pulses, 2, blocks, LANES).transpose(0, 2, 1, 3)
    shared = (jnp.reshape(start_cell, (1,)), x4.reshape(pulses, 2 * blocks, LANES))
    small = (shifts, shifts[None, :], tap_weights.T, angles[None, :], slopes[None, :], steering)
    inner_a, partial = make_inner(0, *shared, small)
    inner_b, below, above, own = make_inner(1, *shared, small, partial)
    inner = [inner_a, inner_b]
    ring = [(i, (i + 1) % range_count) for i in range(range_count)]
    left = lax.ppermute(above, "range", ring)
    right = lax.ppermute(below, "range", [(target, source) for source, target in ring])
    place = jnp.reshape(lax.axis_index("range"), (1,))
    edges = seal(range_count - 1, place, own, left, right)

    entries = TILE_DEV * FOOT
    chips = pulse_count // 2
    beam_dev = pulses // SUB * BEAMS
    ids = lax.dynamic_index_in_dim(footprint.reshape(pulse_count, entries), me, 0, keepdims=False)
    owner = ids // beam_dev
    inside = ids % beam_dev
    place = 2 * ((me // 2 - owner // 2) % chips) + (me % 2 + owner % 2) % 2
    sub = inside // BEAMS
    where = place * 64 + (sub % 4) * (2 * BEAMS) + inside % BEAMS + (sub // 4) * (pulse_count * 64)
    coeffs = pl.pallas_call(
        expand_kernel,
        name="expand",
        compiler_params=grant(6),
        out_shape=jax.ShapeDtypeStruct((TILE_DEV * 2 * AZ, pulse_count * 2 * beam_dev), jnp.bfloat16),
    )(where[:, None], tile_coeffs.transpose(0, 1, 3, 2))

    swap = [(i, i ^ 1) for i in range(pulse_count)]

    def spread(own):
        sources = []
        for hop in range(chips):
            ahead = own
            if hop:
                ahead = lax.ppermute(own, "pulse", [(i, (i + 2 * hop) % pulse_count) for i in range(pulse_count)])
            sources += [ahead, lax.ppermute(ahead, "pulse", swap)]
        return sources

    spread_inner = [spread(own) for own in inner]
    spread_edges = spread(edges)
    width = cells - 2 * LANES
    image = project(coeffs, sum(spread_inner, []), None, ((0, LANES, width),), cells)
    pieces = ((0, 0, LANES), (LANES, cells - LANES, LANES))
    image = project(coeffs, spread_edges, image, pieces, cells)
    return image.reshape(TILE_DEV, 2, AZ, cells)


def solution(mesh):
    placed = (
        P(("groups", "pulse"), None, "range"),
        P(("groups", "pulse")),
        P(("groups", "pulse"), None),
        P(("groups", "pulse")),
        P(("groups", "pulse")),
        P(),
        P("groups", None),
        P(("groups", "pulse"), None, None, None),
    )
    return jax.shard_map(
        body,
        mesh=mesh,
        in_specs=placed,
        out_specs=P(("groups", "pulse"), None, None, "range"),
        check_vma=False,
    )
```

time: 249 us -> 33.8 us (0.14)
  matrix products: 106 us -> 0 us
  local copies, waits for them, and re-layouts: 82.2 us -> 2.05 us
  waiting for transfers between devices: 25.9 us -> 6.75 us
  Pallas kernels: 0 us -> 13.8 us
  between operations: 13.7 us -> 0.1 us
  other arithmetic: 13.4 us -> 0.3 us
  starting transfers between devices: 6.26 us -> 10.5 us
    conv_general_dilated x1 -> x0, matrix products: 103 us -> none  [align_block(): lax.conv_general_dilated(source, kernel, (1,), 'VALID', dimension_numbers...]
    conv_general_dilated x7 -> x0, local copies, waits for them, and re-layouts: 31.2 us -> none  [align_block(): lax.conv_general_dilated(source, kernel, (1,), 'VALID', dimension_numbers...]
    all_gather x1 -> x0, waiting for transfers between devices: 22.7 us -> none  [body(): gathered = lax.all_gather(beam_rows, 'pulse', axis=0, tiled=True)]
    slice x3 -> x0, local copies, waits for them, and re-layouts: 15.5 us -> none  [the longest x1 7.79 us: align_block(): real_part = cosine_values * summed[:, 0] - sine_values * summed[:, 1]]
    concatenate x1 -> x0, local copies, waits for them, and re-layouts: 14.3 us -> none  [padded_2(): jnp.concatenate([lax.ppermute(tail, axis, [(i, (i + 1) % count) for i in...]
    pallas_call x0 -> x6, Pallas kernels: none -> 13.8 us  [the longest x2 10.2 us: make_inner(): pl.pallas_call(functools.partial(inner_kernel, group), out_shape=outs, in...]
    reshape x4 -> x1, local copies, waits for them, and re-layouts: 12.5 us -> 0.08 us  [body(): footprint.reshape(pulse_count, entries)]
    another operation x3 -> x0, other arithmetic: 11.3 us -> none
  transfers between devices with their start and end apart: 3 -> 11, of which waited for: 2 -> 3; matrix products, arithmetic and copies ran while one was open for 1% -> 1% of each run, Pallas kernels for 0% -> 24%
where the time goes in v3:
time: 33.8 us; the launch traced here: 33.6 us
  Pallas kernels  13.8 us (41%)
  starting transfers between devices  10.5 us (31%)
  waiting for transfers between devices  6.75 us (20%)
  local copies, waits for them, and re-layouts  2.05 us (6%)
    pallas_call x2, Pallas kernels, make_inner(): pl.pallas_call(functools.partial(inner_kernel, group), out_shape=outs, in...  10.2 us
    ppermute x3, starting transfers between devices, spread(): lax.ppermute(own, 'pulse', [(i, (i + 2 * hop) % pulse_count) for i in ran...  4.95 us
    ppermute x1, waiting for transfers between devices, body(): left = lax.ppermute(above, 'range', ring)  3.53 us
    pallas_call x2, Pallas kernels, project(): pl.pallas_call(functools.partial(project_kernel, count, pieces), out_shap...  3.17 us
    ppermute x1, starting transfers between devices, body(): left = lax.ppermute(above, 'range', ring)  2.04 us
    ppermute x1, starting transfers between devices, body(): lax.ppermute(below, 'range', [(target, source) for source, target in ring])  2.02 us
    unnamed x10, local copies, waits for them, and re-layouts  1.85 us
    ppermute x3, waiting for transfers between devices, spread(): lax.ppermute(own, 'pulse', [(i, (i + 2 * hop) % pulse_count) for i in ran...  1.76 us
  transfers between devices with their start and end apart: 11, of which 3 were waited for; matrix products, arithmetic and copies ran while one was open for 1% of the time, Pallas kernels for 24%

profile of v3, /device:TPU:0, one launch (start us, length us, event | category | flops | bytes accessed | tf_op | source)
XLA Modules:
  0.0 33.6 jit_solution(6494382181336739063)
XLA Ops:
  0.0 4.6 %shard_map.82 = (bf16[64,1792]{1,0:T(8,128)(2,1)}, f32[64,512]{1,0:T(8,128)}) custom-call(s32[1]{0:T(128)} %bitcast.3.start_ref, bf16[256,32,128]{2,1,0:T(8,128)(2,1)} %bitcast.16, s32[256]{0:T(256)} %shift_hbm.3, s32[1,256]{1,0:T(1,128)} %bitcast.20, f32[8,256]{1,0:T(8,128)} %bitcast.18, f32[1,256]{1,0:T(1,128)} %bitcast.22, f32[1,256]{1,0:T(1,128)} %bitcast.24, ...), custom_call_target="tpu_custom_call" | custom-call | flops 2000000000 | bytes 4000000 | tf_op jit(solution)/shard_map/pallas_call | solution.py:237
  4.6 3.0 %collective-permute-start.6 = (bf16[64,1792]{1,0:T(8,128)(2,1)}, bf16[64,1792]{1,0:T(8,128)(2,1)S(1)}, u32[]{:S(2)}, u32[]{:S(2)}) collective-permute-start(bf16[64,1792]{1,0:T(8,128)(2,1)} %get-tuple-element.15.refs_0_), channel_id=1, source_target_pairs={{0,8},{4,12},{8,0},{12,4},{1,9},{5,13},{9,1},{13,5},{2,10},{6,14},... | collective-permute-start | bytes 688136 | tf_op jit(solution)/shard_map/ppermute | solution.py:375
  7.6 0.0 copy-start
  7.6 0.0 copy-start.4
  7.7 0.0 copy-start.3
  7.7 5.5 %shard_map.83 = (bf16[64,1792]{1,0:T(8,128)(2,1)}, bf16[128,128]{1,0:T(8,128)(2,1)}, bf16[128,128]{1,0:T(8,128)(2,1)}, f32[128,256]{1,0:T(8,128)}) custom-call(s32[1]{0:T(128)} %bitcast.3.start_ref, bf16[256,32,128]{2,1,0:T(8,128)(2,1)} %bitcast.17, s32[256]{0:T(256)} %shift_hbm.3, s32[1,256]{1,0:T(1,128)} %bitcast.21, f32[8,256]{1,0:T(8,128)} %bitcast.19, ...), custom_call_target="tpu_custom_call" | custom-call | flops 2000000000 | bytes 4000000 | tf_op jit(solution)/shard_map/pallas_call | solution.py:237
  13.2 0.1 collective-permute-start.9
  13.3 2.0 %collective-permute-start = (bf16[128,128]{1,0:T(8,128)(2,1)}, bf16[128,128]{1,0:T(8,128)(2,1)S(1)}, u32[]{:S(2)}, u32[]{:S(2)}) collective-permute-start(bf16[128,128]{1,0:T(8,128)(2,1)} %get-tuple-element.13), channel_id=1, source_target_pairs={{0,1},{1,2},{2,3},{3,0},{4,5},{5,6},{6,7},{7,4},{8,9},{9,10},{10,1... | collective-permute-start | bytes 98312 | tf_op jit(solution)/shard_map/ppermute | solution.py:347
  15.4 0.0 copy-done
  15.4 0.0 collective-permute-start.5
  15.4 0.5 %collective-permute-start.8 = (bf16[64,1792]{1,0:T(8,128)(2,1)}, bf16[64,1792]{1,0:T(8,128)(2,1)S(1)}, u32[]{:S(2)}, u32[]{:S(2)}) collective-permute-start(bf16[64,1792]{1,0:T(8,128)(2,1)} %get-tuple-element.16.refs_4_), channel_id=1, source_target_pairs={{0,4},{4,0},{8,12},{12,8},{1,5},{5,1},{9,13},{13,9},{2,6},{6,2},{1... | collective-permute-start | bytes 688136 | tf_op jit(solution)/shard_map/ppermute | solution.py:376
  15.9 0.0 copy-done.4
  15.9 0.1 reshape.401
  16.0 3.5 %collective-permute-done.left_ref = bf16[128,128]{1,0:T(8,128)(2,1)S(1)} collective-permute-done((bf16[128,128]{1,0:T(8,128)(2,1)}, bf16[128,128]{1,0:T(8,128)(2,1)S(1)}, u32[]{:S(2)}, u32[]{:S(2)}) %collective-permute-start) | collective-permute-done | bytes 32800 | tf_op jit(solution)/shard_map/ppermute | solution.py:347
  19.5 2.0 %collective-permute-start.1 = (bf16[128,128]{1,0:T(8,128)(2,1)}, bf16[128,128]{1,0:T(8,128)(2,1)S(1)}, u32[]{:S(2)}, u32[]{:S(2)}) collective-permute-start(bf16[128,128]{1,0:T(8,128)(2,1)} %get-tuple-element.14), channel_id=1, source_target_pairs={{1,0},{2,1},{3,2},{0,3},{5,4},{6,5},{7,6},{4,7},{9,8},{10,9},{11,1... | collective-permute-start | bytes 98312 | tf_op jit(solution)/shard_map/ppermute | solution.py:348
  21.5 0.0 collective-permute-done.6.refs_2_
  21.5 0.0 collective-permute-start.7
  21.5 0.0 collective-permute-done.9.refs_6_
  21.5 0.5 %collective-permute-start.10 = (bf16[64,1792]{1,0:T(8,128)(2,1)S(1)}, bf16[64,1792]{1,0:T(8,128)(2,1)S(1)}, u32[]{:S(2)}, u32[]{:S(2)}) collective-permute-start(bf16[64,1792]{1,0:T(8,128)(2,1)S(1)} %collective-permute-done.9.refs_6_), channel_id=1, source_target_pairs={{0,4},{4,0},{8,12},{12,8},{1,5},{5,1},{9,13},{13,9},{2,6},{6,2},{1... | collective-permute-start | bytes 688136 | tf_op jit(solution)/shard_map/ppermute | solution.py:376
  22.1 0.1 copy.10
  22.2 1.5 %collective-permute-done.1.right_ref = bf16[128,128]{1,0:T(8,128)(2,1)S(1)} collective-permute-done((bf16[128,128]{1,0:T(8,128)(2,1)}, bf16[128,128]{1,0:T(8,128)(2,1)S(1)}, u32[]{:S(2)}, u32[]{:S(2)}) %collective-permute-start.1) | collective-permute-done | bytes 32800 | tf_op jit(solution)/shard_map/ppermute | solution.py:348
  23.6 0.0 copy-start.2
  23.6 0.9 %copy-done.2 = f32[128,256]{1,0:T(8,128)S(1)} copy-done((f32[128,256]{1,0:T(8,128)S(1)}, f32[128,256]{1,0:T(8,128)}, u32[]{:S(2)}) %copy-start.2) | copy-done | bytes 131096
  24.6 1.8 %collective-permute-start.3 = (bf16[128,256]{1,0:T(8,128)(2,1)S(1)}, bf16[128,256]{1,0:T(8,128)(2,1)S(1)}, u32[]{:S(2)}, u32[]{:S(2)}) collective-permute-start(bf16[128,256]{1,0:T(8,128)(2,1)S(1)} %seal.1.refs_0_), channel_id=1, source_target_pairs={{0,8},{4,12},{8,0},{12,4},{1,9},{5,13},{9,1},{13,5},{2,10},{6,14},... | collective-permute-start | bytes 196616 | tf_op jit(solution)/shard_map/ppermute | solution.py:375
  26.3 0.3 fusion.7.where_ref
  26.6 0.0 copy-done.3
  26.6 0.5 %expand.1.coeff_ref = bf16[512,512]{1,0:T(8,128)(2,1)S(1)} custom-call(s32[128,1]{1,0:T(8,128)S(1)} %fusion.7.where_ref, bf16[4,2,32,64]{3,2,1,0:T(8,128)(2,1)S(1)} %bitcast.15), custom_call_target="tpu_custom_call" | custom-call | tf_op jit(solution)/shard_map/expand/pallas_call | solution.py:361
  27.1 1.8 %collective-permute-done.3.refs_2_ = bf16[128,256]{1,0:T(8,128)(2,1)S(1)} collective-permute-done((bf16[128,256]{1,0:T(8,128)(2,1)S(1)}, bf16[128,256]{1,0:T(8,128)(2,1)S(1)}, u32[]{:S(2)}, u32[]{:S(2)}) %collective-permute-start.3) | collective-permute-done | bytes 65568 | tf_op jit(solution)/shard_map/ppermute | solution.py:375
  28.9 0.0 collective-permute-start.2
  28.9 0.0 collective-permute-done.5.refs_1_
  28.9 0.5 %collective-permute-start.4 = (bf16[128,256]{1,0:T(8,128)(2,1)S(1)}, bf16[128,256]{1,0:T(8,128)(2,1)S(1)}, u32[]{:S(2)}, u32[]{:S(2)}) collective-permute-start(bf16[128,256]{1,0:T(8,128)(2,1)S(1)} %collective-permute-done.3.refs_2_), channel_id=1, source_target_pairs={{0,4},{4,0},{8,12},{12,8},{1,5},{5,1},{9,13},{13,9},{2,6},{6,2},{1... | collective-permute-start | bytes 196616 | tf_op jit(solution)/shard_map/ppermute | solution.py:376
  29.4 0.0 collective-permute-done.8.refs_5_
  29.4 0.0 collective-permute-done.7.refs_3_
  29.4 0.0 collective-permute-done.10.refs_7_
  29.4 0.0 copy-start.1
  29.4 0.9 %copy-done.1 = bf16[64,1792]{1,0:T(8,128)(2,1)S(1)} copy-done((bf16[64,1792]{1,0:T(8,128)(2,1)S(1)}, bf16[64,1792]{1,0:T(8,128)(2,1)}, u32[]{:S(2)}) %copy-start.1) | copy-done | bytes 229400
  30.4 2.0 %shard_map.84.refs_4_ = bf16[512,2048]{1,0:T(8,128)(2,1)} custom-call(bf16[512,512]{1,0:T(8,128)(2,1)S(1)} %expand.1.coeff_ref, bf16[64,1792]{1,0:T(8,128)(2,1)S(1)} %copy-done, bf16[64,1792]{1,0:T(8,128)(2,1)S(1)} %collective-permute-done.5.refs_1_, bf16[64,1792]{1,0:T(8,128)(2,1)S(1)} %collective-permute-done.6.refs_2_, ...), custom_call_target="tpu_custom_call" | custom-call | flops 939524096 | bytes 3000000 | tf_op jit(solution)/shard_map/pallas_call | solution.py:317
  32.4 0.0 collective-permute-done.2.refs_1_
  32.4 0.0 collective-permute-done.4.refs_3_
  32.4 1.2 %shard_map.85 = bf16[512,2048]{1,0:T(8,128)(2,1)} custom-call(bf16[512,512]{1,0:T(8,128)(2,1)S(1)} %expand.1.coeff_ref, bf16[128,256]{1,0:T(8,128)(2,1)S(1)} %seal.1.refs_0_, bf16[128,256]{1,0:T(8,128)(2,1)S(1)} %collective-permute-done.2.refs_1_, bf16[128,256]{1,0:T(8,128)(2,1)S(1)} %collective-permute-done.3.refs_2_, ...), custom_call_target="tpu_custom_call", output_to_operand_aliasing={{}: (5, {})} | custom-call | flops 134217728 | bytes 3000000 | tf_op jit(solution)/shard_map/pallas_call | solution.py:317
  (2 shorter events, 0.0 us)
Async XLA Ops:
  4.6 16.9 %collective-permute-start.6 = (bf16[64,1792]{1,0:T(8,128)(2,1)}, bf16[64,1792]{1,0:T(8,128)(2,1)S(1)}, u32[]{:S(2)}, u32[]{:S(2)}) collective-permute-start(bf16[64,1792]{1,0:T(8,128)(2,1)} %get-tuple-element.15.refs_0_), channel_id=1, source_target_pairs={{0,8},{4,12},{8,0},{12,4},{1,9},{5,13},{9,1},{13,5},{2,10},{6,14},... | collective-permute-start | bytes 688136 | tf_op jit(solution)/shard_map/ppermute | solution.py:375
  7.6 7.7 %copy-start = (bf16[64,1792]{1,0:T(8,128)(2,1)S(1)}, bf16[64,1792]{1,0:T(8,128)(2,1)}, u32[]{:S(2)}) copy-start(bf16[64,1792]{1,0:T(8,128)(2,1)} %get-tuple-element.15.refs_0_) | copy-start | bytes 688132
  7.6 8.3 %copy-start.4 = (s32[16,32]{1,0:T(8,128)S(1)}, s32[16,32]{1,0:T(8,128)}, u32[]{:S(2)}) copy-start(s32[16,32]{1,0:T(8,128)} %param.14) | copy-start | bytes 6148
  7.7 19.0 %copy-start.3 = (bf16[4,2,64,32]{2,3,1,0:T(8,128)(2,1)S(1)}, bf16[4,2,64,32]{2,3,1,0:T(8,128)(2,1)}, u32[]{:S(2)}) copy-start(bf16[4,2,64,32]{2,3,1,0:T(8,128)(2,1)} %param.15) | copy-start | bytes 98308
  13.2 8.3 %collective-permute-start.9 = (bf16[64,1792]{1,0:T(8,128)(2,1)}, bf16[64,1792]{1,0:T(8,128)(2,1)S(1)}, u32[]{:S(2)}, u32[]{:S(2)}) collective-permute-start(bf16[64,1792]{1,0:T(8,128)(2,1)} %get-tuple-element.16.refs_4_), channel_id=1, source_target_pairs={{0,8},{4,12},{8,0},{12,4},{1,9},{5,13},{9,1},{13,5},{2,10},{6,14},... | collective-permute-start | bytes 688136 | tf_op jit(solution)/shard_map/ppermute | solution.py:375
  13.3 6.2 %collective-permute-start = (bf16[128,128]{1,0:T(8,128)(2,1)}, bf16[128,128]{1,0:T(8,128)(2,1)S(1)}, u32[]{:S(2)}, u32[]{:S(2)}) collective-permute-start(bf16[128,128]{1,0:T(8,128)(2,1)} %get-tuple-element.13), channel_id=1, source_target_pairs={{0,1},{1,2},{2,3},{3,0},{4,5},{5,6},{6,7},{7,4},{8,9},{9,10},{10,1... | collective-permute-start | bytes 98312 | tf_op jit(solution)/shard_map/ppermute | solution.py:347
  15.4 13.5 %collective-permute-start.5 = (bf16[64,1792]{1,0:T(8,128)(2,1)S(1)}, bf16[64,1792]{1,0:T(8,128)(2,1)S(1)}, u32[]{:S(2)}, u32[]{:S(2)}) collective-permute-start(bf16[64,1792]{1,0:T(8,128)(2,1)S(1)} %copy-done), channel_id=1, source_target_pairs={{0,4},{4,0},{8,12},{12,8},{1,5},{5,1},{9,13},{13,9},{2,6},{6,2},{1... | collective-permute-start | bytes 688136 | tf_op jit(solution)/shard_map/ppermute | solution.py:376
  15.4 14.0 %collective-permute-start.8 = (bf16[64,1792]{1,0:T(8,128)(2,1)}, bf16[64,1792]{1,0:T(8,128)(2,1)S(1)}, u32[]{:S(2)}, u32[]{:S(2)}) collective-permute-start(bf16[64,1792]{1,0:T(8,128)(2,1)} %get-tuple-element.16.refs_4_), channel_id=1, source_target_pairs={{0,4},{4,0},{8,12},{12,8},{1,5},{5,1},{9,13},{13,9},{2,6},{6,2},{1... | collective-permute-start | bytes 688136 | tf_op jit(solution)/shard_map/ppermute | solution.py:376
  19.5 4.1 %collective-permute-start.1 = (bf16[128,128]{1,0:T(8,128)(2,1)}, bf16[128,128]{1,0:T(8,128)(2,1)S(1)}, u32[]{:S(2)}, u32[]{:S(2)}) collective-permute-start(bf16[128,128]{1,0:T(8,128)(2,1)} %get-tuple-element.14), channel_id=1, source_target_pairs={{1,0},{2,1},{3,2},{0,3},{5,4},{6,5},{7,6},{4,7},{9,8},{10,9},{11,1... | collective-permute-start | bytes 98312 | tf_op jit(solution)/shard_map/ppermute | solution.py:348
  21.5 7.9 %collective-permute-start.7 = (bf16[64,1792]{1,0:T(8,128)(2,1)S(1)}, bf16[64,1792]{1,0:T(8,128)(2,1)S(1)}, u32[]{:S(2)}, u32[]{:S(2)}) collective-permute-start(bf16[64,1792]{1,0:T(8,128)(2,1)S(1)} %collective-permute-done.6.refs_2_), channel_id=1, source_target_pairs={{0,4},{4,0},{8,12},{12,8},{1,5},{5,1},{9,13},{13,9},{2,6},{6,2},{1... | collective-permute-start | bytes 688136 | tf_op jit(solution)/shard_map/ppermute | solution.py:376
  21.5 7.9 %collective-permute-start.10 = (bf16[64,1792]{1,0:T(8,128)(2,1)S(1)}, bf16[64,1792]{1,0:T(8,128)(2,1)S(1)}, u32[]{:S(2)}, u32[]{:S(2)}) collective-permute-start(bf16[64,1792]{1,0:T(8,128)(2,1)S(1)} %collective-permute-done.9.refs_6_), channel_id=1, source_target_pairs={{0,4},{4,0},{8,12},{12,8},{1,5},{5,1},{9,13},{13,9},{2,6},{6,2},{1... | collective-permute-start | bytes 688136 | tf_op jit(solution)/shard_map/ppermute | solution.py:376
  23.6 0.9 %copy-start.2 = (f32[128,256]{1,0:T(8,128)S(1)}, f32[128,256]{1,0:T(8,128)}, u32[]{:S(2)}) copy-start(f32[128,256]{1,0:T(8,128)} %get-tuple-element.12.own_ref) | copy-start | bytes 393220
  24.6 4.3 %collective-permute-start.3 = (bf16[128,256]{1,0:T(8,128)(2,1)S(1)}, bf16[128,256]{1,0:T(8,128)(2,1)S(1)}, u32[]{:S(2)}, u32[]{:S(2)}) collective-permute-start(bf16[128,256]{1,0:T(8,128)(2,1)S(1)} %seal.1.refs_0_), channel_id=1, source_target_pairs={{0,8},{4,12},{8,0},{12,4},{1,9},{5,13},{9,1},{13,5},{2,10},{6,14},... | collective-permute-start | bytes 196616 | tf_op jit(solution)/shard_map/ppermute | solution.py:375
  28.9 3.5 %collective-permute-start.2 = (bf16[128,256]{1,0:T(8,128)(2,1)S(1)}, bf16[128,256]{1,0:T(8,128)(2,1)S(1)}, u32[]{:S(2)}, u32[]{:S(2)}) collective-permute-start(bf16[128,256]{1,0:T(8,128)(2,1)S(1)} %seal.1.refs_0_), channel_id=1, source_target_pairs={{0,4},{4,0},{8,12},{12,8},{1,5},{5,1},{9,13},{13,9},{2,6},{6,2},{1... | collective-permute-start | bytes 196616 | tf_op jit(solution)/shard_map/ppermute | solution.py:376
  28.9 3.5 %collective-permute-start.4 = (bf16[128,256]{1,0:T(8,128)(2,1)S(1)}, bf16[128,256]{1,0:T(8,128)(2,1)S(1)}, u32[]{:S(2)}, u32[]{:S(2)}) collective-permute-start(bf16[128,256]{1,0:T(8,128)(2,1)S(1)} %collective-permute-done.3.refs_2_), channel_id=1, source_target_pairs={{0,4},{4,0},{8,12},{12,8},{1,5},{5,1},{9,13},{13,9},{2,6},{6,2},{1... | collective-permute-start | bytes 196616 | tf_op jit(solution)/shard_map/ppermute | solution.py:376
  29.4 0.9 %copy-start.1 = (bf16[64,1792]{1,0:T(8,128)(2,1)S(1)}, bf16[64,1792]{1,0:T(8,128)(2,1)}, u32[]{:S(2)}) copy-start(bf16[64,1792]{1,0:T(8,128)(2,1)} %get-tuple-element.16.refs_4_) | copy-start | bytes 688132

commit v4 on v3

--- a/solution.py
+++ b/solution.py
@@ -15,6 +15,7 @@
 AZ = 64
 LANES = 128
 STRIDE = 136
+GRANTS = (60, 40)
 GROUP = 128
 
 
@@ -139,31 +140,24 @@
     return copies
 
 
-def inner_kernel(group, start_ref, x_hbm, shift_hbm, row_hbm, tap_hbm, angle_hbm, slope_hbm, steer_hbm, *refs):
+def inner_kernel(group, start_ref, *refs):
+    first_pulse = group * GROUP
     if group:
-        given_ref, out_ref, below_ref, above_ref, own_ref = refs[:5]
-        refs = refs[5:]
+        x_ref, row_ref, tap_ref, angle_ref, slope_ref, steer_ref, shift_ref = refs[:7]
+        base, small, fetches = first_pulse, [], []
+        refs = refs[7:]
     else:
-        out_ref, partial_ref = refs[:2]
-        refs = refs[2:]
-    shift_ref, row_ref, tap_ref, angle_ref, slope_ref, steer_ref, small_sems = refs[:7]
-    xbuf, aligned, weights, demod, products, carry, sems = refs[7:]
-    small = fetch_small(
-        (shift_hbm, row_hbm, tap_hbm, angle_hbm, slope_hbm, steer_hbm),
-        (shift_ref, row_ref, tap_ref, angle_ref, slope_ref, steer_ref),
-        small_sems,
-    )
-    first_pulse = group * GROUP
-    rows = x_hbm.shape[1]
-    fetches = []
-    for sub in range(GROUP // SUB):
-        window = pl.ds(sub * SUB, SUB)
-        fetches.append(
-            pltpu.make_async_copy(
-                x_hbm.at[pl.ds(first_pulse + sub * SUB, SUB)], xbuf.at[window], sems.at[sub]
-            )
-        )
-        fetches[-1].start()
+        given, (x_hbm, refs) = refs[1:7], (refs[0], refs[7:])
+        row_ref, tap_ref, angle_ref, slope_ref, steer_ref, shift_ref, small_sems, x_ref, sems = refs[2:11]
+        refs = refs[:2] + refs[11:]
+        small = fetch_small(given, (row_ref, tap_ref, angle_ref, slope_ref, steer_ref, shift_ref), small_sems)
+        base, fetches = 0, []
+        for sub in range(GROUP // SUB):
+            window = pl.ds(sub * SUB, SUB)
+            fetches.append(pltpu.make_async_copy(x_hbm.at[window], x_ref.at[window], sems.at[sub]))
+            fetches[-1].start()
+    out_ref, partial_ref, aligned, weights, demod, products, carry = refs
+    rows = x_ref.shape[1]
     for copy in small:
         copy.wait()
     here = slice(first_pulse, first_pulse + GROUP)
@@ -173,10 +167,10 @@
     offset = jnp.broadcast_to((row_ref[:, here] - 3).astype(jnp.float32), (GROUP, GROUP)).T.astype(jnp.int32)
     lane = lax.broadcasted_iota(jnp.int32, (rows, LANES), 1)
     for local in range(GROUP):
-        if local % SUB == 0:
+        if fetches and local % SUB == 0:
             fetches[local // SUB].wait()
         rest, back, first = place_of(shift_ref, first_pulse + local, local)
-        data = xbuf[local].astype(jnp.float32)
+        data = x_ref[base + local].astype(jnp.float32)
         mixed = jnp.where(lane >= rest, data, pltpu.roll(data, rows - 2, 0))
         aligned[pl.ds(first, rows, stride=STRIDE), :] = pltpu.roll(mixed, back, 1)
 
@@ -186,24 +180,24 @@
     def store(row, block, total):
         if 0 < block < last:
             out_ref[pl.ds(row, 8), pl.ds((block - 1) * LANES, LANES)] = total.astype(jnp.bfloat16)
-            return
-        spot = edges.index(block)
-        if not group:
-            partial_ref[pl.ds(row, 8), pl.ds(spot * LANES, LANES)] = total
-            return
-        target, column = ((below_ref, 0), (own_ref, 0), (own_ref, LANES), (above_ref, 0))[spot]
-        here = pl.ds(column, LANES)
-        target[pl.ds(64 + row, 8), here] = total.astype(target.dtype)
-        target[pl.ds(row, 8), here] = given_ref[pl.ds(row, 8), pl.ds(spot * LANES, LANES)].astype(target.dtype)
+        else:
+            partial_ref[pl.ds(row, 8), pl.ds(edges.index(block) * LANES, LANES)] = total
 
     sweep(last, aligned, offset, phase, step, weights, demod, products, carry, store)
 
 
-def seal_kernel(ends, place_ref, own_ref, left_ref, right_ref, out_ref):
+def join_kernel(a_ref, b_ref, below_ref, above_ref):
+    for row, ref in ((0, a_ref), (64, b_ref)):
+        below_ref[pl.ds(row, 64), :] = ref[:, 0:LANES].astype(jnp.bfloat16)
+        above_ref[pl.ds(row, 64), :] = ref[:, 3 * LANES : 4 * LANES].astype(jnp.bfloat16)
+
+
+def seal_kernel(ends, place_ref, a_ref, b_ref, left_ref, right_ref, out_ref):
     for column, ref, outer in ((0, left_ref, 0), (LANES, right_ref, ends)):
-        here = pl.ds(column, LANES)
         side = jnp.where(place_ref[0] == outer, 0.0, ref[...].astype(jnp.float32))
-        out_ref[:, here] = (own_ref[:, here] + side).astype(jnp.bfloat16)
+        for row, own in ((0, a_ref), (64, b_ref)):
+            total = own[:, LANES + column : 2 * LANES + column] + side[row : row + 64]
+            out_ref[pl.ds(row, 64), pl.ds(column, LANES)] = total.astype(jnp.bfloat16)
 
 
 def grant(mebibytes):
@@ -216,54 +210,62 @@
 HBM = pl.BlockSpec(memory_space=pltpu.HBM)
 
 
-def small_scratch(small):
-    spaces = [pltpu.SMEM] + [pltpu.VMEM] * (len(small) - 1)
-    return [space(item.shape, item.dtype) for space, item in zip(spaces, small)] + [
-        pltpu.SemaphoreType.DMA((len(small),))
-    ]
-
-
-def make_inner(group, start, x3, small, partial=None):
+def make_inner(group, start, x3, small, shifts):
     _, rows, _ = x3.shape
     width = (rows // 2 + 2) * LANES
-    inner = jax.ShapeDtypeStruct((64, width - 4 * LANES), jnp.bfloat16)
-    if group:
-        side = jax.ShapeDtypeStruct((128, LANES), jnp.bfloat16)
-        outs = (inner, side, side, jax.ShapeDtypeStruct((128, 2 * LANES), jnp.float32))
-        given = (partial,)
-    else:
-        outs = (inner, jax.ShapeDtypeStruct((64, 4 * LANES), jnp.float32))
-        given = ()
+    fetched = []
+    if not group:
+        fetched = [pltpu.VMEM(item.shape, item.dtype) for item in small] + [
+            pltpu.SMEM(shifts.shape, shifts.dtype),
+            pltpu.SemaphoreType.DMA((len(small) + 1,)),
+            pltpu.VMEM((GROUP, rows, LANES), jnp.bfloat16),
+            pltpu.SemaphoreType.DMA((GROUP // SUB,)),
+        ]
+    specs = [VMEM] * (1 + len(small)) + [SMEM] if group else [HBM] * (2 + len(small))
     return pl.pallas_call(
         functools.partial(inner_kernel, group),
-        out_shape=outs,
-        in_specs=[SMEM] + [HBM] * (1 + len(small)) + [VMEM] * len(given),
-        out_specs=(VMEM,) * len(outs),
-        scratch_shapes=small_scratch(small)
+        out_shape=(
+            jax.ShapeDtypeStruct((64, width - 4 * LANES), jnp.bfloat16),
+            jax.ShapeDtypeStruct((64, 4 * LANES), jnp.float32),
+        ),
+        in_specs=[SMEM] + specs,
+        out_specs=(VMEM, VMEM),
+        scratch_shapes=fetched
         + [
-            pltpu.VMEM((GROUP, rows, LANES), jnp.bfloat16),
             pltpu.VMEM(((rows + 2) * STRIDE, LANES), jnp.float32),
             pltpu.VMEM((64 * TAPS, 2 * GROUP), jnp.bfloat16),
             pltpu.VMEM((2 * GROUP, width), jnp.bfloat16),
             pltpu.VMEM((64 * TAPS, width), jnp.float32),
             pltpu.VMEM((64 * TAPS, LANES), jnp.float32),
-            pltpu.SemaphoreType.DMA((GROUP // SUB,)),
         ],
-        compiler_params=grant(60),
+        compiler_params=grant(GRANTS[group]),
         cost_estimate=pl.CostEstimate(flops=2000000000, bytes_accessed=4000000, transcendentals=0),
-    )(start, x3, *small, *given)
-
-
-def seal(ends, place, own, left, right):
+    )(start, x3, *small, shifts)
+
+
+def join(part_a, part_b):
+    side = jax.ShapeDtypeStruct((128, LANES), jnp.bfloat16)
+    return pl.pallas_call(
+        join_kernel,
+        name="join",
+        out_shape=(side, side),
+        in_specs=[VMEM, VMEM],
+        out_specs=(VMEM, VMEM),
+        compiler_params=grant(4),
+        cost_estimate=pl.CostEstimate(flops=1000000, bytes_accessed=300000, transcendentals=0),
+    )(part_a, part_b)
+
+
+def seal(ends, place, part_a, part_b, left, right):
     return pl.pallas_call(
         functools.partial(seal_kernel, ends),
         name="seal",
-        out_shape=jax.ShapeDtypeStruct(own.shape, jnp.bfloat16),
-        in_specs=[SMEM] + [VMEM] * 3,
+        out_shape=jax.ShapeDtypeStruct((128, 2 * LANES), jnp.bfloat16),
+        in_specs=[SMEM] + [VMEM] * 4,
         out_specs=VMEM,
         compiler_params=grant(4),
         cost_estimate=pl.CostEstimate(flops=1000000, bytes_accessed=300000, transcendentals=0),
-    )(place, own, left, right)
+    )(place, part_a, part_b, left, right)
 
 
 def expand_kernel(where_ref, coeff_ref, out_ref):
@@ -281,52 +283,47 @@
         out_ref[pl.ds(at + AZ, AZ), :] = (dot(c_im, hot_re) + dot(c_re, hot_im)).astype(jnp.bfloat16)
 
 
-def project_kernel(count, pieces, coeff_ref, *refs):
-    sources = refs[:count]
-    if sources[0].shape[0] > 64:
-        sources = [ref.at[pl.ds(row, 64)] for row in range(0, sources[0].shape[0], 64) for ref in sources]
-    out_hbm, tile, sems = refs[-3:]
-    depth, count = 64, len(sources)
+def project_kernel(members, coeff_ref, *refs):
+    inner, edges = refs[: 2 * members], refs[2 * members : 3 * members]
+    out_hbm, tile, sems = refs[3 * members :]
+    cells = tile.shape[1]
+    width = cells - 2 * LANES
+    edges = [ref.at[pl.ds(row, 64)] for row in (0, 64) for ref in edges]
+    jobs = [(inner, start, LANES + start, ((LANES + start, 256, 0),)) for start in range(0, width, 256)]
+    jobs.append((edges, 0, 0, ((0, LANES, 0), (cells - LANES, LANES, LANES))))
     copies = []
-    for source, target, width in pieces:
-        for start in range(0, width, 256):
-            size = min(256, width - start)
-            here = pl.ds(source + start, size)
-            total = None
-            for first in range(0, count, 256 // depth):
-                part = sources[first : first + 256 // depth]
-                data = jnp.concatenate([ref[:, here] for ref in part], axis=0)
-                window = pl.ds(first * depth, len(part) * depth)
-                term = jnp.dot(coeff_ref[:, window], data, preferred_element_type=jnp.float32)
-                total = term if total is None else total + term
-            tile[:, here] = total.astype(jnp.bfloat16)
-            copy = pltpu.make_async_copy(
-                tile.at[:, here], out_hbm.at[:, pl.ds(target + start, size)], sems.at[len(copies)]
-            )
-            copy.start()
-            copies.append(copy)
+    for sources, start, _, targets in jobs:
+        here = pl.ds(start, 256)
+        total = None
+        for first in range(0, 2 * members, 4):
+            data = jnp.concatenate([ref[:, here] for ref in sources[first : first + 4]], axis=0)
+            term = jnp.dot(coeff_ref[:, pl.ds(first * 64, 256)], data, preferred_element_type=jnp.float32)
+            total = term if total is None else total + term
+        total = total.astype(jnp.bfloat16)
+        for target, size, skip in targets:
+            there = pl.ds(target, size)
+            tile[:, there] = total[:, skip : skip + size]
+            copies.append(pltpu.make_async_copy(tile.at[:, there], out_hbm.at[:, there], sems.at[len(copies)]))
+            copies[-1].start()
     for copy in copies:
         copy.wait()
 
 
-def project(coeffs, sources, image, pieces, cells):
-    count = len(sources)
-    width = sources[0].shape[1]
+def project(coeffs, inner, edges, cells):
     rows, depth = coeffs.shape
-    extra = [] if image is None else [image]
     return pl.pallas_call(
-        functools.partial(project_kernel, count, pieces),
+        functools.partial(project_kernel, len(edges)),
+        name="project",
         out_shape=jax.ShapeDtypeStruct((rows, cells), jnp.bfloat16),
-        in_specs=[VMEM] * (1 + count) + [HBM] * len(extra),
+        in_specs=[VMEM] * (1 + len(inner) + len(edges)),
         out_specs=HBM,
-        input_output_aliases={1 + count: 0} if extra else {},
         scratch_shapes=[
-            pltpu.VMEM((rows, width), jnp.bfloat16),
-            pltpu.SemaphoreType.DMA((sum(-(-piece[2] // 256) for piece in pieces),)),
+            pltpu.VMEM((rows, cells), jnp.bfloat16),
+            pltpu.SemaphoreType.DMA(((cells - 2 * LANES) // 256 + 2,)),
         ],
-        compiler_params=grant(10 + 2 * depth // 1024),
-        cost_estimate=pl.CostEstimate(flops=2 * rows * width * depth, bytes_accessed=3000000, transcendentals=0),
-    )(coeffs, *sources, *extra)
+        compiler_params=grant(10 + 8 * depth // 1024),
+        cost_estimate=pl.CostEstimate(flops=2 * rows * cells * depth, bytes_accessed=3000000, transcendentals=0),
+    )(coeffs, *inner, *edges)
 
 
 def body(echoes, shifts, tap_weights, angles, slopes, steering, footprint, tile_coeffs):
@@ -339,15 +336,16 @@
 
     x4 = echoes.reshape(pulses, 2, blocks, LANES).transpose(0, 2, 1, 3)
     shared = (jnp.reshape(start_cell, (1,)), x4.reshape(pulses, 2 * blocks, LANES))
-    small = (shifts, shifts[None, :], tap_weights.T, angles[None, :], slopes[None, :], steering)
-    inner_a, partial = make_inner(0, *shared, small)
-    inner_b, below, above, own = make_inner(1, *shared, small, partial)
+    small = (shifts[None, :], tap_weights.T, angles[None, :], slopes[None, :], steering)
+    inner_a, part_a = make_inner(0, *shared, small, shifts)
+    inner_b, part_b = make_inner(1, *shared, small, shifts)
     inner = [inner_a, inner_b]
+    below, above = join(part_a, part_b)
     ring = [(i, (i + 1) % range_count) for i in range(range_count)]
     left = lax.ppermute(above, "range", ring)
     right = lax.ppermute(below, "range", [(target, source) for source, target in ring])
     place = jnp.reshape(lax.axis_index("range"), (1,))
-    edges = seal(range_count - 1, place, own, left, right)
+    edges = seal(range_count - 1, place, part_a, part_b, left, right)
 
     entries = TILE_DEV * FOOT
     chips = pulse_count // 2
@@ -378,10 +376,7 @@
 
     spread_inner = [spread(own) for own in inner]
     spread_edges = spread(edges)
-    width = cells - 2 * LANES
-    image = project(coeffs, sum(spread_inner, []), None, ((0, LANES, width),), cells)
-    pieces = ((0, 0, LANES), (LANES, cells - LANES, LANES))
-    image = project(coeffs, spread_edges, image, pieces, cells)
+    image = project(coeffs, sum(spread_inner, []), spread_edges, cells)
     return image.reshape(TILE_DEV, 2, AZ, cells)
 
 

time: 33.8 us -> 33.6 us (level)
  local copies, waits for them, and re-layouts: 2.05 us -> 7.06 us
  Pallas kernels: 13.8 us -> 10.4 us
  waiting for transfers between devices: 6.75 us -> 5.15 us
    unnamed x10 -> x20, local copies, waits for them, and re-layouts: 1.85 us -> 6.86 us
    pallas_call x4, Pallas kernels: 13.3 us -> 9.94 us  [the longest x2 7.66 us: make_inner(): pl.pallas_call(functools.partial(inner_kernel, group), out_shape=(jax.Sha...]
    ppermute x1, waiting for transfers between devices: 1.45 us -> 0.04 us  [body(): lax.ppermute(below, 'range', [(target, source) for source, target in ring])]
    ppermute x1, waiting for transfers between devices: 3.53 us -> 2.13 us  [body(): left = lax.ppermute(above, 'range', ring)]
    ppermute x6, waiting for transfers between devices: 0.02 us -> 0.85 us  [spread(): sources += [ahead, lax.ppermute(ahead, 'pulse', swap)]]
    ppermute x3, waiting for transfers between devices: 1.76 us -> 2.13 us  [spread(): lax.ppermute(own, 'pulse', [(i, (i + 2 * hop) % pulse_count) for i in ran...]
  transfers between devices with their start and end apart: 11 -> 11, of which waited for: 3 -> 4; matrix products, arithmetic and copies ran while one was open for 1% -> 1% of each run, Pallas kernels for 24% -> 15%
where the time goes in v4:
time: 33.6 us; the launch traced here: 33.3 us
  Pallas kernels  10.4 us (31%)
  starting transfers between devices  10.2 us (30%)
  local copies, waits for them, and re-layouts  7.06 us (21%)
  waiting for transfers between devices  5.15 us (15%)
    pallas_call x2, Pallas kernels, make_inner(): pl.pallas_call(functools.partial(inner_kernel, group), out_shape=(jax.Sha...  7.66 us
    unnamed x20, local copies, waits for them, and re-layouts  6.86 us
    ppermute x3, starting transfers between devices, spread(): lax.ppermute(own, 'pulse', [(i, (i + 2 * hop) % pulse_count) for i in ran...  4.73 us
    pallas_call x1, Pallas kernels, project(): pl.pallas_call(functools.partial(project_kernel, len(edges)), name='proje...  2.27 us
    ppermute x1, starting transfers between devices, body(): left = lax.ppermute(above, 'range', ring)  2.15 us
    ppermute x1, waiting for transfers between devices, body(): left = lax.ppermute(above, 'range', ring)  2.13 us
    ppermute x3, waiting for transfers between devices, spread(): lax.ppermute(own, 'pulse', [(i, (i + 2 * hop) % pulse_count) for i in ran...  2.13 us
    ppermute x1, starting transfers between devices, body(): lax.ppermute(below, 'range', [(target, source) for source, target in ring])  2.09 us
  transfers between devices with their start and end apart: 11, of which 4 were waited for; matrix products, arithmetic and copies ran while one was open for 1% of the time, Pallas kernels for 15%

profile of v4, /device:TPU:0, one launch (start us, length us, event | category | flops | bytes accessed | tf_op | source)
XLA Modules:
  0.0 33.3 jit_solution(1893519713099652204)
XLA Ops:
  0.0 0.0 copy-start.3
  0.0 1.6 %copy-done.3 = bf16[256,2,2048]{2,1,0:T(2,128)(2,1)S(1)} copy-done((bf16[256,2,2048]{2,1,0:T(2,128)(2,1)S(1)}, bf16[256,2,2048]{2,1,0:T(2,128)(2,1)}, u32[]{:S(2)}) %copy-start.3) | copy-done | bytes 2097176
  1.6 0.0 copy-start.4
  1.6 0.7 %copy-done.4 = f32[256,8]{0,1:T(8,128)S(1)} copy-done((f32[256,8]{0,1:T(8,128)S(1)}, f32[256,8]{0,1:T(8,128)}, u32[]{:S(2)}) %copy-start.4) | copy-done | bytes 8216
  2.3 0.0 copy-start.5
  2.3 0.7 %copy-done.5 = bf16[2,8,32]{2,1,0:T(8,128)(2,1)S(1)} copy-done((bf16[2,8,32]{2,1,0:T(8,128)(2,1)S(1)}, bf16[2,8,32]{2,1,0:T(8,128)(2,1)}, u32[]{:S(2)}) %copy-start.5) | copy-done | bytes 1048
  3.0 0.0 copy-start.6
  3.0 0.7 %copy-done.6 = s32[256]{0:T(256)S(1)} copy-done((s32[256]{0:T(256)S(1)}, s32[256]{0:T(256)}, u32[]{:S(2)}) %copy-start.6) | copy-done | bytes 1048
  3.7 0.0 copy-start.7
  3.7 0.7 %copy-done.7 = f32[256]{0:T(256)S(1)} copy-done((f32[256]{0:T(256)S(1)}, f32[256]{0:T(256)}, u32[]{:S(2)}) %copy-start.7) | copy-done | bytes 1048
  4.3 0.0 copy-start.8
  4.3 0.7 %copy-done.8 = f32[256]{0:T(256)S(1)} copy-done((f32[256]{0:T(256)S(1)}, f32[256]{0:T(256)}, u32[]{:S(2)}) %copy-start.8) | copy-done | bytes 1048
  5.0 3.1 %shard_map.83 = (bf16[64,1792]{1,0:T(8,128)(2,1)S(1)}, f32[64,512]{1,0:T(8,128)S(1)}) custom-call(s32[1]{0:T(128)} %bitcast.2.start_ref, bf16[256,32,128]{2,1,0:T(8,128)(2,1)S(1)} %bitcast.17, s32[1,256]{1,0:T(1,128)S(1)} %bitcast.21, f32[8,256]{1,0:T(8,128)S(1)} %bitcast.19, f32[1,256]{1,0:T(1,128)S(1)} %bitcast.23, f32[1,256]{1,0:T(1,128)S(1)} %bitcast.25, ...), custom_call_target="tpu_custom_call" | custom-call | flops 2000000000 | bytes 4000000 | tf_op jit(solution)/shard_map/pallas_call | solution.py:225
  8.1 0.0 copy-start.9
  8.1 0.0 copy-start.2
  8.2 3.0 %collective-permute-start.4 = (bf16[64,1792]{1,0:T(8,128)(2,1)S(1)}, bf16[64,1792]{1,0:T(8,128)(2,1)S(1)}, u32[]{:S(2)}, u32[]{:S(2)}) collective-permute-start(bf16[64,1792]{1,0:T(8,128)(2,1)S(1)} %get-tuple-element.12.refs_4_), channel_id=1, source_target_pairs={{0,8},{4,12},{8,0},{12,4},{1,9},{5,13},{9,1},{13,5},{2,10},{6,14},... | collective-permute-start | bytes 688136 | tf_op jit(solution)/shard_map/ppermute | solution.py:373
  11.2 4.6 %shard_map.82 = (bf16[64,1792]{1,0:T(8,128)(2,1)}, f32[64,512]{1,0:T(8,128)}) custom-call(s32[1]{0:T(128)} %bitcast.2.start_ref, bf16[256,32,128]{2,1,0:T(8,128)(2,1)} %bitcast.16, s32[1,256]{1,0:T(1,128)} %bitcast.20, f32[8,256]{1,0:T(8,128)} %bitcast.18, f32[1,256]{1,0:T(1,128)} %bitcast.22, f32[1,256]{1,0:T(1,128)} %bitcast.24, ...), custom_call_target="tpu_custom_call" | custom-call | flops 2000000000 | bytes 4000000 | tf_op jit(solution)/shard_map/pallas_call | solution.py:225
  15.7 0.1 collective-permute-start.1
  15.8 0.0 copy-start
  15.8 0.9 %copy-done = f32[64,512]{1,0:T(8,128)S(1)} copy-done((f32[64,512]{1,0:T(8,128)S(1)}, f32[64,512]{1,0:T(8,128)}, u32[]{:S(2)}) %copy-start) | copy-done | bytes 131096
  16.7 2.1 %collective-permute-start.6 = (bf16[128,128]{1,0:T(8,128)(2,1)S(1)}, bf16[128,128]{1,0:T(8,128)(2,1)S(1)}, u32[]{:S(2)}, u32[]{:S(2)}) collective-permute-start(bf16[128,128]{1,0:T(8,128)(2,1)S(1)} %get-tuple-element.15), channel_id=1, source_target_pairs={{0,1},{1,2},{2,3},{3,0},{4,5},{5,6},{6,7},{7,4},{8,9},{9,10},{10,1... | collective-permute-start | bytes 98312 | tf_op jit(solution)/shard_map/ppermute | solution.py:345
  18.9 2.1 %collective-permute-start.7 = (bf16[128,128]{1,0:T(8,128)(2,1)S(1)}, bf16[128,128]{1,0:T(8,128)(2,1)S(1)}, u32[]{:S(2)}, u32[]{:S(2)}) collective-permute-start(bf16[128,128]{1,0:T(8,128)(2,1)S(1)} %get-tuple-element.16), channel_id=1, source_target_pairs={{1,0},{2,1},{3,2},{0,3},{5,4},{6,5},{7,6},{4,7},{9,8},{10,9},{11,1... | collective-permute-start | bytes 98312 | tf_op jit(solution)/shard_map/ppermute | solution.py:346
  21.0 2.1 %collective-permute-done.6.left_ref = bf16[128,128]{1,0:T(8,128)(2,1)S(1)} collective-permute-done((bf16[128,128]{1,0:T(8,128)(2,1)S(1)}, bf16[128,128]{1,0:T(8,128)(2,1)S(1)}, u32[]{:S(2)}, u32[]{:S(2)}) %collective-permute-start.6) | collective-permute-done | bytes 32800 | tf_op jit(solution)/shard_map/ppermute | solution.py:345
  23.1 0.0 collective-permute-done.7.right_ref
  23.2 1.6 %collective-permute-start.9 = (bf16[128,256]{1,0:T(8,128)(2,1)S(1)}, bf16[128,256]{1,0:T(8,128)(2,1)S(1)}, u32[]{:S(2)}, u32[]{:S(2)}) collective-permute-start(bf16[128,256]{1,0:T(8,128)(2,1)S(1)} %seal.1.refs_8_), channel_id=1, source_target_pairs={{0,8},{4,12},{8,0},{12,4},{1,9},{5,13},{9,1},{13,5},{2,10},{6,14},... | collective-permute-start | bytes 196616 | tf_op jit(solution)/shard_map/ppermute | solution.py:373
  24.8 0.0 collective-permute-start.3
  24.8 0.5 %collective-permute-start = (bf16[64,1792]{1,0:T(8,128)(2,1)}, bf16[64,1792]{1,0:T(8,128)(2,1)S(1)}, u32[]{:S(2)}, u32[]{:S(2)}) collective-permute-start(bf16[64,1792]{1,0:T(8,128)(2,1)} %get-tuple-element.11.refs_0_), channel_id=1, source_target_pairs={{0,4},{4,0},{8,12},{12,8},{1,5},{5,1},{9,13},{13,9},{2,6},{6,2},{1... | collective-permute-start | bytes 688136 | tf_op jit(solution)/shard_map/ppermute | solution.py:374
  25.3 0.0 copy-done.9
  25.3 0.1 reshape.401
  25.4 2.1 %collective-permute-done.9.refs_10_ = bf16[128,256]{1,0:T(8,128)(2,1)S(1)} collective-permute-done((bf16[128,256]{1,0:T(8,128)(2,1)S(1)}, bf16[128,256]{1,0:T(8,128)(2,1)S(1)}, u32[]{:S(2)}, u32[]{:S(2)}) %collective-permute-start.9) | collective-permute-done | bytes 65568 | tf_op jit(solution)/shard_map/ppermute | solution.py:373
  27.5 0.0 collective-permute-start.8
  27.5 0.0 collective-permute-done.4.refs_6_
  27.5 0.5 %collective-permute-start.5 = (bf16[64,1792]{1,0:T(8,128)(2,1)S(1)}, bf16[64,1792]{1,0:T(8,128)(2,1)S(1)}, u32[]{:S(2)}, u32[]{:S(2)}) collective-permute-start(bf16[64,1792]{1,0:T(8,128)(2,1)S(1)} %collective-permute-done.4.refs_6_), channel_id=1, source_target_pairs={{0,4},{4,0},{8,12},{12,8},{1,5},{5,1},{9,13},{13,9},{2,6},{6,2},{1... | collective-permute-start | bytes 688136 | tf_op jit(solution)/shard_map/ppermute | solution.py:374
  28.0 0.0 collective-permute-done.1.refs_2_
  28.0 0.1 collective-permute-start.2
  28.1 0.1 copy.9
  28.2 0.5 %collective-permute-done.8.refs_9_ = bf16[128,256]{1,0:T(8,128)(2,1)S(1)} collective-permute-done((bf16[128,256]{1,0:T(8,128)(2,1)S(1)}, bf16[128,256]{1,0:T(8,128)(2,1)S(1)}, u32[]{:S(2)}, u32[]{:S(2)}) %collective-permute-start.8) | collective-permute-done | bytes 65568 | tf_op jit(solution)/shard_map/ppermute | solution.py:374
  28.8 0.2 collective-permute-start.10
  28.9 0.3 fusion.7.where_ref
  29.2 0.0 copy-done.2
  29.2 0.5 %expand.1.coeff_ref = bf16[512,512]{1,0:T(8,128)(2,1)S(1)} custom-call(s32[128,1]{1,0:T(8,128)S(1)} %fusion.7.where_ref, bf16[4,2,32,64]{3,2,1,0:T(8,128)(2,1)S(1)} %bitcast.15), custom_call_target="tpu_custom_call" | custom-call | tf_op jit(solution)/shard_map/expand/pallas_call | solution.py:359
  29.7 0.3 collective-permute-done.10.refs_11_
  30.0 0.0 collective-permute-done.3.refs_5_
  30.0 0.0 collective-permute-done.refs_1_
  30.0 0.0 collective-permute-done.5.refs_7_
  30.0 0.0 collective-permute-done.2.refs_3_
  30.1 0.0 copy-start.1
  30.1 0.9 %copy-done.1 = bf16[64,1792]{1,0:T(8,128)(2,1)S(1)} copy-done((bf16[64,1792]{1,0:T(8,128)(2,1)S(1)}, bf16[64,1792]{1,0:T(8,128)(2,1)}, u32[]{:S(2)}) %copy-start.1) | copy-done | bytes 229400
  31.0 2.3 %project.1 = bf16[512,2048]{1,0:T(8,128)(2,1)} custom-call(bf16[512,512]{1,0:T(8,128)(2,1)S(1)} %expand.1.coeff_ref, bf16[64,1792]{1,0:T(8,128)(2,1)S(1)} %copy-done.1, bf16[64,1792]{1,0:T(8,128)(2,1)S(1)} %collective-permute-done.refs_1_, bf16[64,1792]{1,0:T(8,128)(2,1)S(1)} %collective-permute-done.1.refs_2_, ...), custom_call_target="tpu_custom_call" | custom-call | flops 1073741824 | bytes 3000000 | tf_op jit(solution)/shard_map/project/pallas_call | solution.py:314
  (3 shorter events, 0.0 us)
Async XLA Ops:
  0.0 1.6 %copy-start.3 = (bf16[256,2,2048]{2,1,0:T(2,128)(2,1)S(1)}, bf16[256,2,2048]{2,1,0:T(2,128)(2,1)}, u32[]{:S(2)}) copy-start(bf16[256,2,2048]{2,1,0:T(2,128)(2,1)} %param.8) | copy-start | bytes 6291460
  1.6 0.7 %copy-start.4 = (f32[256,8]{0,1:T(8,128)S(1)}, f32[256,8]{0,1:T(8,128)}, u32[]{:S(2)}) copy-start(f32[256,8]{0,1:T(8,128)} %param.10) | copy-start | bytes 24580
  2.3 0.7 %copy-start.5 = (bf16[2,8,32]{2,1,0:T(8,128)(2,1)S(1)}, bf16[2,8,32]{2,1,0:T(8,128)(2,1)}, u32[]{:S(2)}) copy-start(bf16[2,8,32]{2,1,0:T(8,128)(2,1)} %refs_5_.3) | copy-start | bytes 3076
  3.0 0.7 %copy-start.6 = (s32[256]{0:T(256)S(1)}, s32[256]{0:T(256)}, u32[]{:S(2)}) copy-start(s32[256]{0:T(256)} %refs_6_.3) | copy-start | bytes 3076
  3.7 0.7 %copy-start.7 = (f32[256]{0:T(256)S(1)}, f32[256]{0:T(256)}, u32[]{:S(2)}) copy-start(f32[256]{0:T(256)} %param.11) | copy-start | bytes 3076
  4.3 0.7 %copy-start.8 = (f32[256]{0:T(256)S(1)}, f32[256]{0:T(256)}, u32[]{:S(2)}) copy-start(f32[256]{0:T(256)} %param.12) | copy-start | bytes 3076
  8.1 17.2 %copy-start.9 = (s32[16,32]{1,0:T(8,128)S(1)}, s32[16,32]{1,0:T(8,128)}, u32[]{:S(2)}) copy-start(s32[16,32]{1,0:T(8,128)} %param.14) | copy-start | bytes 6148
  8.1 21.1 %copy-start.2 = (bf16[4,2,64,32]{2,3,1,0:T(8,128)(2,1)S(1)}, bf16[4,2,64,32]{2,3,1,0:T(8,128)(2,1)}, u32[]{:S(2)}) copy-start(bf16[4,2,64,32]{2,3,1,0:T(8,128)(2,1)} %param.15) | copy-start | bytes 98308
  8.2 19.4 %collective-permute-start.4 = (bf16[64,1792]{1,0:T(8,128)(2,1)S(1)}, bf16[64,1792]{1,0:T(8,128)(2,1)S(1)}, u32[]{:S(2)}, u32[]{:S(2)}) collective-permute-start(bf16[64,1792]{1,0:T(8,128)(2,1)S(1)} %get-tuple-element.12.refs_4_), channel_id=1, source_target_pairs={{0,8},{4,12},{8,0},{12,4},{1,9},{5,13},{9,1},{13,5},{2,10},{6,14},... | collective-permute-start | bytes 688136 | tf_op jit(solution)/shard_map/ppermute | solution.py:373
  15.7 12.3 %collective-permute-start.1 = (bf16[64,1792]{1,0:T(8,128)(2,1)}, bf16[64,1792]{1,0:T(8,128)(2,1)S(1)}, u32[]{:S(2)}, u32[]{:S(2)}) collective-permute-start(bf16[64,1792]{1,0:T(8,128)(2,1)} %get-tuple-element.11.refs_0_), channel_id=1, source_target_pairs={{0,8},{4,12},{8,0},{12,4},{1,9},{5,13},{9,1},{13,5},{2,10},{6,14},... | collective-permute-start | bytes 688136 | tf_op jit(solution)/shard_map/ppermute | solution.py:373
  15.8 0.9 %copy-start = (f32[64,512]{1,0:T(8,128)S(1)}, f32[64,512]{1,0:T(8,128)}, u32[]{:S(2)}) copy-start(f32[64,512]{1,0:T(8,128)} %get-tuple-element.13.a_ref) | copy-start | bytes 393220
  16.7 6.4 %collective-permute-start.6 = (bf16[128,128]{1,0:T(8,128)(2,1)S(1)}, bf16[128,128]{1,0:T(8,128)(2,1)S(1)}, u32[]{:S(2)}, u32[]{:S(2)}) collective-permute-start(bf16[128,128]{1,0:T(8,128)(2,1)S(1)} %get-tuple-element.15), channel_id=1, source_target_pairs={{0,1},{1,2},{2,3},{3,0},{4,5},{5,6},{6,7},{7,4},{8,9},{9,10},{10,1... | collective-permute-start | bytes 98312 | tf_op jit(solution)/shard_map/ppermute | solution.py:345
  18.9 4.3 %collective-permute-start.7 = (bf16[128,128]{1,0:T(8,128)(2,1)S(1)}, bf16[128,128]{1,0:T(8,128)(2,1)S(1)}, u32[]{:S(2)}, u32[]{:S(2)}) collective-permute-start(bf16[128,128]{1,0:T(8,128)(2,1)S(1)} %get-tuple-element.16), channel_id=1, source_target_pairs={{1,0},{2,1},{3,2},{0,3},{5,4},{6,5},{7,6},{4,7},{9,8},{10,9},{11,1... | collective-permute-start | bytes 98312 | tf_op jit(solution)/shard_map/ppermute | solution.py:346
  23.2 4.3 %collective-permute-start.9 = (bf16[128,256]{1,0:T(8,128)(2,1)S(1)}, bf16[128,256]{1,0:T(8,128)(2,1)S(1)}, u32[]{:S(2)}, u32[]{:S(2)}) collective-permute-start(bf16[128,256]{1,0:T(8,128)(2,1)S(1)} %seal.1.refs_8_), channel_id=1, source_target_pairs={{0,8},{4,12},{8,0},{12,4},{1,9},{5,13},{9,1},{13,5},{2,10},{6,14},... | collective-permute-start | bytes 196616 | tf_op jit(solution)/shard_map/ppermute | solution.py:373
  24.8 5.2 %collective-permute-start.3 = (bf16[64,1792]{1,0:T(8,128)(2,1)S(1)}, bf16[64,1792]{1,0:T(8,128)(2,1)S(1)}, u32[]{:S(2)}, u32[]{:S(2)}) collective-permute-start(bf16[64,1792]{1,0:T(8,128)(2,1)S(1)} %get-tuple-element.12.refs_4_), channel_id=1, source_target_pairs={{0,4},{4,0},{8,12},{12,8},{1,5},{5,1},{9,13},{13,9},{2,6},{6,2},{1... | collective-permute-start | bytes 688136 | tf_op jit(solution)/shard_map/ppermute | solution.py:374
  24.8 5.2 %collective-permute-start = (bf16[64,1792]{1,0:T(8,128)(2,1)}, bf16[64,1792]{1,0:T(8,128)(2,1)S(1)}, u32[]{:S(2)}, u32[]{:S(2)}) collective-permute-start(bf16[64,1792]{1,0:T(8,128)(2,1)} %get-tuple-element.11.refs_0_), channel_id=1, source_target_pairs={{0,4},{4,0},{8,12},{12,8},{1,5},{5,1},{9,13},{13,9},{2,6},{6,2},{1... | collective-permute-start | bytes 688136 | tf_op jit(solution)/shard_map/ppermute | solution.py:374
  27.5 1.3 %collective-permute-start.8 = (bf16[128,256]{1,0:T(8,128)(2,1)S(1)}, bf16[128,256]{1,0:T(8,128)(2,1)S(1)}, u32[]{:S(2)}, u32[]{:S(2)}) collective-permute-start(bf16[128,256]{1,0:T(8,128)(2,1)S(1)} %seal.1.refs_8_), channel_id=1, source_target_pairs={{0,4},{4,0},{8,12},{12,8},{1,5},{5,1},{9,13},{13,9},{2,6},{6,2},{1... | collective-permute-start | bytes 196616 | tf_op jit(solution)/shard_map/ppermute | solution.py:374
  27.5 2.5 %collective-permute-start.5 = (bf16[64,1792]{1,0:T(8,128)(2,1)S(1)}, bf16[64,1792]{1,0:T(8,128)(2,1)S(1)}, u32[]{:S(2)}, u32[]{:S(2)}) collective-permute-start(bf16[64,1792]{1,0:T(8,128)(2,1)S(1)} %collective-permute-done.4.refs_6_), channel_id=1, source_target_pairs={{0,4},{4,0},{8,12},{12,8},{1,5},{5,1},{9,13},{13,9},{2,6},{6,2},{1... | collective-permute-start | bytes 688136 | tf_op jit(solution)/shard_map/ppermute | solution.py:374
  28.0 2.0 %collective-permute-start.2 = (bf16[64,1792]{1,0:T(8,128)(2,1)S(1)}, bf16[64,1792]{1,0:T(8,128)(2,1)S(1)}, u32[]{:S(2)}, u32[]{:S(2)}) collective-permute-start(bf16[64,1792]{1,0:T(8,128)(2,1)S(1)} %collective-permute-done.1.refs_2_), channel_id=1, source_target_pairs={{0,4},{4,0},{8,12},{12,8},{1,5},{5,1},{9,13},{13,9},{2,6},{6,2},{1... | collective-permute-start | bytes 688136 | tf_op jit(solution)/shard_map/ppermute | solution.py:374
  28.8 1.3 %collective-permute-start.10 = (bf16[128,256]{1,0:T(8,128)(2,1)S(1)}, bf16[128,256]{1,0:T(8,128)(2,1)S(1)}, u32[]{:S(2)}, u32[]{:S(2)}) collective-permute-start(bf16[128,256]{1,0:T(8,128)(2,1)S(1)} %collective-permute-done.9.refs_10_), channel_id=1, source_target_pairs={{0,4},{4,0},{8,12},{12,8},{1,5},{5,1},{9,13},{13,9},{2,6},{6,2},{1... | collective-permute-start | bytes 196616 | tf_op jit(solution)/shard_map/ppermute | solution.py:374
  30.1 0.9 %copy-start.1 = (bf16[64,1792]{1,0:T(8,128)(2,1)S(1)}, bf16[64,1792]{1,0:T(8,128)(2,1)}, u32[]{:S(2)}) copy-start(bf16[64,1792]{1,0:T(8,128)(2,1)} %get-tuple-element.11.refs_0_) | copy-start | bytes 688132

commit v5 on v4

--- a/solution.py
+++ b/solution.py
@@ -51,7 +51,7 @@
     return taps * cosine, taps * sine
 
 
-def fill_weights(factors, steer_ref, weight_ref):
+def fill_weights(factors, steer_ref, weight_ref, per_row):
     lane = lax.broadcasted_iota(jnp.int32, (8, LANES), 1)
     steer = tuple(
         jnp.concatenate([steer_ref[part].astype(jnp.float32)] * (GROUP // SUB), axis=1) for part in range(2)
@@ -64,9 +64,9 @@
             p_im = jnp.where(keep, w_im, 0.0)
             top = jnp.concatenate([p_re, 0.0 - p_im], axis=1)
             bottom = jnp.concatenate([p_im, p_re], axis=1)
-            weight_ref[pl.ds(tap * 64 + sub * 16, 16), :] = jnp.concatenate([top, bottom], axis=0).astype(
-                jnp.bfloat16
-            )
+            column = tap % per_row * 2 * GROUP
+            spot = pl.ds(tap // per_row * 64 + sub * 16, 16), pl.ds(column, 2 * GROUP)
+            weight_ref[spot] = jnp.concatenate([top, bottom], axis=0).astype(jnp.bfloat16)
 
 
 def place_of(shift_ref, pulse, local):
@@ -133,6 +133,60 @@
                 store(row, last + 1, total)
 
 
+def sweep_pairs(last, aligned, offset, phase, step, weight_ref, demod, products, carry, store):
+    lane = lax.broadcasted_iota(jnp.int32, (8, LANES), 1)
+    wide = lax.broadcasted_iota(jnp.int32, (2 * GROUP, LANES), 1)
+    ends = split_ends(aligned, offset, last)
+    pairs = TAPS // 2
+
+    def mixed(before, turned):
+        total = before[0]
+        for pair in range(1, pairs):
+            later = turned[pair] if turned else 0.0
+            total = total + jnp.where(lane < LANES - 2 * pair, before[pair], later)
+        return total
+
+    held = None
+    for block in range(-1, last + 3):
+        if block > last + 1:
+            data = jnp.zeros((2 * GROUP, LANES), jnp.float32)
+        else:
+            if block in ends:
+                data = ends[block](0), ends[block](1)
+            else:
+                at = 2 * block * STRIDE
+                data = aligned[pl.ds(at, GROUP), :], aligned[pl.ds(at + STRIDE, GROUP), :]
+            data = jnp.concatenate(turn_by(data, phase), axis=0)
+            phase = turn_by(phase, step)
+            demod[0 : 2 * GROUP, pl.ds((block + 1) * LANES, LANES)] = data.astype(jnp.bfloat16)
+        if held is not None:
+            further = pltpu.roll(jnp.where(wide >= 1, held, data).astype(jnp.bfloat16), LANES - 1, 1)
+            demod[2 * GROUP : 4 * GROUP, pl.ds(block * LANES, LANES)] = further
+        held = data
+        start = block - 2
+        if start < -1 or start % 2 == 0:
+            continue
+        here = pl.ds((start + 1) * LANES, 2 * LANES)
+        products[:, here] = jnp.dot(weight_ref[...], demod[:, here], preferred_element_type=jnp.float32)
+        for row in range(0, 64, 8):
+            before = None
+            if start >= 0:
+                before = [carry[pl.ds(pair * 64 + row, 8), :] for pair in range(pairs)]
+            for tile in (start, start + 1):
+                turned = []
+                for pair in range(pairs):
+                    piece = products[pl.ds(pair * 64 + row, 8), pl.ds((tile + 1) * LANES, LANES)]
+                    turned.append(pltpu.roll(piece, LANES - 2 * pair, 1) if pair else piece)
+                if before is not None:
+                    store(row, tile - 1, mixed(before, turned))
+                before = turned
+            if start + 2 < last + 2:
+                for pair in range(pairs):
+                    carry[pl.ds(pair * 64 + row, 8), :] = before[pair]
+            else:
+                store(row, last + 1, mixed(before, None))
+
+
 def fetch_small(sources, targets, sems):
     copies = [pltpu.make_async_copy(s, t, sems.at[i]) for i, (s, t) in enumerate(zip(sources, targets))]
     for copy in copies:
@@ -163,7 +217,7 @@
     here = slice(first_pulse, first_pulse + GROUP)
     slope, angle = slope_ref[:, here], angle_ref[:, here]
     phase, step = lane_phases(slope)
-    fill_weights(tap_factors(start_ref, tap_ref, angle, slope, here), steer_ref, weights)
+    fill_weights(tap_factors(start_ref, tap_ref, angle, slope, here), steer_ref, weights, 1 if group else 2)
     offset = jnp.broadcast_to((row_ref[:, here] - 3).astype(jnp.float32), (GROUP, GROUP)).T.astype(jnp.int32)
     lane = lax.broadcasted_iota(jnp.int32, (rows, LANES), 1)
     for local in range(GROUP):
@@ -183,7 +237,8 @@
         else:
             partial_ref[pl.ds(row, 8), pl.ds(edges.index(block) * LANES, LANES)] = total
 
-    sweep(last, aligned, offset, phase, step, weights, demod, products, carry, store)
+    run = sweep if group else sweep_pairs
+    run(last, aligned, offset, phase, step, weights, demod, products, carry, store)
 
 
 def join_kernel(a_ref, b_ref, below_ref, above_ref):
@@ -213,6 +268,7 @@
 def make_inner(group, start, x3, small, shifts):
     _, rows, _ = x3.shape
     width = (rows // 2 + 2) * LANES
+    per_row = 1 if group else 2
     fetched = []
     if not group:
         fetched = [pltpu.VMEM(item.shape, item.dtype) for item in small] + [
@@ -233,10 +289,10 @@
         scratch_shapes=fetched
         + [
             pltpu.VMEM(((rows + 2) * STRIDE, LANES), jnp.float32),
-            pltpu.VMEM((64 * TAPS, 2 * GROUP), jnp.bfloat16),
-            pltpu.VMEM((2 * GROUP, width), jnp.bfloat16),
-            pltpu.VMEM((64 * TAPS, width), jnp.float32),
-            pltpu.VMEM((64 * TAPS, LANES), jnp.float32),
+            pltpu.VMEM((64 * TAPS // per_row, 2 * GROUP * per_row), jnp.bfloat16),
+            pltpu.VMEM((2 * GROUP * per_row, width), jnp.bfloat16),
+            pltpu.VMEM((64 * TAPS // per_row, width), jnp.float32),
+            pltpu.VMEM((64 * TAPS // per_row, LANES), jnp.float32),
         ],
         compiler_params=grant(GRANTS[group]),
         cost_estimate=pl.CostEstimate(flops=2000000000, bytes_accessed=4000000, transcendentals=0),

time: 33.6 us -> 33.4 us (level)
  no operation moved by 1% of the time
where the time goes in v5:
time: 33.4 us; the launch traced here: 33.1 us
  Pallas kernels  10.2 us (31%)
  starting transfers between devices  10.2 us (31%)
  local copies, waits for them, and re-layouts  7.06 us (21%)
  waiting for transfers between devices  5.15 us (15%)
    pallas_call x2, Pallas kernels, make_inner(): pl.pallas_call(functools.partial(inner_kernel, group), out_shape=(jax.Sha...  7.44 us
    unnamed x20, local copies, waits for them, and re-layouts  6.86 us
    ppermute x3, starting transfers between devices, spread(): lax.ppermute(own, 'pulse', [(i, (i + 2 * hop) % pulse_count) for i in ran...  4.73 us
    pallas_call x1, Pallas kernels, project(): pl.pallas_call(functools.partial(project_kernel, len(edges)), name='proje...  2.27 us
    ppermute x1, starting transfers between devices, body(): left = lax.ppermute(above, 'range', ring)  2.14 us
    ppermute x3, waiting for transfers between devices, spread(): lax.ppermute(own, 'pulse', [(i, (i + 2 * hop) % pulse_count) for i in ran...  2.13 us
    ppermute x1, waiting for transfers between devices, body(): left = lax.ppermute(above, 'range', ring)  2.13 us
    ppermute x1, starting transfers between devices, body(): lax.ppermute(below, 'range', [(target, source) for source, target in ring])  2.09 us
  transfers between devices with their start and end apart: 11, of which 4 were waited for; matrix products, arithmetic and copies ran while one was open for 1% of the time, Pallas kernels for 15%

profile of v5, /device:TPU:0, one launch (start us, length us, event | category | flops | bytes accessed | tf_op | source)
XLA Modules:
  0.0 33.1 jit_solution(8490959121559941350)
XLA Ops:
  0.0 0.0 copy-start.3
  0.0 1.6 %copy-done.3 = bf16[256,2,2048]{2,1,0:T(2,128)(2,1)S(1)} copy-done((bf16[256,2,2048]{2,1,0:T(2,128)(2,1)S(1)}, bf16[256,2,2048]{2,1,0:T(2,128)(2,1)}, u32[]{:S(2)}) %copy-start.3) | copy-done | bytes 2097176
  1.6 0.0 copy-start.4
  1.6 0.7 %copy-done.4 = f32[256,8]{0,1:T(8,128)S(1)} copy-done((f32[256,8]{0,1:T(8,128)S(1)}, f32[256,8]{0,1:T(8,128)}, u32[]{:S(2)}) %copy-start.4) | copy-done | bytes 8216
  2.3 0.0 copy-start.5
  2.3 0.7 %copy-done.5 = bf16[2,8,32]{2,1,0:T(8,128)(2,1)S(1)} copy-done((bf16[2,8,32]{2,1,0:T(8,128)(2,1)S(1)}, bf16[2,8,32]{2,1,0:T(8,128)(2,1)}, u32[]{:S(2)}) %copy-start.5) | copy-done | bytes 1048
  3.0 0.0 copy-start.6
  3.0 0.7 %copy-done.6 = s32[256]{0:T(256)S(1)} copy-done((s32[256]{0:T(256)S(1)}, s32[256]{0:T(256)}, u32[]{:S(2)}) %copy-start.6) | copy-done | bytes 1048
  3.7 0.0 copy-start.7
  3.7 0.7 %copy-done.7 = f32[256]{0:T(256)S(1)} copy-done((f32[256]{0:T(256)S(1)}, f32[256]{0:T(256)}, u32[]{:S(2)}) %copy-start.7) | copy-done | bytes 1048
  4.3 0.0 copy-start.8
  4.3 0.7 %copy-done.8 = f32[256]{0:T(256)S(1)} copy-done((f32[256]{0:T(256)S(1)}, f32[256]{0:T(256)}, u32[]{:S(2)}) %copy-start.8) | copy-done | bytes 1048
  5.0 3.1 %shard_map.83 = (bf16[64,1792]{1,0:T(8,128)(2,1)S(1)}, f32[64,512]{1,0:T(8,128)S(1)}) custom-call(s32[1]{0:T(128)} %bitcast.2.start_ref, bf16[256,32,128]{2,1,0:T(8,128)(2,1)S(1)} %bitcast.17, s32[1,256]{1,0:T(1,128)S(1)} %bitcast.21, f32[8,256]{1,0:T(8,128)S(1)} %bitcast.19, f32[1,256]{1,0:T(1,128)S(1)} %bitcast.23, f32[1,256]{1,0:T(1,128)S(1)} %bitcast.25, ...), custom_call_target="tpu_custom_call" | custom-call | flops 2000000000 | bytes 4000000 | tf_op jit(solution)/shard_map/pallas_call | solution.py:281
  8.1 0.0 copy-start.9
  8.1 0.0 copy-start.2
  8.2 3.0 %collective-permute-start.4 = (bf16[64,1792]{1,0:T(8,128)(2,1)S(1)}, bf16[64,1792]{1,0:T(8,128)(2,1)S(1)}, u32[]{:S(2)}, u32[]{:S(2)}) collective-permute-start(bf16[64,1792]{1,0:T(8,128)(2,1)S(1)} %get-tuple-element.12.refs_4_), channel_id=1, source_target_pairs={{0,8},{4,12},{8,0},{12,4},{1,9},{5,13},{9,1},{13,5},{2,10},{6,14},... | collective-permute-start | bytes 688136 | tf_op jit(solution)/shard_map/ppermute | solution.py:429
  11.2 4.3 %shard_map.82 = (bf16[64,1792]{1,0:T(8,128)(2,1)}, f32[64,512]{1,0:T(8,128)}) custom-call(s32[1]{0:T(128)} %bitcast.2.start_ref, bf16[256,32,128]{2,1,0:T(8,128)(2,1)} %bitcast.16, s32[1,256]{1,0:T(1,128)} %bitcast.20, f32[8,256]{1,0:T(8,128)} %bitcast.18, f32[1,256]{1,0:T(1,128)} %bitcast.22, f32[1,256]{1,0:T(1,128)} %bitcast.24, ...), custom_call_target="tpu_custom_call" | custom-call | flops 2000000000 | bytes 4000000 | tf_op jit(solution)/shard_map/pallas_call | solution.py:281
  15.5 0.1 collective-permute-start.1
  15.6 0.0 copy-start
  15.6 0.9 %copy-done = f32[64,512]{1,0:T(8,128)S(1)} copy-done((f32[64,512]{1,0:T(8,128)S(1)}, f32[64,512]{1,0:T(8,128)}, u32[]{:S(2)}) %copy-start) | copy-done | bytes 131096
  16.5 2.1 %collective-permute-start.6 = (bf16[128,128]{1,0:T(8,128)(2,1)S(1)}, bf16[128,128]{1,0:T(8,128)(2,1)S(1)}, u32[]{:S(2)}, u32[]{:S(2)}) collective-permute-start(bf16[128,128]{1,0:T(8,128)(2,1)S(1)} %get-tuple-element.15), channel_id=1, source_target_pairs={{0,1},{1,2},{2,3},{3,0},{4,5},{5,6},{6,7},{7,4},{8,9},{9,10},{10,1... | collective-permute-start | bytes 98312 | tf_op jit(solution)/shard_map/ppermute | solution.py:401
  18.7 2.1 %collective-permute-start.7 = (bf16[128,128]{1,0:T(8,128)(2,1)S(1)}, bf16[128,128]{1,0:T(8,128)(2,1)S(1)}, u32[]{:S(2)}, u32[]{:S(2)}) collective-permute-start(bf16[128,128]{1,0:T(8,128)(2,1)S(1)} %get-tuple-element.16), channel_id=1, source_target_pairs={{1,0},{2,1},{3,2},{0,3},{5,4},{6,5},{7,6},{4,7},{9,8},{10,9},{11,1... | collective-permute-start | bytes 98312 | tf_op jit(solution)/shard_map/ppermute | solution.py:402
  20.8 2.1 %collective-permute-done.6.left_ref = bf16[128,128]{1,0:T(8,128)(2,1)S(1)} collective-permute-done((bf16[128,128]{1,0:T(8,128)(2,1)S(1)}, bf16[128,128]{1,0:T(8,128)(2,1)S(1)}, u32[]{:S(2)}, u32[]{:S(2)}) %collective-permute-start.6) | collective-permute-done | bytes 32800 | tf_op jit(solution)/shard_map/ppermute | solution.py:401
  22.9 0.0 collective-permute-done.7.right_ref
  23.0 1.6 %collective-permute-start.9 = (bf16[128,256]{1,0:T(8,128)(2,1)S(1)}, bf16[128,256]{1,0:T(8,128)(2,1)S(1)}, u32[]{:S(2)}, u32[]{:S(2)}) collective-permute-start(bf16[128,256]{1,0:T(8,128)(2,1)S(1)} %seal.1.refs_8_), channel_id=1, source_target_pairs={{0,8},{4,12},{8,0},{12,4},{1,9},{5,13},{9,1},{13,5},{2,10},{6,14},... | collective-permute-start | bytes 196616 | tf_op jit(solution)/shard_map/ppermute | solution.py:429
  24.6 0.0 collective-permute-start.3
  24.6 0.5 %collective-permute-start = (bf16[64,1792]{1,0:T(8,128)(2,1)}, bf16[64,1792]{1,0:T(8,128)(2,1)S(1)}, u32[]{:S(2)}, u32[]{:S(2)}) collective-permute-start(bf16[64,1792]{1,0:T(8,128)(2,1)} %get-tuple-element.11.refs_0_), channel_id=1, source_target_pairs={{0,4},{4,0},{8,12},{12,8},{1,5},{5,1},{9,13},{13,9},{2,6},{6,2},{1... | collective-permute-start | bytes 688136 | tf_op jit(solution)/shard_map/ppermute | solution.py:430
  25.1 0.0 copy-done.9
  25.1 0.1 reshape.401
  25.2 2.1 %collective-permute-done.9.refs_10_ = bf16[128,256]{1,0:T(8,128)(2,1)S(1)} collective-permute-done((bf16[128,256]{1,0:T(8,128)(2,1)S(1)}, bf16[128,256]{1,0:T(8,128)(2,1)S(1)}, u32[]{:S(2)}, u32[]{:S(2)}) %collective-permute-start.9) | collective-permute-done | bytes 65568 | tf_op jit(solution)/shard_map/ppermute | solution.py:429
  27.3 0.0 collective-permute-start.8
  27.3 0.0 collective-permute-done.4.refs_6_
  27.3 0.5 %collective-permute-start.5 = (bf16[64,1792]{1,0:T(8,128)(2,1)S(1)}, bf16[64,1792]{1,0:T(8,128)(2,1)S(1)}, u32[]{:S(2)}, u32[]{:S(2)}) collective-permute-start(bf16[64,1792]{1,0:T(8,128)(2,1)S(1)} %collective-permute-done.4.refs_6_), channel_id=1, source_target_pairs={{0,4},{4,0},{8,12},{12,8},{1,5},{5,1},{9,13},{13,9},{2,6},{6,2},{1... | collective-permute-start | bytes 688136 | tf_op jit(solution)/shard_map/ppermute | solution.py:430
  27.8 0.0 collective-permute-done.1.refs_2_
  27.8 0.1 collective-permute-start.2
  27.9 0.1 copy.9
  28.0 0.5 %collective-permute-done.8.refs_9_ = bf16[128,256]{1,0:T(8,128)(2,1)S(1)} collective-permute-done((bf16[128,256]{1,0:T(8,128)(2,1)S(1)}, bf16[128,256]{1,0:T(8,128)(2,1)S(1)}, u32[]{:S(2)}, u32[]{:S(2)}) %collective-permute-start.8) | collective-permute-done | bytes 65568 | tf_op jit(solution)/shard_map/ppermute | solution.py:430
  28.6 0.2 collective-permute-start.10
  28.7 0.3 fusion.7.where_ref
  29.0 0.0 copy-done.2
  29.0 0.5 %expand.1.coeff_ref = bf16[512,512]{1,0:T(8,128)(2,1)S(1)} custom-call(s32[128,1]{1,0:T(8,128)S(1)} %fusion.7.where_ref, bf16[4,2,32,64]{3,2,1,0:T(8,128)(2,1)S(1)} %bitcast.15), custom_call_target="tpu_custom_call" | custom-call | tf_op jit(solution)/shard_map/expand/pallas_call | solution.py:415
  29.5 0.3 collective-permute-done.10.refs_11_
  29.8 0.0 collective-permute-done.3.refs_5_
  29.8 0.0 collective-permute-done.refs_1_
  29.8 0.0 collective-permute-done.5.refs_7_
  29.8 0.0 collective-permute-done.2.refs_3_
  29.8 0.0 copy-start.1
  29.9 0.9 %copy-done.1 = bf16[64,1792]{1,0:T(8,128)(2,1)S(1)} copy-done((bf16[64,1792]{1,0:T(8,128)(2,1)S(1)}, bf16[64,1792]{1,0:T(8,128)(2,1)}, u32[]{:S(2)}) %copy-start.1) | copy-done | bytes 229400
  30.8 2.3 %project.1 = bf16[512,2048]{1,0:T(8,128)(2,1)} custom-call(bf16[512,512]{1,0:T(8,128)(2,1)S(1)} %expand.1.coeff_ref, bf16[64,1792]{1,0:T(8,128)(2,1)S(1)} %copy-done.1, bf16[64,1792]{1,0:T(8,128)(2,1)S(1)} %collective-permute-done.refs_1_, bf16[64,1792]{1,0:T(8,128)(2,1)S(1)} %collective-permute-done.1.refs_2_, ...), custom_call_target="tpu_custom_call" | custom-call | flops 1073741824 | bytes 3000000 | tf_op jit(solution)/shard_map/project/pallas_call | solution.py:370
  (3 shorter events, 0.0 us)
Async XLA Ops:
  0.0 1.6 %copy-start.3 = (bf16[256,2,2048]{2,1,0:T(2,128)(2,1)S(1)}, bf16[256,2,2048]{2,1,0:T(2,128)(2,1)}, u32[]{:S(2)}) copy-start(bf16[256,2,2048]{2,1,0:T(2,128)(2,1)} %param.8) | copy-start | bytes 6291460
  1.6 0.7 %copy-start.4 = (f32[256,8]{0,1:T(8,128)S(1)}, f32[256,8]{0,1:T(8,128)}, u32[]{:S(2)}) copy-start(f32[256,8]{0,1:T(8,128)} %param.10) | copy-start | bytes 24580
  2.3 0.7 %copy-start.5 = (bf16[2,8,32]{2,1,0:T(8,128)(2,1)S(1)}, bf16[2,8,32]{2,1,0:T(8,128)(2,1)}, u32[]{:S(2)}) copy-start(bf16[2,8,32]{2,1,0:T(8,128)(2,1)} %refs_5_.3) | copy-start | bytes 3076
  3.0 0.7 %copy-start.6 = (s32[256]{0:T(256)S(1)}, s32[256]{0:T(256)}, u32[]{:S(2)}) copy-start(s32[256]{0:T(256)} %refs_6_.3) | copy-start | bytes 3076
  3.7 0.7 %copy-start.7 = (f32[256]{0:T(256)S(1)}, f32[256]{0:T(256)}, u32[]{:S(2)}) copy-start(f32[256]{0:T(256)} %param.11) | copy-start | bytes 3076
  4.3 0.7 %copy-start.8 = (f32[256]{0:T(256)S(1)}, f32[256]{0:T(256)}, u32[]{:S(2)}) copy-start(f32[256]{0:T(256)} %param.12) | copy-start | bytes 3076
  8.1 17.0 %copy-start.9 = (s32[16,32]{1,0:T(8,128)S(1)}, s32[16,32]{1,0:T(8,128)}, u32[]{:S(2)}) copy-start(s32[16,32]{1,0:T(8,128)} %param.14) | copy-start | bytes 6148
  8.1 20.9 %copy-start.2 = (bf16[4,2,64,32]{2,3,1,0:T(8,128)(2,1)S(1)}, bf16[4,2,64,32]{2,3,1,0:T(8,128)(2,1)}, u32[]{:S(2)}) copy-start(bf16[4,2,64,32]{2,3,1,0:T(8,128)(2,1)} %param.15) | copy-start | bytes 98308
  8.2 19.2 %collective-permute-start.4 = (bf16[64,1792]{1,0:T(8,128)(2,1)S(1)}, bf16[64,1792]{1,0:T(8,128)(2,1)S(1)}, u32[]{:S(2)}, u32[]{:S(2)}) collective-permute-start(bf16[64,1792]{1,0:T(8,128)(2,1)S(1)} %get-tuple-element.12.refs_4_), channel_id=1, source_target_pairs={{0,8},{4,12},{8,0},{12,4},{1,9},{5,13},{9,1},{13,5},{2,10},{6,14},... | collective-permute-start | bytes 688136 | tf_op jit(solution)/shard_map/ppermute | solution.py:429
  15.5 12.3 %collective-permute-start.1 = (bf16[64,1792]{1,0:T(8,128)(2,1)}, bf16[64,1792]{1,0:T(8,128)(2,1)S(1)}, u32[]{:S(2)}, u32[]{:S(2)}) collective-permute-start(bf16[64,1792]{1,0:T(8,128)(2,1)} %get-tuple-element.11.refs_0_), channel_id=1, source_target_pairs={{0,8},{4,12},{8,0},{12,4},{1,9},{5,13},{9,1},{13,5},{2,10},{6,14},... | collective-permute-start | bytes 688136 | tf_op jit(solution)/shard_map/ppermute | solution.py:429
  15.6 0.9 %copy-start = (f32[64,512]{1,0:T(8,128)S(1)}, f32[64,512]{1,0:T(8,128)}, u32[]{:S(2)}) copy-start(f32[64,512]{1,0:T(8,128)} %get-tuple-element.13.a_ref) | copy-start | bytes 393220
  16.5 6.4 %collective-permute-start.6 = (bf16[128,128]{1,0:T(8,128)(2,1)S(1)}, bf16[128,128]{1,0:T(8,128)(2,1)S(1)}, u32[]{:S(2)}, u32[]{:S(2)}) collective-permute-start(bf16[128,128]{1,0:T(8,128)(2,1)S(1)} %get-tuple-element.15), channel_id=1, source_target_pairs={{0,1},{1,2},{2,3},{3,0},{4,5},{5,6},{6,7},{7,4},{8,9},{9,10},{10,1... | collective-permute-start | bytes 98312 | tf_op jit(solution)/shard_map/ppermute | solution.py:401
  18.7 4.3 %collective-permute-start.7 = (bf16[128,128]{1,0:T(8,128)(2,1)S(1)}, bf16[128,128]{1,0:T(8,128)(2,1)S(1)}, u32[]{:S(2)}, u32[]{:S(2)}) collective-permute-start(bf16[128,128]{1,0:T(8,128)(2,1)S(1)} %get-tuple-element.16), channel_id=1, source_target_pairs={{1,0},{2,1},{3,2},{0,3},{5,4},{6,5},{7,6},{4,7},{9,8},{10,9},{11,1... | collective-permute-start | bytes 98312 | tf_op jit(solution)/shard_map/ppermute | solution.py:402
  23.0 4.3 %collective-permute-start.9 = (bf16[128,256]{1,0:T(8,128)(2,1)S(1)}, bf16[128,256]{1,0:T(8,128)(2,1)S(1)}, u32[]{:S(2)}, u32[]{:S(2)}) collective-permute-start(bf16[128,256]{1,0:T(8,128)(2,1)S(1)} %seal.1.refs_8_), channel_id=1, source_target_pairs={{0,8},{4,12},{8,0},{12,4},{1,9},{5,13},{9,1},{13,5},{2,10},{6,14},... | collective-permute-start | bytes 196616 | tf_op jit(solution)/shard_map/ppermute | solution.py:429
  24.6 5.2 %collective-permute-start.3 = (bf16[64,1792]{1,0:T(8,128)(2,1)S(1)}, bf16[64,1792]{1,0:T(8,128)(2,1)S(1)}, u32[]{:S(2)}, u32[]{:S(2)}) collective-permute-start(bf16[64,1792]{1,0:T(8,128)(2,1)S(1)} %get-tuple-element.12.refs_4_), channel_id=1, source_target_pairs={{0,4},{4,0},{8,12},{12,8},{1,5},{5,1},{9,13},{13,9},{2,6},{6,2},{1... | collective-permute-start | bytes 688136 | tf_op jit(solution)/shard_map/ppermute | solution.py:430
  24.6 5.2 %collective-permute-start = (bf16[64,1792]{1,0:T(8,128)(2,1)}, bf16[64,1792]{1,0:T(8,128)(2,1)S(1)}, u32[]{:S(2)}, u32[]{:S(2)}) collective-permute-start(bf16[64,1792]{1,0:T(8,128)(2,1)} %get-tuple-element.11.refs_0_), channel_id=1, source_target_pairs={{0,4},{4,0},{8,12},{12,8},{1,5},{5,1},{9,13},{13,9},{2,6},{6,2},{1... | collective-permute-start | bytes 688136 | tf_op jit(solution)/shard_map/ppermute | solution.py:430
  27.3 1.3 %collective-permute-start.8 = (bf16[128,256]{1,0:T(8,128)(2,1)S(1)}, bf16[128,256]{1,0:T(8,128)(2,1)S(1)}, u32[]{:S(2)}, u32[]{:S(2)}) collective-permute-start(bf16[128,256]{1,0:T(8,128)(2,1)S(1)} %seal.1.refs_8_), channel_id=1, source_target_pairs={{0,4},{4,0},{8,12},{12,8},{1,5},{5,1},{9,13},{13,9},{2,6},{6,2},{1... | collective-permute-start | bytes 196616 | tf_op jit(solution)/shard_map/ppermute | solution.py:430
  27.3 2.5 %collective-permute-start.5 = (bf16[64,1792]{1,0:T(8,128)(2,1)S(1)}, bf16[64,1792]{1,0:T(8,128)(2,1)S(1)}, u32[]{:S(2)}, u32[]{:S(2)}) collective-permute-start(bf16[64,1792]{1,0:T(8,128)(2,1)S(1)} %collective-permute-done.4.refs_6_), channel_id=1, source_target_pairs={{0,4},{4,0},{8,12},{12,8},{1,5},{5,1},{9,13},{13,9},{2,6},{6,2},{1... | collective-permute-start | bytes 688136 | tf_op jit(solution)/shard_map/ppermute | solution.py:430
  27.8 2.0 %collective-permute-start.2 = (bf16[64,1792]{1,0:T(8,128)(2,1)S(1)}, bf16[64,1792]{1,0:T(8,128)(2,1)S(1)}, u32[]{:S(2)}, u32[]{:S(2)}) collective-permute-start(bf16[64,1792]{1,0:T(8,128)(2,1)S(1)} %collective-permute-done.1.refs_2_), channel_id=1, source_target_pairs={{0,4},{4,0},{8,12},{12,8},{1,5},{5,1},{9,13},{13,9},{2,6},{6,2},{1... | collective-permute-start | bytes 688136 | tf_op jit(solution)/shard_map/ppermute | solution.py:430
  28.6 1.3 %collective-permute-start.10 = (bf16[128,256]{1,0:T(8,128)(2,1)S(1)}, bf16[128,256]{1,0:T(8,128)(2,1)S(1)}, u32[]{:S(2)}, u32[]{:S(2)}) collective-permute-start(bf16[128,256]{1,0:T(8,128)(2,1)S(1)} %collective-permute-done.9.refs_10_), channel_id=1, source_target_pairs={{0,4},{4,0},{8,12},{12,8},{1,5},{5,1},{9,13},{13,9},{2,6},{6,2},{1... | collective-permute-start | bytes 196616 | tf_op jit(solution)/shard_map/ppermute | solution.py:430
  29.8 0.9 %copy-start.1 = (bf16[64,1792]{1,0:T(8,128)(2,1)S(1)}, bf16[64,1792]{1,0:T(8,128)(2,1)}, u32[]{:S(2)}) copy-start(bf16[64,1792]{1,0:T(8,128)(2,1)} %get-tuple-element.11.refs_0_) | copy-start | bytes 688132
